TPU v7x, 32 devices: a whole 2x2x4 slice. The times are simulated.
32 devices in a mesh: row: 4 (over y, x), col: 8 (over z, core).
Axes of the slice: x: 2, y: 2, z: 4, core: 2. Of those that a mesh axis runs over, the one named last changes fastest.
Arguments:
- features: bfloat16 [2, 4, 512, 512], P(None, 'row', 'col'), may hold values from -1 to 1, as said below
- amplitude: float32 [1], replicated, may hold values from 0.5 to 2
- noise: float32 [2, 4, 512], P(None, 'row'), may hold values from 0.1 to 1
Outputs:
- factored: float32 [2, 4, 512, 1, 8, 512], P(None, 'row', None, None, 'col')
Inputs may be any that keep to these rules, and one draw needn't show every extreme that they name: `features`: coordinates of points after the length scale.
All inputs are finite; a program needn't handle non-finite values.
Results may differ from a plain program's by a relative error of at most 0.0015.
Values may be sent and summed in bfloat16 or wider, within the bound.
No kernel may reach another device: no remote copies, remote signals or barrier semaphores. Data moves between devices by JAX's collectives and lax.ppermute only.
A program may use at most 128 MiB of HBM per device.

v0:
```python
import jax
import jax.numpy as jnp
from jax import lax
from jax.sharding import PartitionSpec as P

PANELS = 2


HIGHEST = lax.Precision.HIGHEST


def from_root(x, axis, root):
    mine = lax.axis_index(axis) == root
    return lax.psum(jnp.where(mine, x, jnp.zeros_like(x)), axis)


def factor_block(block):
    lower = jnp.linalg.cholesky(block)
    ident = jnp.eye(block.shape[0], dtype=jnp.float32)
    inverse = jax.scipy.linalg.solve_triangular(lower, ident, lower=True)
    return (lower, inverse)


def keep_blocks(solved, lower, global_ids, step):
    later = (global_ids > step)[:, None, None]
    here = (global_ids == step)[:, None, None]
    return jnp.where(later, solved, jnp.where(here, lower[None], 0.0))


def update_blocks(matrix, row_panel, col_panel, row_ids, col_ids, step):
    product = jnp.einsum("aip,bjp->aibj", row_panel, col_panel, precision=HIGHEST)
    row_later = (row_ids > step)[:, None, None, None]
    col_later = (col_ids > step)[None, None, :, None]
    result = jnp.where(row_later & col_later, matrix - product, matrix)
    result = jnp.where((col_ids == step)[None, None, :, None], row_panel[:, :, None, :], result)
    result = jnp.where((row_ids == step)[:, None, None, None] & col_later, 0.0, result)
    return result


def trail_update(tiles, left_panel, right_panel, left_ids, right_ids, step):
    product = jnp.einsum("aip,bjp->aibj", left_panel, right_panel, precision=HIGHEST)
    later = (left_ids > step)[:, None, None, None] & (right_ids > step)[None, None, :, None]
    return jnp.where(later, tiles - product, tiles)


def pick_stride(whole, col_at, row_n, col_n):
    folded = whole.reshape((whole.shape[0] * row_n // col_n, col_n // row_n) + whole.shape[1:])
    return lax.dynamic_index_in_dim(folded, col_at // row_n, axis=1, keepdims=False)


def kernel_tiles(left, right, amplitude):
    left_sq = jnp.sum(left.astype(jnp.float32) ** 2, axis=2)
    right_sq = jnp.sum(right.astype(jnp.float32) ** 2, axis=2)
    cross = jnp.einsum("aif,bjf->aibj", left, right, preferred_element_type=jnp.float32)
    dist = left_sq[:, :, None, None] + right_sq[None, None, :, :] - 2.0 * cross
    return amplitude[0] * jnp.exp(-0.5 * dist)


def add_noise(tiles, left_ids, right_ids, noise_rows):
    block = tiles.shape[1]
    same_block = left_ids[:, None] == right_ids[None, :]
    same_entry = jnp.eye(block, dtype=jnp.bool_)
    diag_mask = same_block[:, None, :, None] & same_entry[None, :, None, :]
    return tiles + jnp.where(diag_mask, noise_rows[:, :, None, None], 0.0)


def lead_share(row_feats, noise_rows, slot, root):
    return (
        from_root(row_feats[slot], "row", root),
        from_root(noise_rows[slot].astype(jnp.bfloat16), "row", root).astype(jnp.float32),
    )


def local(features, amplitude, noise):
    row_n = lax.axis_size("row")
    col_n = lax.axis_size("col")
    row_at = lax.axis_index("row")
    col_at = lax.axis_index("col")
    gathered = lax.all_gather(features, "col", axis=2, tiled=True)
    row_feats = gathered.reshape(gathered.shape[0], gathered.shape[2], gathered.shape[3])
    shared = from_root(row_feats, "row", col_at % row_n)
    col_feats = pick_stride(shared, col_at, row_n, col_n)
    nrows = row_feats.shape[0]
    ncols = col_feats.shape[0]
    block = row_feats.shape[1]
    noise_rows = noise.reshape(nrows, block)
    row_ids = jnp.arange(nrows, dtype=jnp.int32) * row_n + row_at
    col_ids = jnp.arange(ncols, dtype=jnp.int32) * col_n + col_at
    matrix = add_noise(kernel_tiles(row_feats, col_feats, amplitude), row_ids, col_ids, noise_rows)
    lead_f = []
    lead_n = []
    for lead in range(PANELS):
        got_f, got_n = lead_share(row_feats, noise_rows, lead // row_n, lead % row_n)
        lead_f.append(got_f)
        lead_n.append(got_n)
    lead_feats = jnp.stack(lead_f)
    lead_noise = jnp.stack(lead_n)
    lead_ids = jnp.arange(PANELS, dtype=jnp.int32)
    rows_lead = add_noise(
        kernel_tiles(row_feats, lead_feats, amplitude), row_ids, lead_ids, noise_rows
    )
    cols_lead = add_noise(
        kernel_tiles(col_feats, lead_feats, amplitude),
        col_ids,
        lead_ids,
        jnp.zeros((ncols, block), jnp.float32),
    )
    cols_lead = cols_lead + jnp.where(
        (col_ids[:, None] == lead_ids[None, :])[:, None, :, None]
        & jnp.eye(block, dtype=jnp.bool_)[None, :, None, :],
        lead_noise[None, None, :, :],
        0.0,
    )
    lead_tiles = add_noise(
        kernel_tiles(lead_feats, lead_feats, amplitude), lead_ids, lead_ids, lead_noise
    )
    for step in range(PANELS):
        lower, inverse = factor_block(lead_tiles[step, :, step, :])
        row_panel = keep_blocks(
            jnp.einsum("aip,qp->aiq", rows_lead[:, :, step, :], inverse, precision=HIGHEST),
            lower,
            row_ids,
            step,
        )
        col_panel = keep_blocks(
            jnp.einsum("aip,qp->aiq", cols_lead[:, :, step, :], inverse, precision=HIGHEST),
            lower,
            col_ids,
            step,
        )
        lead_panel = keep_blocks(
            jnp.einsum("aip,qp->aiq", lead_tiles[:, :, step, :], inverse, precision=HIGHEST),
            lower,
            lead_ids,
            step,
        )
        rows_lead = trail_update(rows_lead, row_panel, lead_panel, row_ids, lead_ids, step)
        cols_lead = trail_update(cols_lead, col_panel, lead_panel, col_ids, lead_ids, step)
        lead_tiles = trail_update(lead_tiles, lead_panel, lead_panel, lead_ids, lead_ids, step)
        matrix = update_blocks(matrix, row_panel, col_panel, row_ids, col_ids, step)
    return matrix.reshape(nrows, 1, block, ncols, 1, block)


def solution(mesh):
    return jax.shard_map(
        local,
        mesh=mesh,
        in_specs=(P(None, "row", "col", None), P(), P(None, "row", None)),
        out_specs=P(None, "row", None, None, "col", None),
        check_vma=False,
    )
```

profile of v0, /device:TPU:31, one launch (start us, length us, event | category | flops | bytes accessed | tf_op | source)
XLA Modules:
  0.0 516.4 jit_solution(16003524634156163595)
XLA Ops:
  7.4 23.6 %all-gather.2.cloned.1.call-done = bf16[2,1,512,512]{3,2,0,1:T(8,128)(2,1)} async-done(((bf16[2,1,64,512]{3,2,0,1:T(8,128)(2,1)}), bf16[2,1,512,512]{3,2,0,1:T(8,128)(2,1)}) %all-gather.2.cloned.1.call-update) | async-done | bytes 1048592 | tf_op jit(solution)/shard_map/all_gather | solution.py:79
  30.9 2.4 bitcast_select_fusion
  37.5 6.4 %all-reduce.1 = (bf16[1,512]{1,0:T(2,128)(2,1)S(1)}, bf16[1,512]{1,0:T(2,128)(2,1)S(1)}) all-reduce(bf16[1,512]{1,0:T(2,128)(2,1)S(1)} %get-tuple-element.73, bf16[1,512]{1,0:T(2,128)(2,1)S(1)} %get-tuple-element.72), channel_id=1, replica_groups=mesh['row'=4,'col'=8] {'row'}, use_global_device_ids=true, to_apply=%region_5.6 | all-reduce | flops 1024 | bytes 4096 | tf_op jit(solution)/shard_map/psum | solution.py:14
  45.5 59.6 %all-reduce.5.cloned.1.call-done = (bf16[1,512,512]{2,1,0:T(8,128)(2,1)}, bf16[1,512,512]{2,1,0:T(8,128)(2,1)}, bf16[2,512,512]{2,1,0:T(8,128)(2,1)}) async-done(((bf16[1,512,512]{2,1,0:T(8,128)(2,1)}, bf16[1,512,512]{2,1,0:T(8,128)(2,1)}, bf16[2,512,512]{2,1,0:T(8,128)(2,1)}), (bf16[1,512,512]{2,1,0:T(8,128)(2,1)}, bf16[1,512,512]{2,1,0:T(8,128)(2,1)}, ...) | async-done | bytes 2097168 | tf_op jit(solution)/shard_map/psum | solution.py:14
  107.5 2.3 broadcast_add_fusion
  109.8 5.4 %copy.10 = f32[2,512,2,512]{1,3,2,0:T(8,128)} copy(f32[2,512,2,512]{3,1,0,2:T(8,128)} %broadcast_add_fusion) | data formatting | bytes 8388608 | tf_op jit(solution)/shard_map/add | solution.py:55
  115.2 4.2 select_add_fusion
  126.4 11.7 %cholesky.286 = f32[128,128]{1,0:T(8,128)S(1)} custom-call(f32[128,128]{1,0:T(8,128)S(1)} %cholesky.426), custom_call_target="Cholesky" | custom-call | tf_op jit(solution)/shard_map/jit(cholesky)/cholesky | solution.py:18
  138.3 9.8 %custom-call.27 = f32[1,128,128]{1,2,0:T(8,128)S(1)} custom-call(f32[1,128,128]{2,1,0:T(8,128)S(1)} %get-tuple-element.71), custom_call_target="InvertDiagBlocksLowerTriangular" | custom-call | tf_op jit(solution)/shard_map/jit(cholesky)/cholesky | solution.py:18
  150.6 12.1 %cholesky.305 = f32[128,128]{1,0:T(8,128)S(1)} custom-call(f32[128,128]{1,0:T(8,128)S(1)} %cholesky.430), custom_call_target="Cholesky" | custom-call | tf_op jit(solution)/shard_map/jit(cholesky)/cholesky | solution.py:18
  162.7 9.8 %custom-call.28 = f32[1,128,128]{1,2,0:T(8,128)S(1)} custom-call(f32[1,128,128]{2,1,0:T(8,128)S(1)} %get-tuple-element.68), custom_call_target="InvertDiagBlocksLowerTriangular" | custom-call | tf_op jit(solution)/shard_map/jit(cholesky)/cholesky | solution.py:18
  174.1 11.7 %cholesky.326 = f32[128,128]{1,0:T(8,128)S(1)} custom-call(f32[128,128]{1,0:T(8,128)S(1)} %cholesky.435), custom_call_target="Cholesky" | custom-call | tf_op jit(solution)/shard_map/jit(cholesky)/cholesky | solution.py:18
  186.6 9.8 %custom-call.29 = f32[1,128,128]{1,2,0:T(8,128)S(1)} custom-call(f32[1,128,128]{2,1,0:T(8,128)S(1)} %get-tuple-element.65), custom_call_target="InvertDiagBlocksLowerTriangular" | custom-call | tf_op jit(solution)/shard_map/jit(cholesky)/cholesky | solution.py:18
  197.9 11.9 %cholesky.343 = f32[128,128]{1,0:T(8,128)S(1)} custom-call(f32[128,128]{1,0:T(8,128)S(1)} %convolution_subtract_fusion.11), custom_call_target="Cholesky" | custom-call | tf_op jit(solution)/shard_map/jit(cholesky)/cholesky | solution.py:18
  215.3 12.0 %while.4 = (s32[]{:T(128)}, f32[512,512]{1,0:T(8,128)}, s32[4,2]{0,1:T(2,128)S(1)}, f32[4,128,128]{2,1,0:T(8,128)S(1)}, s32[]{:T(128)}) while((s32[]{:T(128)}, f32[512,512]{1,0:T(8,128)}, s32[4,2]{0,1:T(2,128)S(1)}, f32[4,128,128]{2,1,0:T(8,128)S(1)}, s32[]{:T(128)}) %tuple.60), condition=%wide.while_cond, body=%wide.while_body.sunk | while | flops 2 | bytes 131181 | solution.py:20
  216.0 2.3 bitcast_dynamic-update-slice_fusion.4
  219.0 2.3 bitcast_dynamic-update-slice_fusion.4
  222.0 2.3 bitcast_dynamic-update-slice_fusion.4
  225.1 2.3 bitcast_dynamic-update-slice_fusion.4
  227.3 39.3 %custom-call.30 = f32[4,128,128]{1,2,0:T(8,128)S(1)} custom-call(f32[4,128,128]{2,1,0:T(8,128)S(1)} %get-tuple-element.21), custom_call_target="InvertDiagBlocksLowerTriangular" | custom-call | tf_op jit(solution)/shard_map/jit(_solve_triangular)/triangular_solve | solution.py:20
  271.6 2.5 convolution_subtract_fusion.5
  274.6 7.1 %select_select_fusion.1 = f32[2,512,512]{2,1,0:T(8,128)S(1)} fusion(f32[2,512,2,512]{1,3,2,0:T(8,128)S(1)} %copy-done.8, f32[512,512]{1,0:T(8,128)S(1)} %copy-done.5, pred[2]{0:T(512)(128)(4,1)S(1)} %get-tuple-element.88, pred[2]{0:T(512)(128)(4,1)S(1)} %get-tuple-element.89, f32[128,512]{1,0:T(8,128)S(1)} %fusion.94, f32[128,512]{1,0:T(8,128)S(1)} %fusion.95, ...), kind=kOutput, calls=%fused_computation.38 | convolution fusion | flops 3223060480 | bytes 6292480 | tf_op jit(solution)/shard_map/aip,qp->aiq/dot_general | solution.py:132
  281.7 8.7 %fusion.13 = f32[2,512,2,512]{1,3,2,0:T(8,128)} fusion(f32[2,512,512]{2,1,0:T(8,128)S(1)} %select_select_fusion.1), kind=kOutput, calls=%fused_computation.25 | convolution fusion | flops 6442450944 | bytes 6291456 | tf_op jit(solution)/shard_map/aip,bjp->aibj/dot_general | solution.py:41
  290.5 3.2 bitcast_subtract_fusion
  293.7 5.3 %copy.8 = f32[2,512,2,512]{1,3,2,0:T(8,128)} copy(f32[2,512,2,512]{3,1,0,2:T(8,128)} %bitcast_subtract_fusion) | data formatting | bytes 8388608 | tf_op jit(solution)/shard_map/sub | solution.py:55
  299.0 3.5 select_add_fusion.1
  302.5 7.0 %select_select_fusion.2 = f32[2,512,512]{2,1,0:T(8,128)S(1)} fusion(f32[2,512,2,512]{1,3,2,0:T(8,128)S(1)} %select_add_fusion.1, f32[512,512]{1,0:T(8,128)S(1)} %copy-done.6, pred[2]{0:T(512)(128)(4,1)S(1)} %get-tuple-element.85, pred[2]{0:T(512)(128)(4,1)S(1)} %get-tuple-element.86, f32[128,512]{1,0:T(8,128)S(1)} %copy-done.18, ...), kind=kOutput, calls=%fused_computation.39 | convolution fusion | flops 3223060480 | bytes 6292480 | tf_op jit(solution)/shard_map/aip,qp->aiq/dot_general | solution.py:120
  309.5 8.5 %fusion.15 = f32[2,512,2,512]{1,3,2,0:T(8,128)} fusion(f32[2,512,512]{2,1,0:T(8,128)S(1)} %select_select_fusion.2, f32[2,512,512]{2,1,0:T(8,128)S(1)} %select_select_fusion.1), kind=kOutput, calls=%fused_computation.27 | convolution fusion | flops 6442450944 | bytes 8388608 | tf_op jit(solution)/shard_map/aip,bjp->aibj/dot_general | solution.py:41
  319.4 3.5 fusion.25
  322.9 4.8 fusion.123
  327.7 4.8 fusion.5
  332.5 2.5 fusion.67
  335.4 2.5 fusion.26
  338.9 11.7 %cholesky.358 = f32[128,128]{1,0:T(8,128)S(1)} custom-call(f32[128,128]{1,0:T(8,128)S(1)} %cholesky.439), custom_call_target="Cholesky" | custom-call | tf_op jit(solution)/shard_map/jit(cholesky)/cholesky | solution.py:18
  350.8 9.8 %custom-call.31 = f32[1,128,128]{1,2,0:T(8,128)S(1)} custom-call(f32[1,128,128]{2,1,0:T(8,128)S(1)} %get-tuple-element.61), custom_call_target="InvertDiagBlocksLowerTriangular" | custom-call | tf_op jit(solution)/shard_map/jit(cholesky)/cholesky | solution.py:18
  363.1 11.7 %cholesky.377 = f32[128,128]{1,0:T(8,128)S(1)} custom-call(f32[128,128]{1,0:T(8,128)S(1)} %cholesky.443), custom_call_target="Cholesky" | custom-call | tf_op jit(solution)/shard_map/jit(cholesky)/cholesky | solution.py:18
  376.2 10.2 %custom-call.32 = f32[1,128,128]{1,2,0:T(8,128)S(1)} custom-call(f32[1,128,128]{2,1,0:T(8,128)S(1)} %get-tuple-element.58), custom_call_target="InvertDiagBlocksLowerTriangular" | custom-call | tf_op jit(solution)/shard_map/jit(cholesky)/cholesky | solution.py:18
  388.0 11.7 %cholesky.398 = f32[128,128]{1,0:T(8,128)S(1)} custom-call(f32[128,128]{1,0:T(8,128)S(1)} %cholesky.448), custom_call_target="Cholesky" | custom-call | tf_op jit(solution)/shard_map/jit(cholesky)/cholesky | solution.py:18
  400.4 9.8 %custom-call.33 = f32[1,128,128]{1,2,0:T(8,128)S(1)} custom-call(f32[1,128,128]{2,1,0:T(8,128)S(1)} %get-tuple-element.55), custom_call_target="InvertDiagBlocksLowerTriangular" | custom-call | tf_op jit(solution)/shard_map/jit(cholesky)/cholesky | solution.py:18
  411.6 11.9 %cholesky.415 = f32[128,128]{1,0:T(8,128)S(1)} custom-call(f32[128,128]{1,0:T(8,128)S(1)} %convolution_subtract_fusion.10), custom_call_target="Cholesky" | custom-call | tf_op jit(solution)/shard_map/jit(cholesky)/cholesky | solution.py:18
  428.1 11.7 %while.5 = (s32[]{:T(128)}, f32[512,512]{1,0:T(8,128)}, s32[4,2]{0,1:T(2,128)S(1)}, f32[4,128,128]{2,1,0:T(8,128)S(1)}, s32[]{:T(128)}) while((s32[]{:T(128)}, f32[512,512]{1,0:T(8,128)}, s32[4,2]{0,1:T(2,128)S(1)}, f32[4,128,128]{2,1,0:T(8,128)S(1)}, s32[]{:T(128)}) %tuple.71), condition=%wide.while_cond.clone, body=%wide.while_body.clone.sunk | while | flops 2 | bytes 131181 | solution.py:20
  428.8 2.3 bitcast_dynamic-update-slice_fusion.5
  439.9 39.3 %custom-call.34 = f32[4,128,128]{1,2,0:T(8,128)S(1)} custom-call(f32[4,128,128]{2,1,0:T(8,128)S(1)} %get-tuple-element.22), custom_call_target="InvertDiagBlocksLowerTriangular" | custom-call | tf_op jit(solution)/shard_map/jit(_solve_triangular)/triangular_solve | solution.py:20
  484.1 2.4 convolution_subtract_fusion.4
  486.9 8.5 %fusion.1 = f32[2,512,512]{2,1,0:T(8,128)S(1)} fusion(f32[2,512,2,512]{1,3,2,0:T(8,128)} %fusion.15, f32[2,512,2,512]{1,3,2,0:T(8,128)S(1)} %copy-done.3, pred[2,1]{1,0:T(4,128)(4,1)S(1)} %slice.141, f32[128,512]{1,0:T(8,128)S(1)} %fusion.88, f32[128,512]{1,0:T(8,128)S(1)} %fusion.89, f32[128,512]{1,0:T(8,128)S(1)} %fusion.91, f32[128,512]{1,0:T(8,128)S(1)} %fusion.70), kind=kOutput, calls=%fused_computation.12 | convolution fusion | flops 3223060480 | bytes 7340544 | tf_op jit(solution)/shard_map/aip,qp->aiq/dot_general | solution.py:120
  495.5 3.8 fusion.24
  500.9 4.9 fusion.8
  505.8 3.5 copy.22
  (175 shorter events, 61.5 us)
Async XLA Ops:
  6.5 24.4 %all-gather.2.cloned.1.call-start = ((), (), s32[]{:S(2)}) async-start(), calls=%async_computation | async-start | bytes 1179648 | tf_op jit(solution)/shard_map/all_gather | solution.py:79
  7.3 97.8 %all-reduce.5.cloned.1.call-start = ((), (), s32[]{:S(2)}) async-start(), calls=%async_computation.1 | async-start | bytes 4194304 | tf_op jit(solution)/shard_map/psum | solution.py:14
  30.9 2.4 copy-start.4
  33.3 3.0 copy-start.30
  36.4 78.7 %copy-start.21 = (pred[512,512]{0,1:T(8,128)(4,1)}, pred[512,512]{0,1:T(8,128)(4,1)S(1)}, u32[]{:S(2)}) copy-start(pred[512,512]{0,1:T(8,128)(4,1)S(1)} %iota_compare_fusion.1) | copy-start | bytes 786436
  45.1 226.5 %copy-start.9 = (f32[512,512]{0,1:T(8,128)}, f32[512,512]{0,1:T(8,128)S(1)}, u32[]{:S(2)}) copy-start(f32[512,512]{0,1:T(8,128)S(1)} %fusion.66) | copy-start | bytes 3145732
  107.2 8.0 %copy-start.23 = (bf16[2,512,512]{2,1,0:T(8,128)(2,1)}, bf16[2,512,512]{2,1,0:T(8,128)(2,1)S(1)}, u32[]{:S(2)}) copy-start(bf16[2,512,512]{2,1,0:T(8,128)(2,1)S(1)} %constant_dynamic-update-slice_fusion) | copy-start | bytes 3145732
  119.4 2.0 copy-start.7
  125.4 1.0 copy-start.20
  267.1 7.4 %copy-start.8 = (f32[2,512,2,512]{1,3,2,0:T(8,128)S(1)}, f32[2,512,2,512]{1,3,2,0:T(8,128)}, u32[]{:S(2)}) copy-start(f32[2,512,2,512]{1,3,2,0:T(8,128)} %copy-done.7) | copy-start | bytes 12582916
  268.7 5.9 %copy-start.5 = (f32[512,512]{1,0:T(8,128)S(1)}, f32[512,512]{1,0:T(8,128)}, u32[]{:S(2)}) copy-start(f32[512,512]{1,0:T(8,128)} %get-tuple-element.47) | copy-start | bytes 3145732
  269.1 12.6 %copy-start.11 = (f32[128,512]{1,0:T(8,128)}, f32[128,512]{1,0:T(8,128)S(1)}, u32[]{:S(2)}) copy-start(f32[128,512]{1,0:T(8,128)S(1)} %fusion.97) | copy-start | bytes 786436
  271.6 10.1 %copy-start.13 = (f32[128,512]{1,0:T(8,128)}, f32[128,512]{1,0:T(8,128)S(1)}, u32[]{:S(2)}) copy-start(f32[128,512]{1,0:T(8,128)S(1)} %fusion.95) | copy-start | bytes 786436
  274.5 7.2 %copy-start.17 = (f32[128,512]{1,0:T(8,128)}, f32[128,512]{1,0:T(8,128)S(1)}, u32[]{:S(2)}) copy-start(f32[128,512]{1,0:T(8,128)S(1)} %fusion.94) | copy-start | bytes 786436
  281.7 8.8 %copy-start.24 = (bf16[2,512,512]{2,1,0:T(8,128)(2,1)S(1)}, bf16[2,512,512]{2,1,0:T(8,128)(2,1)}, u32[]{:S(2)}) copy-start(bf16[2,512,512]{2,1,0:T(8,128)(2,1)} %copy-done.23) | copy-start | bytes 3145732
  299.0 3.5 copy-start.6
  299.0 3.5 copy-start.12
  299.0 3.5 copy-start.14
  299.0 3.5 copy-start.18
  302.5 7.0 %copy-start.2 = (f32[2,512,2,512]{1,3,2,0:T(8,128)}, f32[2,512,2,512]{1,3,2,0:T(8,128)S(1)}, u32[]{:S(2)}) copy-start(f32[2,512,2,512]{1,3,2,0:T(8,128)S(1)} %select_add_fusion.1) | copy-start | bytes 12582916
  309.5 13.4 %copy-start = (f32[2,512,512]{2,1,0:T(8,128)}, f32[2,512,512]{2,1,0:T(8,128)S(1)}, u32[]{:S(2)}) copy-start(f32[2,512,512]{2,1,0:T(8,128)S(1)} %select_select_fusion.2) | copy-start | bytes 6291460
  309.5 8.5 %copy-start.27 = (bf16[2,512,512]{2,1,0:T(8,128)(2,1)S(1)}, bf16[2,512,512]{2,1,0:T(8,128)(2,1)}, u32[]{:S(2)}) copy-start(bf16[2,512,512]{2,1,0:T(8,128)(2,1)} %get-tuple-element.43) | copy-start | bytes 3145732
  309.5 8.7 %copy-start.22 = (pred[512,512]{0,1:T(8,128)(4,1)S(1)}, pred[512,512]{0,1:T(8,128)(4,1)}, u32[]{:S(2)}) copy-start(pred[512,512]{0,1:T(8,128)(4,1)} %copy-done.21) | copy-start | bytes 786436
  309.5 8.7 %copy-start.25 = (bf16[2,512,512]{2,1,0:T(8,128)(2,1)S(1)}, bf16[2,512,512]{2,1,0:T(8,128)(2,1)}, u32[]{:S(2)}) copy-start(bf16[2,512,512]{2,1,0:T(8,128)(2,1)} %copy-done.23) | copy-start | bytes 3145732
  309.5 8.7 %copy-start.32 = (pred[2]{0:T(512)(128)(4,1)S(1)}, pred[2]{0:T(512)(128)(4,1)}, u32[]{:S(2)}) copy-start(pred[2]{0:T(512)(128)(4,1)} %iota_compare_fusion.6) | copy-start | bytes 10
  337.9 1.0 copy-start.19
  426.5 52.7 %copy-start.10 = (f32[512,512]{0,1:T(8,128)S(1)}, f32[512,512]{0,1:T(8,128)}, u32[]{:S(2)}) copy-start(f32[512,512]{0,1:T(8,128)} %copy-done.9) | copy-start | bytes 3145732
  481.1 5.8 %copy-start.3 = (f32[2,512,2,512]{1,3,2,0:T(8,128)S(1)}, f32[2,512,2,512]{1,3,2,0:T(8,128)}, u32[]{:S(2)}) copy-start(f32[2,512,2,512]{1,3,2,0:T(8,128)} %copy-done.2) | copy-start | bytes 12582916
  486.9 8.6 %copy-start.15 = (f32[1,512,2,512]{1,3,2,0:T(8,128)S(1)}, f32[1,512,2,512]{1,3,2,0:T(8,128)}, u32[]{:S(2)}) copy-start(f32[1,512,2,512]{1,3,2,0:T(8,128)} %fusion.5) | copy-start | bytes 6291460
  486.9 8.6 %copy-start.16 = (f32[512,512]{1,0:T(8,128)S(1)}, f32[512,512]{1,0:T(8,128)}, u32[]{:S(2)}) copy-start(f32[512,512]{1,0:T(8,128)} %get-tuple-element.45) | copy-start | bytes 3145732
  495.5 3.8 copy-start.28
  495.5 4.6 copy-start.26
  499.3 1.6 copy-start.1
  499.3 1.6 copy-start.29
  499.3 1.6 copy-start.31
Sparse Core Ops, SparseCore 0:
  9.0 21.9 all-gather.1
  35.1 69.8 all-reduce.4
where the time goes:
time: 523 us; the launch traced here: 516 us
  other arithmetic  259 us (50%)
  matrix products  97.3 us (19%)
  waiting for transfers between devices  83.9 us (16%)
  local copies, waits for them, and re-layouts  49.6 us (9%)
  between operations  20.2 us (4%)
  blocking collectives  6.38 us (1%)
    another operation x29, other arithmetic, factor_block(): lower = jnp.linalg.cholesky(block)  159 us
    another operation x5, other arithmetic, factor_block(): inverse = jax.scipy.linalg.solve_triangular(lower, ident, lower=True)  81.8 us
    psum x1, waiting for transfers between devices, from_root(): return lax.psum(jnp.where(mine, x, jnp.zeros_like(x)), axis)  59.6 us
    another operation x27, local copies, waits for them, and re-layouts, factor_block(): inverse = jax.scipy.linalg.solve_triangular(lower, ident, lower=True)  23.6 us
    all_gather x1, waiting for transfers between devices, local(): gathered = lax.all_gather(features, 'col', axis=2, tiled=True)  23.6 us
    dot_general x3, matrix products, trail_update(): jnp.einsum('aip,bjp->aibj', left_panel, right_panel, precision=HIGHEST)  22.1 us
    dot_general x2, matrix products, local(): jnp.einsum('aip,qp->aiq', rows_lead[:, :, step, :], inverse, precision=HI...  15.5 us
    another operation x14, matrix products, factor_block(): inverse = jax.scipy.linalg.solve_triangular(lower, ident, lower=True)  15.4 us
  transfers between devices with their start and end apart: 2, of which 2 were waited for; matrix products, arithmetic and copies ran while one was open for 1% of the time, Pallas kernels for 0%

commit v1 on v0

v1 whole, which is shorter than its diff:
```python
import functools

import jax
import jax.numpy as jnp
from jax import lax
from jax.experimental import pallas as pl
from jax.experimental.pallas import tpu as pltpu
from jax.sharding import PartitionSpec as P

PANELS = 2
NB = 128
WB = 256
f32 = jnp.float32
bf16 = jnp.bfloat16
TRANS_B = (((1,), (1,)), ((), ()))
TRANS_A = (((0,), (0,)), ((), ()))


def split(x):
    hi = x.astype(bf16)
    return hi, (x - hi.astype(f32)).astype(bf16)


def dot_nn(ah, al, bh, bl):
    return jnp.dot(
        jnp.concatenate([ah, ah, al], 1), jnp.concatenate([bh, bl, bh], 0), preferred_element_type=f32
    )


def dot_nt(ah, al, bh, bl):
    return lax.dot_general(
        jnp.concatenate([ah, ah, al], 1), jnp.concatenate([bh, bl, bh], 1), TRANS_B, preferred_element_type=f32
    )


def dot_tn(ah, al, bh, bl):
    return lax.dot_general(
        jnp.concatenate([ah, ah, al], 0), jnp.concatenate([bh, bl, bh], 0), TRANS_A, preferred_element_type=f32
    )


def spread(x):
    return jnp.broadcast_to(x, (8, NB))


def tree_sum(xs):
    while len(xs) > 1:
        xs = [xs[i] + xs[i + 1] if i + 1 < len(xs) else xs[i] for i in range(0, len(xs), 2)]
    return xs[0]


def factor_tile(t, rows, cols, lane, sub):
    scaled, ratio, inverses, pivots = [], {}, [], None
    for j in range(8):
        pivot = spread(cols[j][j : j + 1, :])
        inv = 1.0 / pivot
        inverses.append(inv)
        pivots = pivot if j == 0 else jnp.where(sub == j, pivot, pivots)
        below = jnp.where(sub > j, cols[j], 0.0)
        for k in range(j + 1, 8):
            entry = spread(cols[k][j : j + 1, :])
            cols[k] = cols[k] - (below * entry) * inv
            ratio[j, k] = entry * inv
        row = spread(rows[j : j + 1, :]) * inv
        row = jnp.where(lane == 8 * t + j, 1.0 + inv, row)
        scaled.append(row)
        if j < 7:
            rows = rows - below * row
    return rows, lax.rsqrt(pivots), scaled, ratio, inverses


def factor_block(tiles, store_u, store_l):
    tiles = list(tiles)
    n = len(tiles)
    lane = lax.broadcasted_iota(jnp.int32, (8, NB), 1)
    sub = lax.broadcasted_iota(jnp.int32, (8, NB), 0)
    cols = [spread(tiles[0][:, k : k + 1]) for k in range(8)]
    for t in range(n):
        last = t + 1 == n
        if not last:
            near = [spread(tiles[t + 1][:, 8 * t + k : 8 * t + k + 1]) for k in range(8)]
            ahead = [spread(tiles[t + 1][:, 8 * t + 8 + k : 8 * t + 9 + k]) for k in range(8)]
        far = {i: [spread(tiles[i][:, 8 * t + k : 8 * t + k + 1]) for k in range(8)] for i in range(t + 2, n)}
        rows, root, scaled, ratio, inverses = factor_tile(t, tiles[t], cols, lane, sub)
        if not last:
            for j in range(8):
                part = near[j] * inverses[j]
                for k in range(j + 1, 8):
                    near[k] = near[k] - near[j] * ratio[j, k]
                for k in range(8):
                    ahead[k] = ahead[k] - near[j] * spread(part[k : k + 1, :])
                tiles[t + 1] = tiles[t + 1] - near[j] * scaled[j]
            cols = ahead
        back = list(scaled)
        for j in range(6, -1, -1):
            for k in range(7, j, -1):
                back[j] = back[j] - ratio[j, k] * back[k]
        for i in range(t + 2, n):
            tiles[i] = tiles[i] - tree_sum([far[i][j] * back[j] for j in range(8)])
        final = rows * root
        diff = lane - sub - 8 * t
        store_u(t, jnp.where(diff >= 0, final, 0.0))
        store_l(t, jnp.where(diff < 0, final, jnp.where(diff == 0, root, 0.0)))


def half_norm_rows(x):
    xf = x.astype(f32)
    hi, lo = split(xf * xf)
    ones = jnp.ones((8, x.shape[1]), bf16)
    total = lax.dot_general(ones, hi, TRANS_B, preferred_element_type=f32)
    total = total + lax.dot_general(ones, lo, TRANS_B, preferred_element_type=f32)
    return 0.5 * total[0:1]


def half_norm_cols(x):
    xf = x.astype(f32)
    return 0.5 * jnp.sum(xf * xf, axis=1, keepdims=True)


def diagonal(n):
    return lax.broadcasted_iota(jnp.int32, (n, n), 0) == lax.broadcasted_iota(jnp.int32, (n, n), 1)


def place(x_ref, base, piece_at, piece, value):
    at = pl.multiple_of(base + piece_at * piece, piece)
    x_ref[pl.ds(at, piece), :] = value


def chain_kernel(at_ref, amp_ref, mine_ref, other_ref, nz_ref, x_ref, uh_ref, ul_ref, inv_ref, a_ref):
    n = a_ref.shape[0]
    count = n // NB
    steps, panels, piece = mine_ref.shape[:3]
    block = n // panels
    me = at_ref[1]
    for m in range(steps):
        for s in range(panels):
            place(x_ref, s * block, me ^ (2 * m), piece, mine_ref[m, s])
            place(x_ref, s * block, me ^ (2 * m + 1), piece, other_ref[m, s])
    amp = amp_ref[0]
    sq_row = half_norm_rows(x_ref[...])
    for i in range(count):
        o = i * NB
        xi = x_ref[o : o + NB, :]
        cross = lax.dot_general(xi, x_ref[o:, :], TRANS_B, preferred_element_type=f32)
        k = amp * jnp.exp(cross - half_norm_cols(xi) - sq_row[:, o:])
        a_ref[o : o + NB, o:] = k
        shift = jnp.where(diagonal(NB), jnp.broadcast_to(nz_ref[:, o : o + NB], (NB, NB)), 0.0)
        a_ref[o : o + NB, o : o + NB] = k[:, :NB] + shift

    def panel(p, carry):
        o = pl.multiple_of(p * NB, NB)
        d = a_ref[pl.ds(o, NB), pl.ds(o, NB)]

        def store_u(t, v):
            a_ref[pl.ds(pl.multiple_of(o + 8 * t, 8), 8), pl.ds(o, NB)] = v

        def store_l(t, v):
            inv_ref[p, 8 * t : 8 * t + 8, :] = v

        factor_block([d[8 * t : 8 * t + 8] for t in range(NB // 8)], store_u, store_l)
        hi, lo = split(a_ref[pl.ds(o, NB), pl.ds(o, NB)])
        uh_ref[pl.ds(o, NB), pl.ds(o, NB)] = hi
        ul_ref[pl.ds(o, NB), pl.ds(o, NB)] = lo
        for k in range(count - 1):

            @pl.when(p == k)
            def _():
                s = k * NB
                e = s + NB
                u = dot_nn(*split(inv_ref[k]), *split(a_ref[s:e, e:]))
                hi, lo = split(u)
                uh_ref[s:e, e:] = hi
                ul_ref[s:e, e:] = lo
                for i in range(k + 1, count):
                    q = i * NB
                    w = q - e
                    a_ref[q : q + NB, q:] = a_ref[q : q + NB, q:] - dot_tn(
                        hi[:, w : w + NB], lo[:, w : w + NB], hi[:, w:], lo[:, w:]
                    )

        return carry

    lax.fori_loop(0, count, panel, 0)


def bulk_kernel(at_ref, amp_ref, *refs):
    *piece_refs, x_ref, uh_ref, ul_ref, inv_ref, nz_ref, out_ref, f_ref, ph_ref, pl_ref, wh_ref, wl_ref = refs
    n = x_ref.shape[0]
    block = n // PANELS
    piece = piece_refs[0].shape[1]
    nrows = nz_ref.shape[0]
    nblocks = f_ref.shape[0] // block
    ncols = nblocks - nrows
    row_at, me, row_n, col_n = at_ref[0], at_ref[1], at_ref[2], at_ref[3]
    amp = amp_ref[0]
    for k, ref in enumerate(piece_refs):
        for b in range(nblocks):
            place(f_ref, b * block, me ^ k, piece, ref[b])
    for q in range(n // WB):
        first, second = inv_ref[2 * q], inv_ref[2 * q + 1]
        s = q * WB
        corner = dot_tn(
            uh_ref[s : s + NB, s + NB : s + WB], ul_ref[s : s + NB, s + NB : s + WB], *split(first)
        )
        corner = -dot_nn(*split(second), *split(corner))
        zero = jnp.zeros((NB, NB), f32)
        full = jnp.concatenate(
            [jnp.concatenate([first, zero], 1), jnp.concatenate([corner, second], 1)], 0
        )
        wh_ref[q], wl_ref[q] = split(full)
    lead_sq = half_norm_rows(x_ref[...])
    chunk = 256

    def solve(step, carry):
        b = step // (block // chunk)
        number = jnp.where(b < nrows, b * row_n + row_at, (b - nrows) * col_n + me)
        o = pl.multiple_of(step * chunk, chunk)

        @pl.when(number >= PANELS)
        def _():
            xb = f_ref[pl.ds(o, chunk), :]
            sq = half_norm_cols(xb)
            for q in range(n // WB):
                s = q * WB
                cross = lax.dot_general(xb, x_ref[s : s + WB, :], TRANS_B, preferred_element_type=f32)
                acc = amp * jnp.exp(cross - sq - lead_sq[:, s : s + WB])
                if q:
                    acc = acc - dot_nn(
                        ph_ref[pl.ds(o, chunk), 0:s],
                        pl_ref[pl.ds(o, chunk), 0:s],
                        uh_ref[0:s, s : s + WB],
                        ul_ref[0:s, s : s + WB],
                    )
                hi, lo = split(dot_nt(*split(acc), wh_ref[q], wl_ref[q]))
                ph_ref[pl.ds(o, chunk), s : s + WB] = hi
                pl_ref[pl.ds(o, chunk), s : s + WB] = lo

        return carry

    lax.fori_loop(0, nblocks * (block // chunk), solve, 0)
    for b in range(ncols):
        j = b * col_n + me
        fo = (nrows + b) * block
        xc = f_ref[fo : fo + block, :]
        col_sq = half_norm_rows(xc)
        for a in range(nrows):
            i = a * row_n + row_at

            @pl.when((i >= PANELS) & (j >= PANELS))
            def _():
                for h in range(block // chunk):
                    o = a * block + h * chunk
                    xr = f_ref[o : o + chunk, :]
                    cross = lax.dot_general(xr, xc, TRANS_B, preferred_element_type=f32)
                    k = amp * jnp.exp(cross - half_norm_cols(xr) - col_sq)
                    row_id = lax.broadcasted_iota(jnp.int32, (chunk, block), 0) + h * chunk
                    col_id = lax.broadcasted_iota(jnp.int32, (chunk, block), 1)
                    on_diag = (row_id == col_id) & (i == j)
                    k = k + jnp.where(on_diag, jnp.broadcast_to(nz_ref[a : a + 1, :], (chunk, block)), 0.0)
                    out_ref[o : o + chunk, b * block : (b + 1) * block] = k - dot_nt(
                        ph_ref[o : o + chunk, :],
                        pl_ref[o : o + chunk, :],
                        ph_ref[fo : fo + block, :],
                        pl_ref[fo : fo + block, :],
                    )

            @pl.when((i >= PANELS) & (j < PANELS))
            def _():
                w = pl.multiple_of(j * block, block)
                rows = slice(a * block, (a + 1) * block)
                out_ref[rows, b * block : (b + 1) * block] = ph_ref[rows, pl.ds(w, block)].astype(f32) + pl_ref[
                    rows, pl.ds(w, block)
                ].astype(f32)

            @pl.when((i < PANELS) & (j > i))
            def _():
                out_ref[a * block : (a + 1) * block, b * block : (b + 1) * block] = jnp.zeros((block, block), f32)

            @pl.when((i < PANELS) & (j <= i))
            def _():
                v = pl.multiple_of(j * block, block)
                w = pl.multiple_of(i * block, block)
                u = uh_ref[pl.ds(v, block), pl.ds(w, block)].astype(f32)
                u = u + ul_ref[pl.ds(v, block), pl.ds(w, block)].astype(f32)
                row_id = lax.broadcasted_iota(jnp.int32, (block, block), 0)
                col_id = lax.broadcasted_iota(jnp.int32, (block, block), 1)
                keep = (row_id >= col_id) | (j < i)
                out_ref[a * block : (a + 1) * block, b * block : (b + 1) * block] = jnp.where(keep, u.T, 0.0)


SMEM = pl.BlockSpec(memory_space=pltpu.SMEM)
VMEM = pl.BlockSpec(memory_space=pltpu.VMEM)


def exchange(x, axis, k):
    return lax.ppermute(x, axis, [(i, i ^ k) for i in range(lax.axis_size(axis))])


def local(features, amplitude, noise):
    row_n = lax.axis_size("row")
    col_n = lax.axis_size("col")
    row_at = lax.axis_index("row")
    col_at = lax.axis_index("col")
    nrows, _, piece, width = features.shape
    block = piece * col_n
    ncols = nrows * row_n // col_n
    n = PANELS * block
    mine = features.reshape(nrows, piece, width)
    noise_rows = noise.reshape(nrows, block)
    lead_noise = lax.all_gather(noise_rows[0], "row")[:PANELS].reshape(1, n)
    plane = jnp.stack([mine] + [exchange(mine, "row", k) for k in range(1, row_n)])
    lead = jnp.stack(
        [lax.dynamic_index_in_dim(plane[:, 0], row_at ^ s, 0, keepdims=False) for s in range(PANELS)]
    )
    near = jnp.stack([lead] + [exchange(lead, "col", k) for k in range(2, col_n, 2)])
    other = exchange(near, "col", 1)
    near, other, plane, mine = lax.optimization_barrier((near, other, plane, mine))

    def for_col(to):
        out = [mine]
        for b in range(ncols):
            number = b * col_n + to
            out.append(
                lax.dynamic_slice(
                    plane, (row_at ^ (number % row_n), number // row_n, 0, 0), (1, 1, piece, width)
                ).reshape(1, piece, width)
            )
        return jnp.concatenate(out, 0)

    pieces = [for_col(col_at)] + [exchange(for_col(col_at ^ k), "col", k) for k in range(1, col_n)]
    at = jnp.stack([row_at, col_at, jnp.int32(row_n), jnp.int32(col_n)])
    half = jax.ShapeDtypeStruct((n, n), bf16)
    points, uh, ul, inverse = pl.pallas_call(
        chain_kernel,
        out_shape=[
            jax.ShapeDtypeStruct((n, width), bf16),
            half,
            half,
            jax.ShapeDtypeStruct((n // NB, NB, NB), f32),
        ],
        in_specs=[SMEM, SMEM, VMEM, VMEM, VMEM],
        out_specs=[VMEM] * 4,
        scratch_shapes=[pltpu.VMEM((n, n), f32)],
        compiler_params=pltpu.CompilerParams(vmem_limit_bytes=40 << 20),
        cost_estimate=pl.CostEstimate(flops=40_000_000_000, bytes_accessed=8_000_000, transcendentals=0),
        name="chain",
    )(at, amplitude, near, other, lead_noise)
    nblocks = nrows + ncols
    out = pl.pallas_call(
        bulk_kernel,
        out_shape=jax.ShapeDtypeStruct((nrows * block, ncols * block), f32),
        in_specs=[SMEM, SMEM] + [VMEM] * (len(pieces) + 5),
        out_specs=VMEM,
        scratch_shapes=[
            pltpu.VMEM((nblocks * block, width), bf16),
            pltpu.VMEM((nblocks * block, n), bf16),
            pltpu.VMEM((nblocks * block, n), bf16),
            pltpu.VMEM((n // WB, WB, WB), bf16),
            pltpu.VMEM((n // WB, WB, WB), bf16),
        ],
        compiler_params=pltpu.CompilerParams(vmem_limit_bytes=56 << 20),
        cost_estimate=pl.CostEstimate(flops=12_000_000_000, bytes_accessed=8_000_000, transcendentals=0),
        name="bulk",
    )(at, amplitude, *pieces, points, uh, ul, inverse, noise_rows)
    return out.reshape(nrows, 1, block, ncols, 1, block)


def solution(mesh):
    return jax.shard_map(
        local,
        mesh=mesh,
        in_specs=(P(None, "row", "col", None), P(), P(None, "row", None)),
        out_specs=P(None, "row", None, None, "col", None),
        check_vma=False,
    )
```

time: 523 us -> 109 us (0.21); the launches traced: 516 us -> 109 us
  other arithmetic: 259 us -> 1.94 us
  matrix products: 97.3 us -> 0 us
  waiting for transfers between devices: 83.9 us -> 13.2 us
  Pallas kernels: 0 us -> 55.6 us
  local copies, waits for them, and re-layouts: 49.6 us -> 11.1 us
  starting transfers between devices: 0.04 us -> 19.5 us
  between operations: 20.2 us -> 0.87 us
    another operation x38 -> x4, other arithmetic: 242 us -> 1.14 us  [the longest x1 0.97 us: local(): jnp.stack([mine] + [exchange(mine, 'row', k) for k in range(1, row_n)])]
    dot_general x14 -> x0, matrix products: 70.9 us -> none  [the longest x3 22.1 us: trail_update(): jnp.einsum('aip,bjp->aibj', left_panel, right_panel, precision=HIGHEST)]
    psum x1 -> x0, waiting for transfers between devices: 59.6 us -> none  [from_root(): return lax.psum(jnp.where(mine, x, jnp.zeros_like(x)), axis)]
    pallas_call x0 -> x2, Pallas kernels: none -> 55.6 us  [the longest x1 29.1 us: local(): pl.pallas_call(chain_kernel, out_shape=[jax.ShapeDtypeStruct((n, width),...]
    another operation x26 -> x0, matrix products: 26.4 us -> none  [the longest x14 15.4 us: factor_block(): inverse = jax.scipy.linalg.solve_triangular(lower, ident, lower=True)]
    another operation x36 -> x0, local copies, waits for them, and re-layouts: 25 us -> none  [the longest x27 23.6 us: factor_block(): inverse = jax.scipy.linalg.solve_triangular(lower, ident, lower=True)]
    all_gather x1 -> x0, waiting for transfers between devices: 23.6 us -> none  [local(): gathered = lax.all_gather(features, 'col', axis=2, tiled=True)]
    ppermute x0 -> x14, starting transfers between devices: none -> 19.5 us  [exchange(): lax.ppermute(x, axis, [(i, i ^ k) for i in range(lax.axis_size(axis))])]
  transfers between devices with their start and end apart: 2 -> 14, of which waited for: 2 -> 4; matrix products, arithmetic and copies ran while one was open for 1% -> 1% of each run, Pallas kernels for 0% -> 27%
where the time goes in v1:
time: 109 us
  Pallas kernels  55.6 us (51%)
  starting transfers between devices  19.5 us (18%)
  waiting for transfers between devices  13.2 us (12%)
  local copies, waits for them, and re-layouts  11.1 us (10%)
  blocking collectives  6.72 us (6%)
  other arithmetic  1.94 us (2%)
    pallas_call x1, Pallas kernels, local(): pl.pallas_call(chain_kernel, out_shape=[jax.ShapeDtypeStruct((n, width),...  29.1 us
    pallas_call x1, Pallas kernels, local(): pl.pallas_call(bulk_kernel, out_shape=jax.ShapeDtypeStruct((nrows * block...  26.5 us
    ppermute x14, starting transfers between devices, exchange(): lax.ppermute(x, axis, [(i, i ^ k) for i in range(lax.axis_size(axis))])  19.5 us
    ppermute x14, waiting for transfers between devices, exchange(): lax.ppermute(x, axis, [(i, i ^ k) for i in range(lax.axis_size(axis))])  13.2 us
    all_gather x1, blocking collectives, local(): lead_noise = lax.all_gather(noise_rows[0], 'row')[:PANELS].reshape(1, n)  6.72 us
    unnamed x29, local copies, waits for them, and re-layouts  5.99 us
    reshape x1, local copies, waits for them, and re-layouts, local(): return out.reshape(nrows, 1, block, ncols, 1, block)  5.06 us
  transfers between devices with their start and end apart: 14, of which 4 were waited for; matrix products, arithmetic and copies ran while one was open for 1% of the time, Pallas kernels for 27%

profile of v1, /device:TPU:31, one launch (start us, length us, event | category | flops | bytes accessed | tf_op | source)
XLA Modules:
  0.0 109.0 jit_solution(815440915877755046)
XLA Ops:
  0.0 0.2 collective-permute-start.2
  0.2 1.2 %collective-permute-start.1 = (bf16[2,64,512]{2,1,0:T(8,128)(2,1)}, bf16[2,64,512]{2,1,0:T(8,128)(2,1)S(1)}, u32[]{:S(2)}, u32[]{:S(2)}) collective-permute-start(bf16[2,64,512]{2,1,0:T(8,128)(2,1)} %bitcast.40), channel_id=1, source_target_pairs={{0,16},{8,24},{16,0},{24,8},{1,17},{9,25},{17,1},{25,9},{2,18},{10... | collective-permute-start | bytes 393224 | tf_op jit(solution)/shard_map/ppermute | solution.py:296
  1.4 1.2 %collective-permute-start = (bf16[2,64,512]{2,1,0:T(8,128)(2,1)}, bf16[2,64,512]{2,1,0:T(8,128)(2,1)S(1)}, u32[]{:S(2)}, u32[]{:S(2)}) collective-permute-start(bf16[2,64,512]{2,1,0:T(8,128)(2,1)} %bitcast.41), channel_id=1, source_target_pairs={{0,8},{8,0},{16,24},{24,16},{1,9},{9,1},{17,25},{25,17},{2,10},{10... | collective-permute-start | bytes 393224 | tf_op jit(solution)/shard_map/ppermute | solution.py:296
  2.6 2.9 %collective-permute-done.2 = bf16[2,64,512]{2,1,0:T(8,128)(2,1)S(1)} collective-permute-done((bf16[2,64,512]{2,1,0:T(8,128)(2,1)}, bf16[2,64,512]{2,1,0:T(8,128)(2,1)S(1)}, u32[]{:S(2)}, u32[]{:S(2)}) %collective-permute-start.2) | collective-permute-done | bytes 131104 | tf_op jit(solution)/shard_map/ppermute | solution.py:296
  5.6 2.3 %collective-permute-done.1 = bf16[2,64,512]{2,1,0:T(8,128)(2,1)S(1)} collective-permute-done((bf16[2,64,512]{2,1,0:T(8,128)(2,1)}, bf16[2,64,512]{2,1,0:T(8,128)(2,1)S(1)}, u32[]{:S(2)}, u32[]{:S(2)}) %collective-permute-start.1) | collective-permute-done | bytes 131104 | tf_op jit(solution)/shard_map/ppermute | solution.py:296
  7.9 0.0 collective-permute-done
  7.9 1.0 pad_maximum_fusion
  8.9 0.0 copy-start.5
  9.0 0.1 collective-permute-start.4
  9.1 0.2 collective-permute-start.3
  9.3 3.3 %collective-permute-start.5 = (bf16[2,64,512]{2,1,0:T(8,128)(2,1)S(1)}, bf16[2,64,512]{2,1,0:T(8,128)(2,1)S(1)}, u32[]{:S(2)}, u32[]{:S(2)}) collective-permute-start(bf16[2,64,512]{2,1,0:T(8,128)(2,1)S(1)} %get-tuple-element.40), channel_id=1, source_target_pairs={{0,6},{1,7},{2,4},{3,5},{4,2},{5,3},{6,0},{7,1},{8,14},{9,15},{10,... | collective-permute-start | bytes 393224 | tf_op jit(solution)/shard_map/ppermute | solution.py:296
  12.6 6.4 %collective-permute-done.4 = bf16[2,64,512]{2,1,0:T(8,128)(2,1)S(1)} collective-permute-done((bf16[2,64,512]{2,1,0:T(8,128)(2,1)S(1)}, bf16[2,64,512]{2,1,0:T(8,128)(2,1)S(1)}, u32[]{:S(2)}, u32[]{:S(2)}) %collective-permute-start.4) | collective-permute-done | bytes 131104 | tf_op jit(solution)/shard_map/ppermute | solution.py:296
  19.0 0.0 collective-permute-done.3
  19.0 0.0 collective-permute-done.5
  19.0 0.1 pad_maximum_fusion.1.mine_ref
  19.1 0.0 copy-start.6
  19.1 0.0 slice-start
  19.1 2.9 %collective-permute-start.6 = (bf16[4,2,64,512]{3,2,1,0:T(8,128)(2,1)S(1)}, bf16[4,2,64,512]{3,2,1,0:T(8,128)(2,1)S(1)}, u32[]{:S(2)}, u32[]{:S(2)}) collective-permute-start(bf16[4,2,64,512]{3,2,1,0:T(8,128)(2,1)S(1)} %pad_maximum_fusion.1.mine_ref), channel_id=1, source_target_pairs={{0,1},{1,0},{2,3},{3,2},{4,5},{5,4},{6,7},{7,6},{8,9},{9,8},{10,11... | collective-permute-start | bytes 1572872 | tf_op jit(solution)/shard_map/ppermute | solution.py:296
  22.0 1.5 %collective-permute-done.6.other_ref = bf16[4,2,64,512]{3,2,1,0:T(8,128)(2,1)S(1)} collective-permute-done((bf16[4,2,64,512]{3,2,1,0:T(8,128)(2,1)S(1)}, bf16[4,2,64,512]{3,2,1,0:T(8,128)(2,1)S(1)}, u32[]{:S(2)}, u32[]{:S(2)}) %collective-permute-start.6) | collective-permute-done | bytes 524320 | tf_op jit(solution)/shard_map/ppermute | solution.py:296
  23.5 0.8 pad_maximum_fusion.2
  24.3 1.0 collective-permute-start.13
  25.4 0.1 collective-permute-start.7
  25.5 0.6 copy.8
  26.8 6.7 %all-gather = f32[4,1,512]{2,1,0:T(1,128)S(1)} all-gather(f32[1,1,512]{2,1,0:T(1,128)S(1)} %slice-done), channel_id=2, replica_groups=mesh['row'=4,'col'=8] {'row'}, dimensions={0}, use_global_device_ids=true | all-gather | bytes 10240 | tf_op jit(solution)/shard_map/all_gather | solution.py:310
  33.5 0.1 pad_add_fusion.at_ref
  33.6 2.1 %collective-permute-start.8 = (bf16[3,64,512]{2,1,0:T(8,128)(2,1)S(1)}, bf16[3,64,512]{2,1,0:T(8,128)(2,1)S(1)}, u32[]{:S(2)}, u32[]{:S(2)}) collective-permute-start(bf16[3,64,512]{2,1,0:T(8,128)(2,1)S(1)} %get-tuple-element.33), channel_id=1, source_target_pairs={{0,2},{1,3},{2,0},{3,1},{4,6},{5,7},{6,4},{7,5},{8,10},{9,11},{10,... | collective-permute-start | bytes 589832 | tf_op jit(solution)/shard_map/ppermute | solution.py:296
  35.7 1.7 %collective-permute-start.9 = (bf16[3,64,512]{2,1,0:T(8,128)(2,1)S(1)}, bf16[3,64,512]{2,1,0:T(8,128)(2,1)S(1)}, u32[]{:S(2)}, u32[]{:S(2)}) collective-permute-start(bf16[3,64,512]{2,1,0:T(8,128)(2,1)S(1)} %get-tuple-element.34), channel_id=1, source_target_pairs={{0,3},{1,2},{2,1},{3,0},{4,7},{5,6},{6,5},{7,4},{8,11},{9,10},{10,... | collective-permute-start | bytes 589832 | tf_op jit(solution)/shard_map/ppermute | solution.py:296
  37.4 3.1 %collective-permute-start.10 = (bf16[3,64,512]{2,1,0:T(8,128)(2,1)S(1)}, bf16[3,64,512]{2,1,0:T(8,128)(2,1)S(1)}, u32[]{:S(2)}, u32[]{:S(2)}) collective-permute-start(bf16[3,64,512]{2,1,0:T(8,128)(2,1)S(1)} %get-tuple-element.35), channel_id=1, source_target_pairs={{0,4},{1,5},{2,6},{3,7},{4,0},{5,1},{6,2},{7,3},{8,12},{9,13},{10,... | collective-permute-start | bytes 589832 | tf_op jit(solution)/shard_map/ppermute | solution.py:296
  40.4 0.0 collective-permute-done.13.refs_7_
  40.5 0.0 collective-permute-start.11
  40.5 0.0 collective-permute-done.7.refs_1_
  40.5 2.3 %collective-permute-start.12 = (bf16[3,64,512]{2,1,0:T(8,128)(2,1)S(1)}, bf16[3,64,512]{2,1,0:T(8,128)(2,1)S(1)}, u32[]{:S(2)}, u32[]{:S(2)}) collective-permute-start(bf16[3,64,512]{2,1,0:T(8,128)(2,1)S(1)} %get-tuple-element.37), channel_id=1, source_target_pairs={{0,6},{1,7},{2,4},{3,5},{4,2},{5,3},{6,0},{7,1},{8,14},{9,15},{10,... | collective-permute-start | bytes 589832 | tf_op jit(solution)/shard_map/ppermute | solution.py:296
  42.8 29.1 %chain.1 = (bf16[1024,512]{1,0:T(8,128)(2,1)S(1)}, bf16[1024,1024]{1,0:T(8,128)(2,1)S(1)}, bf16[1024,1024]{1,0:T(8,128)(2,1)S(1)}, f32[8,128,128]{2,1,0:T(8,128)S(1)}) custom-call(s32[4]{0:T(128)S(1)} %pad_add_fusion.at_ref, f32[1]{0:T(128)S(6)} %copy.9.amp_ref, bf16[4,2,64,512]{3,2,1,0:T(8,128)(2,1)S(1)} %pad_maximum_fusion.1.mine_ref, ...), custom_call_target="tpu_custom_call" | custom-call | flops 40000000000 | bytes 8000000 | tf_op jit(solution)/shard_map/chain/pallas_call | solution.py:333
  71.9 0.0 copy-start.1
  71.9 1.3 %copy-done.1 = bf16[1024,1024]{1,0:T(8,128)(2,1)} copy-done((bf16[1024,1024]{1,0:T(8,128)(2,1)}, bf16[1024,1024]{1,0:T(8,128)(2,1)S(1)}, u32[]{:S(2)}) %copy-start.1) | copy-done | bytes 2097176
  73.3 1.3 %copy-done.2 = bf16[1024,1024]{1,0:T(8,128)(2,1)} copy-done((bf16[1024,1024]{1,0:T(8,128)(2,1)}, bf16[1024,1024]{1,0:T(8,128)(2,1)S(1)}, u32[]{:S(2)}) %copy-start.2) | copy-done | bytes 2097176
  74.6 1.0 copy-done.3
  75.6 0.8 copy-done.4
  76.4 0.0 collective-permute-done.8.refs_2_
  76.5 0.0 collective-permute-done.10.refs_4_
  76.5 0.0 collective-permute-done.12.refs_6_
  76.5 0.6 copy-done.9
  77.1 0.1 copy-done.10
  77.2 0.1 copy-done.11
  77.3 0.1 copy-done.12
  77.3 0.1 copy-done.13
  77.4 26.5 %bulk.1 = f32[1024,512]{1,0:T(8,128)} custom-call(s32[4]{0:T(128)} %copy-done, f32[1]{0:T(128)S(6)} %copy.9.amp_ref, bf16[3,64,512]{2,1,0:T(8,128)(2,1)} %get-tuple-element.38.refs_0_, bf16[3,64,512]{2,1,0:T(8,128)(2,1)} %copy-done.8, bf16[3,64,512]{2,1,0:T(8,128)(2,1)} %copy-done.9, bf16[3,64,512]{2,1,0:T(8,128)(2,1)} %copy-done.10, ...), custom_call_target="tpu_custom_call" | custom-call | flops 12000000000 | bytes 8000000 | tf_op jit(solution)/shard_map/bulk/pallas_call | solution.py:349
  103.9 5.1 %copy.5 = f32[2,1,512,1,1,512]{5,4,3,2,1,0:T(1,128)} copy(f32[2,1,512,1,1,512]{5,2,0,4,3,1:T(8,128)} %bitcast.38) | data formatting | bytes 4194304 | tf_op jit(solution)/shard_map/reshape | solution.py:365
  (24 shorter events, 0.1 us)
Async XLA Ops:
  0.0 5.6 %collective-permute-start.2 = (bf16[2,64,512]{2,1,0:T(8,128)(2,1)}, bf16[2,64,512]{2,1,0:T(8,128)(2,1)S(1)}, u32[]{:S(2)}, u32[]{:S(2)}) collective-permute-start(bf16[2,64,512]{2,1,0:T(8,128)(2,1)} %bitcast.39), channel_id=1, source_target_pairs={{0,24},{8,16},{16,8},{24,0},{1,25},{9,17},{17,9},{25,1},{2,26},{10... | collective-permute-start | bytes 393224 | tf_op jit(solution)/shard_map/ppermute | solution.py:296
  0.2 7.7 %collective-permute-start.1 = (bf16[2,64,512]{2,1,0:T(8,128)(2,1)}, bf16[2,64,512]{2,1,0:T(8,128)(2,1)S(1)}, u32[]{:S(2)}, u32[]{:S(2)}) collective-permute-start(bf16[2,64,512]{2,1,0:T(8,128)(2,1)} %bitcast.40), channel_id=1, source_target_pairs={{0,16},{8,24},{16,0},{24,8},{1,17},{9,25},{17,1},{25,9},{2,18},{10... | collective-permute-start | bytes 393224 | tf_op jit(solution)/shard_map/ppermute | solution.py:296
  1.4 6.4 %collective-permute-start = (bf16[2,64,512]{2,1,0:T(8,128)(2,1)}, bf16[2,64,512]{2,1,0:T(8,128)(2,1)S(1)}, u32[]{:S(2)}, u32[]{:S(2)}) collective-permute-start(bf16[2,64,512]{2,1,0:T(8,128)(2,1)} %bitcast.41), channel_id=1, source_target_pairs={{0,8},{8,0},{16,24},{24,16},{1,9},{9,1},{17,25},{25,17},{2,10},{10... | collective-permute-start | bytes 393224 | tf_op jit(solution)/shard_map/ppermute | solution.py:296
  8.9 14.7 %copy-start.5 = (bf16[2,1,64,512]{3,2,1,0:T(8,128)(2,1)S(1)}, bf16[2,1,64,512]{3,2,1,0:T(8,128)(2,1)}, u32[]{:S(2)}) copy-start(bf16[2,1,64,512]{3,2,1,0:T(8,128)(2,1)} %param.3) | copy-start | bytes 393220
  9.0 10.0 %collective-permute-start.4 = (bf16[2,64,512]{2,1,0:T(8,128)(2,1)S(1)}, bf16[2,64,512]{2,1,0:T(8,128)(2,1)S(1)}, u32[]{:S(2)}, u32[]{:S(2)}) collective-permute-start(bf16[2,64,512]{2,1,0:T(8,128)(2,1)S(1)} %get-tuple-element.40), channel_id=1, source_target_pairs={{0,4},{1,5},{2,6},{3,7},{4,0},{5,1},{6,2},{7,3},{8,12},{9,13},{10,... | collective-permute-start | bytes 393224 | tf_op jit(solution)/shard_map/ppermute | solution.py:296
  9.1 9.9 %collective-permute-start.3 = (bf16[2,64,512]{2,1,0:T(8,128)(2,1)S(1)}, bf16[2,64,512]{2,1,0:T(8,128)(2,1)S(1)}, u32[]{:S(2)}, u32[]{:S(2)}) collective-permute-start(bf16[2,64,512]{2,1,0:T(8,128)(2,1)S(1)} %get-tuple-element.40), channel_id=1, source_target_pairs={{0,2},{1,3},{2,0},{3,1},{4,6},{5,7},{6,4},{7,5},{8,10},{9,11},{10,... | collective-permute-start | bytes 393224 | tf_op jit(solution)/shard_map/ppermute | solution.py:296
  9.3 9.7 %collective-permute-start.5 = (bf16[2,64,512]{2,1,0:T(8,128)(2,1)S(1)}, bf16[2,64,512]{2,1,0:T(8,128)(2,1)S(1)}, u32[]{:S(2)}, u32[]{:S(2)}) collective-permute-start(bf16[2,64,512]{2,1,0:T(8,128)(2,1)S(1)} %get-tuple-element.40), channel_id=1, source_target_pairs={{0,6},{1,7},{2,4},{3,5},{4,2},{5,3},{6,0},{7,1},{8,14},{9,15},{10,... | collective-permute-start | bytes 393224 | tf_op jit(solution)/shard_map/ppermute | solution.py:296
  19.1 6.5 %copy-start.6 = (f32[2,1,512]{2,1,0:T(1,128)S(1)}, f32[2,1,512]{2,1,0:T(1,128)}, u32[]{:S(2)}) copy-start(f32[2,1,512]{2,1,0:T(1,128)} %param.5) | copy-start | bytes 12292
  19.1 7.7 %slice-start = ((f32[2,1,512]{2,1,0:T(1,128)}), f32[1,1,512]{2,1,0:T(1,128)S(1)}, s32[]{:S(2)}) async-start(f32[2,1,512]{2,1,0:T(1,128)} %param.5), calls=%async_computation | async-start | bytes 4096 | tf_op jit(solution)/shard_map/slice | solution.py:310
  19.1 4.4 %collective-permute-start.6 = (bf16[4,2,64,512]{3,2,1,0:T(8,128)(2,1)S(1)}, bf16[4,2,64,512]{3,2,1,0:T(8,128)(2,1)S(1)}, u32[]{:S(2)}, u32[]{:S(2)}) collective-permute-start(bf16[4,2,64,512]{3,2,1,0:T(8,128)(2,1)S(1)} %pad_maximum_fusion.1.mine_ref), channel_id=1, source_target_pairs={{0,1},{1,0},{2,3},{3,2},{4,5},{5,4},{6,7},{7,6},{8,9},{9,8},{10,11... | collective-permute-start | bytes 1572872 | tf_op jit(solution)/shard_map/ppermute | solution.py:296
  24.3 16.1 %collective-permute-start.13 = (bf16[3,64,512]{2,1,0:T(8,128)(2,1)S(1)}, bf16[3,64,512]{2,1,0:T(8,128)(2,1)S(1)}, u32[]{:S(2)}, u32[]{:S(2)}) collective-permute-start(bf16[3,64,512]{2,1,0:T(8,128)(2,1)S(1)} %get-tuple-element.31), channel_id=1, source_target_pairs={{0,7},{1,6},{2,5},{3,4},{4,3},{5,2},{6,1},{7,0},{8,15},{9,14},{10,... | collective-permute-start | bytes 589832 | tf_op jit(solution)/shard_map/ppermute | solution.py:296
  25.4 15.1 %collective-permute-start.7 = (bf16[3,64,512]{2,1,0:T(8,128)(2,1)S(1)}, bf16[3,64,512]{2,1,0:T(8,128)(2,1)S(1)}, u32[]{:S(2)}, u32[]{:S(2)}) collective-permute-start(bf16[3,64,512]{2,1,0:T(8,128)(2,1)S(1)} %get-tuple-element.32), channel_id=1, source_target_pairs={{0,1},{1,0},{2,3},{3,2},{4,5},{5,4},{6,7},{7,6},{8,9},{9,8},{10,11... | collective-permute-start | bytes 589832 | tf_op jit(solution)/shard_map/ppermute | solution.py:296
  33.6 38.3 %copy-start = (s32[4]{0:T(128)}, s32[4]{0:T(128)S(1)}, u32[]{:S(2)}) copy-start(s32[4]{0:T(128)S(1)} %pad_add_fusion.at_ref) | copy-start | bytes 52
  33.6 42.9 %collective-permute-start.8 = (bf16[3,64,512]{2,1,0:T(8,128)(2,1)S(1)}, bf16[3,64,512]{2,1,0:T(8,128)(2,1)S(1)}, u32[]{:S(2)}, u32[]{:S(2)}) collective-permute-start(bf16[3,64,512]{2,1,0:T(8,128)(2,1)S(1)} %get-tuple-element.33), channel_id=1, source_target_pairs={{0,2},{1,3},{2,0},{3,1},{4,6},{5,7},{6,4},{7,5},{8,10},{9,11},{10,... | collective-permute-start | bytes 589832 | tf_op jit(solution)/shard_map/ppermute | solution.py:296
  35.7 40.8 %collective-permute-start.9 = (bf16[3,64,512]{2,1,0:T(8,128)(2,1)S(1)}, bf16[3,64,512]{2,1,0:T(8,128)(2,1)S(1)}, u32[]{:S(2)}, u32[]{:S(2)}) collective-permute-start(bf16[3,64,512]{2,1,0:T(8,128)(2,1)S(1)} %get-tuple-element.34), channel_id=1, source_target_pairs={{0,3},{1,2},{2,1},{3,0},{4,7},{5,6},{6,5},{7,4},{8,11},{9,10},{10,... | collective-permute-start | bytes 589832 | tf_op jit(solution)/shard_map/ppermute | solution.py:296
  37.4 39.1 %collective-permute-start.10 = (bf16[3,64,512]{2,1,0:T(8,128)(2,1)S(1)}, bf16[3,64,512]{2,1,0:T(8,128)(2,1)S(1)}, u32[]{:S(2)}, u32[]{:S(2)}) collective-permute-start(bf16[3,64,512]{2,1,0:T(8,128)(2,1)S(1)} %get-tuple-element.35), channel_id=1, source_target_pairs={{0,4},{1,5},{2,6},{3,7},{4,0},{5,1},{6,2},{7,3},{8,12},{9,13},{10,... | collective-permute-start | bytes 589832 | tf_op jit(solution)/shard_map/ppermute | solution.py:296
  40.5 31.5 %copy-start.7 = (bf16[3,64,512]{2,1,0:T(8,128)(2,1)}, bf16[3,64,512]{2,1,0:T(8,128)(2,1)S(1)}, u32[]{:S(2)}) copy-start(bf16[3,64,512]{2,1,0:T(8,128)(2,1)S(1)} %collective-permute-done.13.refs_7_) | copy-start | bytes 589828
  40.5 36.0 %collective-permute-start.11 = (bf16[3,64,512]{2,1,0:T(8,128)(2,1)S(1)}, bf16[3,64,512]{2,1,0:T(8,128)(2,1)S(1)}, u32[]{:S(2)}, u32[]{:S(2)}) collective-permute-start(bf16[3,64,512]{2,1,0:T(8,128)(2,1)S(1)} %get-tuple-element.36), channel_id=1, source_target_pairs={{0,5},{1,4},{2,7},{3,6},{4,1},{5,0},{6,3},{7,2},{8,13},{9,12},{10,... | collective-permute-start | bytes 589832 | tf_op jit(solution)/shard_map/ppermute | solution.py:296
  40.5 31.5 %copy-start.8 = (bf16[3,64,512]{2,1,0:T(8,128)(2,1)}, bf16[3,64,512]{2,1,0:T(8,128)(2,1)S(1)}, u32[]{:S(2)}) copy-start(bf16[3,64,512]{2,1,0:T(8,128)(2,1)S(1)} %collective-permute-done.7.refs_1_) | copy-start | bytes 589828
  40.5 36.0 %collective-permute-start.12 = (bf16[3,64,512]{2,1,0:T(8,128)(2,1)S(1)}, bf16[3,64,512]{2,1,0:T(8,128)(2,1)S(1)}, u32[]{:S(2)}, u32[]{:S(2)}) collective-permute-start(bf16[3,64,512]{2,1,0:T(8,128)(2,1)S(1)} %get-tuple-element.37), channel_id=1, source_target_pairs={{0,6},{1,7},{2,4},{3,5},{4,2},{5,3},{6,0},{7,1},{8,14},{9,15},{10,... | collective-permute-start | bytes 589832 | tf_op jit(solution)/shard_map/ppermute | solution.py:296
  71.9 1.3 %copy-start.1 = (bf16[1024,1024]{1,0:T(8,128)(2,1)}, bf16[1024,1024]{1,0:T(8,128)(2,1)S(1)}, u32[]{:S(2)}) copy-start(bf16[1024,1024]{1,0:T(8,128)(2,1)S(1)} %get-tuple-element.18.refs_9_) | copy-start | bytes 6291460
  73.3 1.4 %copy-start.2 = (bf16[1024,1024]{1,0:T(8,128)(2,1)}, bf16[1024,1024]{1,0:T(8,128)(2,1)S(1)}, u32[]{:S(2)}) copy-start(bf16[1024,1024]{1,0:T(8,128)(2,1)S(1)} %get-tuple-element.19.refs_10_) | copy-start | bytes 6291460
  74.6 1.0 copy-start.3
  75.6 0.8 copy-start.4
  76.4 0.7 copy-start.9
  76.5 0.8 copy-start.10
  76.5 0.8 copy-start.11
  76.5 0.8 copy-start.12
  76.5 0.9 copy-start.13

commit v2 on v1

v2 whole, which is shorter than its diff:
```python
import functools

import jax
import jax.numpy as jnp
from jax import lax
from jax.experimental import pallas as pl
from jax.experimental.pallas import tpu as pltpu
from jax.sharding import PartitionSpec as P

PANELS = 2
NB = 128
WB = 256
f32 = jnp.float32
bf16 = jnp.bfloat16
TRANS_B = (((1,), (1,)), ((), ()))
TRANS_A = (((0,), (0,)), ((), ()))


def split(x):
    hi = x.astype(bf16)
    return hi, (x - hi.astype(f32)).astype(bf16)


def dot_nn(ah, al, bh, bl):
    return jnp.dot(
        jnp.concatenate([ah, ah, al], 1), jnp.concatenate([bh, bl, bh], 0), preferred_element_type=f32
    )


def dot_nt(ah, al, bh, bl):
    return lax.dot_general(
        jnp.concatenate([ah, ah, al], 1), jnp.concatenate([bh, bl, bh], 1), TRANS_B, preferred_element_type=f32
    )


def dot_tn(ah, al, bh, bl):
    return lax.dot_general(
        jnp.concatenate([ah, ah, al], 0), jnp.concatenate([bh, bl, bh], 0), TRANS_A, preferred_element_type=f32
    )


def spread(x):
    return jnp.broadcast_to(x, (8, NB))


def tree_sum(xs):
    while len(xs) > 1:
        xs = [xs[i] + xs[i + 1] if i + 1 < len(xs) else xs[i] for i in range(0, len(xs), 2)]
    return xs[0]


def factor_tile(t, rows, cols, lane, sub):
    scaled, ratio, inverses, pivots = [], {}, [], None
    for j in range(8):
        pivot = spread(cols[j][j : j + 1, :])
        inv = 1.0 / pivot
        inverses.append(inv)
        pivots = pivot if j == 0 else jnp.where(sub == j, pivot, pivots)
        below = jnp.where(sub > j, cols[j], 0.0)
        for k in range(j + 1, 8):
            entry = spread(cols[k][j : j + 1, :])
            cols[k] = cols[k] - (below * entry) * inv
            ratio[j, k] = entry * inv
        row = spread(rows[j : j + 1, :]) * inv
        row = jnp.where(lane == 8 * t + j, 1.0 + inv, row)
        scaled.append(row)
        if j < 7:
            rows = rows - below * row
    return rows, lax.rsqrt(pivots), scaled, ratio, inverses


def factor_block(tiles, store_u, store_l):
    tiles = list(tiles)
    n = len(tiles)
    lane = lax.broadcasted_iota(jnp.int32, (8, NB), 1)
    sub = lax.broadcasted_iota(jnp.int32, (8, NB), 0)
    cols = [spread(tiles[0][:, k : k + 1]) for k in range(8)]
    for t in range(n):
        last = t + 1 == n
        if not last:
            near = [spread(tiles[t + 1][:, 8 * t + k : 8 * t + k + 1]) for k in range(8)]
            ahead = [spread(tiles[t + 1][:, 8 * t + 8 + k : 8 * t + 9 + k]) for k in range(8)]
        far = {i: [spread(tiles[i][:, 8 * t + k : 8 * t + k + 1]) for k in range(8)] for i in range(t + 2, n)}
        rows, root, scaled, ratio, inverses = factor_tile(t, tiles[t], cols, lane, sub)
        if not last:
            for j in range(8):
                part = near[j] * inverses[j]
                for k in range(j + 1, 8):
                    near[k] = near[k] - near[j] * ratio[j, k]
                for k in range(8):
                    ahead[k] = ahead[k] - near[j] * spread(part[k : k + 1, :])
                tiles[t + 1] = tiles[t + 1] - near[j] * scaled[j]
            cols = ahead
        back = list(scaled)
        for j in range(6, -1, -1):
            for k in range(7, j, -1):
                back[j] = back[j] - ratio[j, k] * back[k]
        for i in range(t + 2, n):
            tiles[i] = tiles[i] - tree_sum([far[i][j] * back[j] for j in range(8)])
        final = rows * root
        diff = lane - sub - 8 * t
        store_u(t, jnp.where(diff >= 0, final, 0.0))
        store_l(t, jnp.where(diff < 0, final, jnp.where(diff == 0, root, 0.0)))


def half_norm_rows(x):
    xf = x.astype(f32)
    hi, lo = split(xf * xf)
    ones = jnp.ones((8, x.shape[1]), bf16)
    total = lax.dot_general(ones, hi, TRANS_B, preferred_element_type=f32)
    total = total + lax.dot_general(ones, lo, TRANS_B, preferred_element_type=f32)
    return 0.5 * total[0:1]


def half_norm_cols(x, width):
    xf = x.astype(f32)
    hi, lo = split(xf * xf)
    ones = jnp.ones((NB, x.shape[1]), bf16)
    total = lax.dot_general(hi, ones, TRANS_B, preferred_element_type=f32)
    total = 0.5 * (total + lax.dot_general(lo, ones, TRANS_B, preferred_element_type=f32))
    return jnp.concatenate([total] * (width // NB), 1)


def diagonal(n):
    return lax.broadcasted_iota(jnp.int32, (n, n), 0) == lax.broadcasted_iota(jnp.int32, (n, n), 1)


def place(x_ref, base, piece_at, piece, value):
    at = pl.multiple_of(base + piece_at * piece, piece)
    x_ref[pl.ds(at, piece), :] = value


def factor_panels(a_ref, uh_ref, ul_ref, inv_ref, count, width):
    def panel(p, carry):
        o = pl.multiple_of(p * NB, NB)
        d = a_ref[pl.ds(o, NB), pl.ds(o, NB)]

        def store_u(t, v):
            a_ref[pl.ds(pl.multiple_of(o + 8 * t, 8), 8), pl.ds(o, NB)] = v

        def store_l(t, v):
            inv_ref[p, 8 * t : 8 * t + 8, :] = v

        factor_block([d[8 * t : 8 * t + 8] for t in range(NB // 8)], store_u, store_l)
        hi, lo = split(a_ref[pl.ds(o, NB), pl.ds(o, NB)])
        uh_ref[pl.ds(o, NB), pl.ds(o, NB)] = hi
        ul_ref[pl.ds(o, NB), pl.ds(o, NB)] = lo
        for k in range(min(count, width // NB - 1)):

            @pl.when(p == k)
            def _():
                s = k * NB
                e = s + NB
                u = dot_nn(*split(inv_ref[k]), *split(a_ref[s:e, e:]))
                hi, lo = split(u)
                uh_ref[s:e, e:] = hi
                ul_ref[s:e, e:] = lo
                for i in range(k + 1, width // NB):
                    q = i * NB
                    w = q - e
                    a_ref[q : q + NB, q:] = a_ref[q : q + NB, q:] - dot_tn(
                        hi[:, w : w + NB], lo[:, w : w + NB], hi[:, w:], lo[:, w:]
                    )

        return carry

    lax.fori_loop(0, count, panel, 0)


def first_kernel(at_ref, amp_ref, mine_ref, other_ref, nz_ref, x_ref, uh_ref, ul_ref, inv_ref, rest_ref, a_ref):
    n = a_ref.shape[0]
    steps, panels, piece = mine_ref.shape[:3]
    block = n // panels
    me = at_ref[1]
    for m in range(steps):
        for s in range(panels):
            place(x_ref, s * block, me ^ (2 * m), piece, mine_ref[m, s])
            place(x_ref, s * block, me ^ (2 * m + 1), piece, other_ref[m, s])
    amp = amp_ref[0]
    sq_row = half_norm_rows(x_ref[...])
    halves = nz_ref[...].astype(f32)
    noise = halves[:, 0] + halves[:, 1] + halves[:, 2]
    for i in range(n // NB):
        o = i * NB
        xi = x_ref[o : o + NB, :]
        cross = lax.dot_general(xi, x_ref[o:, :], TRANS_B, preferred_element_type=f32)
        k = amp * jnp.exp(cross - half_norm_cols(xi, n - o) - sq_row[:, o:])
        a_ref[o : o + NB, o:] = k
        row = noise[o // block : o // block + 1, o % block : o % block + NB]
        a_ref[o : o + NB, o : o + NB] = k[:, :NB] + jnp.where(diagonal(NB), jnp.broadcast_to(row, (NB, NB)), 0.0)
    first = inv_ref.shape[0]
    factor_panels(a_ref, uh_ref, ul_ref, inv_ref, first, n)
    rest_ref[...] = a_ref[first * NB :, first * NB :]


def second_kernel(rest_ref, uh_ref, ul_ref, inv_ref, a_ref):
    a_ref[...] = rest_ref[...]
    factor_panels(a_ref, uh_ref, ul_ref, inv_ref, inv_ref.shape[0], a_ref.shape[1])


def store_block(out_ref, a, b, row, ncols, value):
    rows, block = value.shape
    per = block // NB
    for q in range(per):
        at = ((a * block + row) * ncols + b) * per + q
        out_ref[pl.ds(at, rows, stride=ncols * per), :] = value[:, q * NB : (q + 1) * NB]


def bulk_kernel(at_ref, amp_ref, *refs):
    (rows_ref, mine_ref, other_ref, x_ref, uh0_ref, ul0_ref, inv0_ref, uh1_ref, ul1_ref, inv1_ref, nz_ref) = refs[:11]
    out_ref, c_ref, ph_ref, pl_ref, wh_ref, wl_ref = refs[11:]
    n = x_ref.shape[0]
    split_at = uh0_ref.shape[0]
    steps, _, _, piece = mine_ref.shape[:4]
    nrows, block, _ = rows_ref.shape
    ncols = c_ref.shape[0] // block
    row_at, me, row_n, col_n = at_ref[0], at_ref[1], at_ref[2], at_ref[3]
    core = me & 1
    amp = amp_ref[0]
    for m in range(steps):
        for b in range(ncols):
            place(c_ref, b * block, me ^ (2 * m), piece, mine_ref[m, core, b])
            place(c_ref, b * block, me ^ (2 * m + 1), piece, other_ref[m, b])

    def upper(r0, r1, c0, c1):
        parts = []
        if r0 < split_at:
            r = min(r1, split_at)
            parts.append((uh0_ref[r0:r, c0:c1], ul0_ref[r0:r, c0:c1]))
        if r1 > split_at:
            r = max(r0, split_at)
            d = split_at
            parts.append((uh1_ref[r - d : r1 - d, c0 - d : c1 - d], ul1_ref[r - d : r1 - d, c0 - d : c1 - d]))
        return tuple(jnp.concatenate([p[h] for p in parts], 0) if len(parts) > 1 else parts[0][h] for h in (0, 1))

    def inverse(k):
        d = split_at // NB
        return inv0_ref[k] if k < d else inv1_ref[k - d]

    for q in range(n // WB):
        top, low = inverse(2 * q), inverse(2 * q + 1)
        s = q * WB
        corner = dot_tn(*upper(s, s + NB, s + NB, s + WB), *split(top))
        corner = -dot_nn(*split(low), *split(corner))
        zero = jnp.zeros((NB, NB), f32)
        full = jnp.concatenate([jnp.concatenate([top, zero], 1), jnp.concatenate([corner, low], 1)], 0)
        wh_ref[q], wl_ref[q] = split(full)
    lead_sq = half_norm_rows(x_ref[...])
    chunk = 256

    def solve(xb, o):
        sq = half_norm_cols(xb, WB)
        for q in range(n // WB):
            s = q * WB
            cross = lax.dot_general(xb, x_ref[s : s + WB, :], TRANS_B, preferred_element_type=f32)
            acc = amp * jnp.exp(cross - sq - lead_sq[:, s : s + WB])
            if q:
                acc = acc - dot_nn(
                    ph_ref[pl.ds(o, chunk), 0:s], pl_ref[pl.ds(o, chunk), 0:s], *upper(0, s, s, s + WB)
                )
            hi, lo = split(dot_nt(*split(acc), wh_ref[q], wl_ref[q]))
            ph_ref[pl.ds(o, chunk), s : s + WB] = hi
            pl_ref[pl.ds(o, chunk), s : s + WB] = lo

    parts = block // chunk

    def solve_rows(step, carry):
        a = step // parts

        @pl.when(a * row_n + row_at >= PANELS)
        def _():
            h = pl.multiple_of((step % parts) * chunk, chunk)
            solve(rows_ref[a, pl.ds(h, chunk), :], pl.multiple_of(step * chunk, chunk))

        return carry

    def solve_cols(step, carry):
        @pl.when((step // parts) * col_n + me >= PANELS)
        def _():
            h = pl.multiple_of(step * chunk, chunk)
            solve(c_ref[pl.ds(h, chunk), :], pl.multiple_of(nrows * block + step * chunk, chunk))

        return carry

    lax.fori_loop(0, nrows * parts, solve_rows, 0)
    lax.fori_loop(0, ncols * parts, solve_cols, 0)
    for b in range(ncols):
        j = b * col_n + me
        fo = (nrows + b) * block
        xc = c_ref[b * block : (b + 1) * block, :]
        col_sq = half_norm_rows(xc)
        for a in range(nrows):
            i = a * row_n + row_at

            @pl.when((i >= PANELS) & (j >= PANELS))
            def _():
                for h in range(0, block, chunk):
                    o = a * block + h
                    xr = rows_ref[a, h : h + chunk, :]
                    cross = lax.dot_general(xr, xc, TRANS_B, preferred_element_type=f32)
                    k = amp * jnp.exp(cross - half_norm_cols(xr, block) - col_sq)
                    row_id = lax.broadcasted_iota(jnp.int32, (chunk, block), 0) + h
                    col_id = lax.broadcasted_iota(jnp.int32, (chunk, block), 1)
                    on_diag = (row_id == col_id) & (i == j)
                    k = k + jnp.where(on_diag, jnp.broadcast_to(nz_ref[a : a + 1, :], (chunk, block)), 0.0)
                    k = k - dot_nt(
                        ph_ref[o : o + chunk, :],
                        pl_ref[o : o + chunk, :],
                        ph_ref[fo : fo + block, :],
                        pl_ref[fo : fo + block, :],
                    )
                    store_block(out_ref, a, b, h, ncols, k)

            for s in range(PANELS):
                w = s * block

                @pl.when((i >= PANELS) & (j == s))
                def _():
                    rows = slice(a * block, (a + 1) * block)
                    hi, lo = ph_ref[rows, w : w + block], pl_ref[rows, w : w + block]
                    store_block(out_ref, a, b, 0, ncols, hi.astype(f32) + lo.astype(f32))

                @pl.when((i == s) & (j > s))
                def _():
                    store_block(out_ref, a, b, 0, ncols, jnp.zeros((block, block), f32))

                for v in range(s + 1):

                    @pl.when((i == s) & (j == v))
                    def _():
                        hi, lo = upper(v * block, (v + 1) * block, w, w + block)
                        u = (hi.astype(f32) + lo.astype(f32)).T
                        if v == s:
                            row_id = lax.broadcasted_iota(jnp.int32, (block, block), 0)
                            col_id = lax.broadcasted_iota(jnp.int32, (block, block), 1)
                            u = jnp.where(row_id >= col_id, u, 0.0)
                        store_block(out_ref, a, b, 0, ncols, u)


SMEM = pl.BlockSpec(memory_space=pltpu.SMEM)
VMEM = pl.BlockSpec(memory_space=pltpu.VMEM)


def exchange(x, axis, k):
    return lax.ppermute(x, axis, [(i, i ^ k) for i in range(lax.axis_size(axis))])


def choose(index, options):
    out = options[0]
    for k in range(1, len(options)):
        out = jnp.where(index == k, options[k], out)
    return out


def split3(x):
    hi, rest = x.astype(bf16), x
    rest = x - lax.reduce_precision(x, 8, 7)
    mid = rest.astype(bf16)
    low = (rest - lax.reduce_precision(rest, 8, 7)).astype(bf16)
    return jnp.stack([hi, mid, low])


def local(features, amplitude, noise):
    row_n = lax.axis_size("row")
    col_n = lax.axis_size("col")
    row_at = lax.axis_index("row")
    col_at = lax.axis_index("col")
    nrows, _, piece, width = features.shape
    block = piece * col_n
    ncols = nrows * row_n // col_n
    n = PANELS * block
    mine = features.reshape(nrows, piece, width)
    noise_rows = noise.reshape(nrows, block)
    rows = lax.all_gather(mine, "col", axis=1, tiled=True)
    extra = split3(noise_rows[0]).reshape(-1, width)
    extra = jnp.pad(extra, ((0, -extra.shape[0] % 16), (0, 0)))
    parcel = jnp.concatenate([mine.reshape(-1, width), extra], 0)
    plane = [parcel] + [exchange(parcel, "row", k) for k in range(1, row_n)]
    lead = jnp.stack([choose(row_at ^ s, [p[:piece] for p in plane]) for s in range(PANELS)])
    lead_noise = jnp.stack([choose(row_at ^ s, [p[nrows * piece :] for p in plane]) for s in range(PANELS)])
    lead_noise = lead_noise[:, : 3 * block // width].reshape(PANELS, 3, block)
    near = jnp.stack([lead] + [exchange(lead, "col", k) for k in range(2, col_n, 2)])
    other = exchange(near, "col", 1)
    near, other, everything = lax.optimization_barrier((near, other, jnp.stack(plane)))

    def for_chip(to):
        out = []
        for core in range(2):
            for b in range(ncols):
                number = b * col_n + (to & ~1) + core
                out.append(
                    lax.dynamic_slice(
                        everything, (row_at ^ (number % row_n), (number // row_n) * piece, 0), (1, piece, width)
                    )
                )
        return jnp.concatenate(out, 0).reshape(2, ncols, piece, width)

    cols_near = [for_chip(col_at)] + [exchange(for_chip(col_at ^ k), "col", k) for k in range(2, col_n, 2)]
    at = jnp.stack([row_at, col_at, jnp.int32(row_n), jnp.int32(col_n)])
    first = n // NB // 2
    n1 = n - first * NB
    points, uh0, ul0, inv0, rest = pl.pallas_call(
        first_kernel,
        out_shape=[
            jax.ShapeDtypeStruct((n, width), bf16),
            jax.ShapeDtypeStruct((first * NB, n), bf16),
            jax.ShapeDtypeStruct((first * NB, n), bf16),
            jax.ShapeDtypeStruct((first, NB, NB), f32),
            jax.ShapeDtypeStruct((n1, n1), f32),
        ],
        in_specs=[SMEM, SMEM, VMEM, VMEM, VMEM],
        out_specs=[VMEM] * 5,
        scratch_shapes=[pltpu.VMEM((n, n), f32)],
        compiler_params=pltpu.CompilerParams(vmem_limit_bytes=20 << 20),
        cost_estimate=pl.CostEstimate(flops=20_000_000_000, bytes_accessed=8_000_000, transcendentals=0),
        name="first",
    )(at, amplitude, near, other, lead_noise)
    cols_near = jnp.stack(cols_near)
    cols_near, rest = lax.optimization_barrier((cols_near, rest))
    core = col_at & 1
    cols_other = exchange(lax.dynamic_index_in_dim(cols_near, 1 - core, 1, keepdims=False), "col", 1)
    uh1, ul1, inv1 = pl.pallas_call(
        second_kernel,
        out_shape=[
            jax.ShapeDtypeStruct((n1, n1), bf16),
            jax.ShapeDtypeStruct((n1, n1), bf16),
            jax.ShapeDtypeStruct((n1 // NB, NB, NB), f32),
        ],
        in_specs=[VMEM],
        out_specs=[VMEM] * 3,
        scratch_shapes=[pltpu.VMEM((n1, n1), f32)],
        compiler_params=pltpu.CompilerParams(vmem_limit_bytes=20 << 20),
        cost_estimate=pl.CostEstimate(flops=20_000_000_000, bytes_accessed=8_000_000, transcendentals=0),
        name="second",
    )(rest)
    out = pl.pallas_call(
        bulk_kernel,
        out_shape=jax.ShapeDtypeStruct((nrows * block * ncols * (block // NB), NB), f32),
        in_specs=[SMEM, SMEM] + [VMEM] * 11,
        out_specs=VMEM,
        scratch_shapes=[
            pltpu.VMEM((ncols * block, width), bf16),
            pltpu.VMEM(((nrows + ncols) * block, n), bf16),
            pltpu.VMEM(((nrows + ncols) * block, n), bf16),
            pltpu.VMEM((n // WB, WB, WB), bf16),
            pltpu.VMEM((n // WB, WB, WB), bf16),
        ],
        compiler_params=pltpu.CompilerParams(vmem_limit_bytes=36 << 20),
        cost_estimate=pl.CostEstimate(flops=12_000_000_000, bytes_accessed=8_000_000, transcendentals=0),
        name="bulk",
    )(at, amplitude, rows, cols_near, cols_other, points, uh0, ul0, inv0, uh1, ul1, inv1, noise_rows)
    return out.reshape(nrows, 1, block, ncols, 1, block)


def solution(mesh):
    return jax.shard_map(
        local,
        mesh=mesh,
        in_specs=(P(None, "row", "col", None), P(), P(None, "row", None)),
        out_specs=P(None, "row", None, None, "col", None),
        check_vma=False,
    )
```

time: 109 us -> 110 us (level); the launches traced: 109 us -> 108 us
  between operations: 0.87 us -> 14.6 us
  blocking collectives: 6.72 us -> 0 us
  starting transfers between devices: 19.5 us -> 15.8 us
  waiting for transfers between devices: 13.2 us -> 10.5 us
  local copies, waits for them, and re-layouts: 11.1 us -> 9.26 us
    all_gather x1 -> x0, blocking collectives: 6.72 us -> none  [local(): lead_noise = lax.all_gather(noise_rows[0], 'row')[:PANELS].reshape(1, n)]
    reshape x2 -> x0, local copies, waits for them, and re-layouts: 5.1 us -> none  [the longest x1 5.06 us: local(): return out.reshape(nrows, 1, block, ncols, 1, block)]
    ppermute x14 -> x11, starting transfers between devices: 19.5 us -> 15.8 us  [exchange(): lax.ppermute(x, axis, [(i, i ^ k) for i in range(lax.axis_size(axis))])]
    ppermute x14 -> x11, waiting for transfers between devices: 13.2 us -> 10.5 us  [exchange(): lax.ppermute(x, axis, [(i, i ^ k) for i in range(lax.axis_size(axis))])]
    unnamed x29 -> x19, local copies, waits for them, and re-layouts: 5.99 us -> 8.53 us
    pallas_call x1 -> x2, Pallas kernels: 29.1 us -> 29.7 us  [the longest x1 17.4 us: local(): pl.pallas_call(first_kernel, out_shape=[jax.ShapeDtypeStruct((n, width),...]
  transfers between devices with their start and end apart: 14 -> 12, of which waited for: 4 -> 4; matrix products, arithmetic and copies ran while one was open for 1% -> 1% of each run, Pallas kernels for 27% -> 27%
where the time goes in v2:
time: 110 us; the launch traced here: 108 us
  Pallas kernels  55.3 us (50%)
  starting transfers between devices  15.8 us (14%)
  between operations  14.6 us (13%)
  waiting for transfers between devices  10.5 us (10%)
  local copies, waits for them, and re-layouts  9.26 us (8%)
  other arithmetic  2.9 us (3%)
    pallas_call x1, Pallas kernels, local(): pl.pallas_call(bulk_kernel, out_shape=jax.ShapeDtypeStruct((nrows * block...  25.5 us
    pallas_call x1, Pallas kernels, local(): pl.pallas_call(first_kernel, out_shape=[jax.ShapeDtypeStruct((n, width),...  17.4 us
    ppermute x11, starting transfers between devices, exchange(): lax.ppermute(x, axis, [(i, i ^ k) for i in range(lax.axis_size(axis))])  15.8 us
    pallas_call x1, Pallas kernels, local(): pl.pallas_call(second_kernel, out_shape=[jax.ShapeDtypeStruct((n1, n1), b...  12.3 us
    ppermute x11, waiting for transfers between devices, exchange(): lax.ppermute(x, axis, [(i, i ^ k) for i in range(lax.axis_size(axis))])  10.5 us
    unnamed x19, local copies, waits for them, and re-layouts  8.53 us
  transfers between devices with their start and end apart: 12, of which 4 were waited for; matrix products, arithmetic and copies ran while one was open for 1% of the time, Pallas kernels for 27%

profile of v2, /device:TPU:31, one launch (start us, length us, event | category | flops | bytes accessed | tf_op | source)
XLA Modules:
  0.0 108.3 jit_solution(597238845796603000)
XLA Ops:
  6.5 0.0 all-gather.3.cloned.1.call-start
  6.5 0.7 bitcast_convert_fusion
  7.2 0.7 fusion.12
  7.9 0.9 fusion.14
  8.9 0.3 collective-permute-start.2
  9.2 0.2 collective-permute-start.1
  9.4 2.2 %collective-permute-start = (bf16[144,512]{1,0:T(8,128)(2,1)S(1)}, bf16[144,512]{1,0:T(8,128)(2,1)S(1)}, u32[]{:S(2)}, u32[]{:S(2)}) collective-permute-start(bf16[144,512]{1,0:T(8,128)(2,1)S(1)} %get-tuple-element.44), channel_id=1, source_target_pairs={{0,24},{8,16},{16,8},{24,0},{1,25},{9,17},{17,9},{25,1},{2,26},{10... | collective-permute-start | bytes 442376 | tf_op jit(solution)/shard_map/ppermute | solution.py:345
  11.6 2.1 %collective-permute-done.2 = bf16[144,512]{1,0:T(8,128)(2,1)S(1)} collective-permute-done((bf16[144,512]{1,0:T(8,128)(2,1)S(1)}, bf16[144,512]{1,0:T(8,128)(2,1)S(1)}, u32[]{:S(2)}, u32[]{:S(2)}) %collective-permute-start.2) | collective-permute-done | bytes 147488 | tf_op jit(solution)/shard_map/ppermute | solution.py:345
  13.6 0.0 collective-permute-done.1
  13.6 3.1 %collective-permute-done = bf16[144,512]{1,0:T(8,128)(2,1)S(1)} collective-permute-done((bf16[144,512]{1,0:T(8,128)(2,1)S(1)}, bf16[144,512]{1,0:T(8,128)(2,1)S(1)}, u32[]{:S(2)}, u32[]{:S(2)}) %collective-permute-start) | collective-permute-done | bytes 147488 | tf_op jit(solution)/shard_map/ppermute | solution.py:345
  16.7 0.9 fusion.2
  17.6 0.1 collective-permute-start.4
  17.8 0.2 collective-permute-start.3
  18.0 3.3 %collective-permute-start.5 = (bf16[2,64,512]{2,1,0:T(8,128)(2,1)S(1)}, bf16[2,64,512]{2,1,0:T(8,128)(2,1)S(1)}, u32[]{:S(2)}, u32[]{:S(2)}) collective-permute-start(bf16[2,64,512]{2,1,0:T(8,128)(2,1)S(1)} %get-tuple-element.46), channel_id=1, source_target_pairs={{0,6},{1,7},{2,4},{3,5},{4,2},{5,3},{6,0},{7,1},{8,14},{9,15},{10,... | collective-permute-start | bytes 393224 | tf_op jit(solution)/shard_map/ppermute | solution.py:345
  21.3 0.0 all-gather.3.cloned.1.call-update
  21.6 0.7 copy.11
  23.0 4.0 %collective-permute-done.4 = bf16[2,64,512]{2,1,0:T(8,128)(2,1)S(1)} collective-permute-done((bf16[2,64,512]{2,1,0:T(8,128)(2,1)S(1)}, bf16[2,64,512]{2,1,0:T(8,128)(2,1)S(1)}, u32[]{:S(2)}, u32[]{:S(2)}) %collective-permute-start.4) | collective-permute-done | bytes 131104 | tf_op jit(solution)/shard_map/ppermute | solution.py:345
  27.0 0.0 collective-permute-done.3
  27.0 0.0 collective-permute-done.5
  27.0 0.1 pad_maximum_fusion.1.mine_ref
  27.1 4.1 %collective-permute-start.6 = (bf16[4,2,64,512]{3,2,1,0:T(8,128)(2,1)S(1)}, bf16[4,2,64,512]{3,2,1,0:T(8,128)(2,1)S(1)}, u32[]{:S(2)}, u32[]{:S(2)}) collective-permute-start(bf16[4,2,64,512]{3,2,1,0:T(8,128)(2,1)S(1)} %pad_maximum_fusion.1.mine_ref), channel_id=1, source_target_pairs={{0,1},{1,0},{2,3},{3,2},{4,5},{5,4},{6,7},{7,6},{8,9},{9,8},{10,11... | collective-permute-start | bytes 1572872 | tf_op jit(solution)/shard_map/ppermute | solution.py:345
  31.2 0.1 pad_add_fusion.at_ref
  31.4 0.1 pad_maximum_fusion
  31.4 1.3 %collective-permute-done.6.other_ref = bf16[4,2,64,512]{3,2,1,0:T(8,128)(2,1)S(1)} collective-permute-done((bf16[4,2,64,512]{3,2,1,0:T(8,128)(2,1)S(1)}, bf16[4,2,64,512]{3,2,1,0:T(8,128)(2,1)S(1)}, u32[]{:S(2)}, u32[]{:S(2)}) %collective-permute-start.6) | collective-permute-done | bytes 524320 | tf_op jit(solution)/shard_map/ppermute | solution.py:345
  32.8 2.1 %collective-permute-start.7 = (bf16[2,1,64,512]{3,2,0,1:T(8,128)(2,1)S(1)}, bf16[2,1,64,512]{3,2,0,1:T(8,128)(2,1)S(1)}, u32[]{:S(2)}, u32[]{:S(2)}) collective-permute-start(bf16[2,1,64,512]{3,2,0,1:T(8,128)(2,1)S(1)} %maximum_bitcast_fusion.1), channel_id=1, source_target_pairs={{0,2},{1,3},{2,0},{3,1},{4,6},{5,7},{6,4},{7,5},{8,10},{9,11},{10,... | collective-permute-start | bytes 393224 | tf_op jit(solution)/shard_map/ppermute | solution.py:345
  34.9 0.1 collective-permute-start.8
  35.0 2.1 %collective-permute-start.9 = (bf16[2,1,64,512]{3,2,0,1:T(8,128)(2,1)S(1)}, bf16[2,1,64,512]{3,2,0,1:T(8,128)(2,1)S(1)}, u32[]{:S(2)}, u32[]{:S(2)}) collective-permute-start(bf16[2,1,64,512]{3,2,0,1:T(8,128)(2,1)S(1)} %maximum_bitcast_fusion.3), channel_id=1, source_target_pairs={{0,6},{1,7},{2,4},{3,5},{4,2},{5,3},{6,0},{7,1},{8,14},{9,15},{10,... | collective-permute-start | bytes 393224 | tf_op jit(solution)/shard_map/ppermute | solution.py:345
  37.2 17.4 %first.1 = (bf16[1024,512]{1,0:T(8,128)(2,1)S(1)}, bf16[512,1024]{1,0:T(8,128)(2,1)S(1)}, bf16[512,1024]{1,0:T(8,128)(2,1)S(1)}, f32[4,128,128]{2,1,0:T(8,128)S(1)}, f32[512,512]{1,0:T(8,128)S(1)}) custom-call(s32[4]{0:T(128)S(1)} %pad_add_fusion.at_ref, f32[1]{0:T(128)S(6)} %copy.12.amp_ref, bf16[4,2,64,512]{3,2,1,0:T(8,128)(2,1)S(1)} %pad_maximum_fusion.1.mine_ref, ...), custom_call_target="tpu_custom_call" | custom-call | flops 20000000000 | bytes 8000000 | tf_op jit(solution)/shard_map/first/pallas_call | solution.py:402
  54.6 0.0 copy-start.1
  54.6 0.0 copy-start.5
  54.7 0.0 collective-permute-done.7
  54.7 0.0 collective-permute-done.8
  54.7 0.0 collective-permute-done.9
  54.7 0.1 pad_maximum_fusion.2.refs_1_
  54.8 0.8 copy-done.1
  55.6 0.1 copy-done.5
  55.7 1.0 collective-permute-start.10
  56.7 12.3 %second.1 = (bf16[512,512]{1,0:T(8,128)(2,1)S(1)}, bf16[512,512]{1,0:T(8,128)(2,1)S(1)}, f32[4,128,128]{2,1,0:T(8,128)S(1)}) custom-call(f32[512,512]{1,0:T(8,128)S(1)} %get-tuple-element.27.rest_ref), custom_call_target="tpu_custom_call" | custom-call | flops 20000000000 | bytes 8000000 | tf_op jit(solution)/shard_map/second/pallas_call | solution.py:422
  69.0 0.0 copy-start.3
  69.0 0.8 copy-done.3
  69.8 0.7 copy-done.7
  70.5 0.0 collective-permute-done.10.refs_2_
  70.5 1.2 %copy-done = bf16[2,1,512,512]{3,2,0,1:T(8,128)(2,1)S(1)} copy-done((bf16[2,1,512,512]{3,2,0,1:T(8,128)(2,1)S(1)}, bf16[2,1,512,512]{3,2,0,1:T(8,128)(2,1)}, u32[]{:S(2)}) %copy-start) | copy-done | bytes 1048600
  71.8 1.2 %copy-done.2 = bf16[512,1024]{1,0:T(8,128)(2,1)S(1)} copy-done((bf16[512,1024]{1,0:T(8,128)(2,1)S(1)}, bf16[512,1024]{1,0:T(8,128)(2,1)}, u32[]{:S(2)}) %copy-start.2) | copy-done | bytes 1048600
  73.0 1.0 copy-done.4
  74.0 0.9 copy-done.6
  75.0 0.9 copy-done.8
  75.9 25.5 %bulk.1 = f32[4096,128]{1,0:T(8,128)} custom-call(s32[4]{0:T(128)S(1)} %pad_add_fusion.at_ref, f32[1]{0:T(128)S(6)} %copy.12.amp_ref, bf16[2,512,512]{2,1,0:T(8,128)(2,1)S(1)} %bitcast.69, bf16[4,2,1,64,512]{4,3,2,1,0:T(8,128)(2,1)S(1)} %pad_maximum_fusion.2.refs_1_, bf16[4,1,64,512]{3,2,1,0:T(8,128)(2,1)S(1)} %collective-permute-done.10.refs_2_, ...), custom_call_target="tpu_custom_call" | custom-call | flops 12000000000 | bytes 8000000 | tf_op jit(solution)/shard_map/bulk/pallas_call | solution.py:436
  (17 shorter events, 0.2 us)
Async XLA Ops:
  6.5 64.0 %all-gather.3.cloned.1.call-start = ((), (), s32[]{:S(2)}) async-start(), calls=%async_computation | async-start | bytes 1179648 | tf_op jit(solution)/shard_map/all_gather | solution.py:374
  8.9 4.8 %collective-permute-start.2 = (bf16[144,512]{1,0:T(8,128)(2,1)S(1)}, bf16[144,512]{1,0:T(8,128)(2,1)S(1)}, u32[]{:S(2)}, u32[]{:S(2)}) collective-permute-start(bf16[144,512]{1,0:T(8,128)(2,1)S(1)} %get-tuple-element.44), channel_id=1, source_target_pairs={{0,8},{8,0},{16,24},{24,16},{1,9},{9,1},{17,25},{25,17},{2,10},{10... | collective-permute-start | bytes 442376 | tf_op jit(solution)/shard_map/ppermute | solution.py:345
  9.2 4.5 %collective-permute-start.1 = (bf16[144,512]{1,0:T(8,128)(2,1)S(1)}, bf16[144,512]{1,0:T(8,128)(2,1)S(1)}, u32[]{:S(2)}, u32[]{:S(2)}) collective-permute-start(bf16[144,512]{1,0:T(8,128)(2,1)S(1)} %get-tuple-element.44), channel_id=1, source_target_pairs={{0,16},{8,24},{16,0},{24,8},{1,17},{9,25},{17,1},{25,9},{2,18},{10... | collective-permute-start | bytes 442376 | tf_op jit(solution)/shard_map/ppermute | solution.py:345
  9.4 7.3 %collective-permute-start = (bf16[144,512]{1,0:T(8,128)(2,1)S(1)}, bf16[144,512]{1,0:T(8,128)(2,1)S(1)}, u32[]{:S(2)}, u32[]{:S(2)}) collective-permute-start(bf16[144,512]{1,0:T(8,128)(2,1)S(1)} %get-tuple-element.44), channel_id=1, source_target_pairs={{0,24},{8,16},{16,8},{24,0},{1,25},{9,17},{17,9},{25,1},{2,26},{10... | collective-permute-start | bytes 442376 | tf_op jit(solution)/shard_map/ppermute | solution.py:345
  17.6 9.4 %collective-permute-start.4 = (bf16[2,64,512]{2,1,0:T(8,128)(2,1)S(1)}, bf16[2,64,512]{2,1,0:T(8,128)(2,1)S(1)}, u32[]{:S(2)}, u32[]{:S(2)}) collective-permute-start(bf16[2,64,512]{2,1,0:T(8,128)(2,1)S(1)} %get-tuple-element.46), channel_id=1, source_target_pairs={{0,4},{1,5},{2,6},{3,7},{4,0},{5,1},{6,2},{7,3},{8,12},{9,13},{10,... | collective-permute-start | bytes 393224 | tf_op jit(solution)/shard_map/ppermute | solution.py:345
  17.8 9.3 %collective-permute-start.3 = (bf16[2,64,512]{2,1,0:T(8,128)(2,1)S(1)}, bf16[2,64,512]{2,1,0:T(8,128)(2,1)S(1)}, u32[]{:S(2)}, u32[]{:S(2)}) collective-permute-start(bf16[2,64,512]{2,1,0:T(8,128)(2,1)S(1)} %get-tuple-element.46), channel_id=1, source_target_pairs={{0,2},{1,3},{2,0},{3,1},{4,6},{5,7},{6,4},{7,5},{8,10},{9,11},{10,... | collective-permute-start | bytes 393224 | tf_op jit(solution)/shard_map/ppermute | solution.py:345
  18.0 9.1 %collective-permute-start.5 = (bf16[2,64,512]{2,1,0:T(8,128)(2,1)S(1)}, bf16[2,64,512]{2,1,0:T(8,128)(2,1)S(1)}, u32[]{:S(2)}, u32[]{:S(2)}) collective-permute-start(bf16[2,64,512]{2,1,0:T(8,128)(2,1)S(1)} %get-tuple-element.46), channel_id=1, source_target_pairs={{0,6},{1,7},{2,4},{3,5},{4,2},{5,3},{6,0},{7,1},{8,14},{9,15},{10,... | collective-permute-start | bytes 393224 | tf_op jit(solution)/shard_map/ppermute | solution.py:345
  27.1 5.7 %collective-permute-start.6 = (bf16[4,2,64,512]{3,2,1,0:T(8,128)(2,1)S(1)}, bf16[4,2,64,512]{3,2,1,0:T(8,128)(2,1)S(1)}, u32[]{:S(2)}, u32[]{:S(2)}) collective-permute-start(bf16[4,2,64,512]{3,2,1,0:T(8,128)(2,1)S(1)} %pad_maximum_fusion.1.mine_ref), channel_id=1, source_target_pairs={{0,1},{1,0},{2,3},{3,2},{4,5},{5,4},{6,7},{7,6},{8,9},{9,8},{10,11... | collective-permute-start | bytes 1572872 | tf_op jit(solution)/shard_map/ppermute | solution.py:345
  32.8 21.9 %collective-permute-start.7 = (bf16[2,1,64,512]{3,2,0,1:T(8,128)(2,1)S(1)}, bf16[2,1,64,512]{3,2,0,1:T(8,128)(2,1)S(1)}, u32[]{:S(2)}, u32[]{:S(2)}) collective-permute-start(bf16[2,1,64,512]{3,2,0,1:T(8,128)(2,1)S(1)} %maximum_bitcast_fusion.1), channel_id=1, source_target_pairs={{0,2},{1,3},{2,0},{3,1},{4,6},{5,7},{6,4},{7,5},{8,10},{9,11},{10,... | collective-permute-start | bytes 393224 | tf_op jit(solution)/shard_map/ppermute | solution.py:345
  34.9 19.8 %collective-permute-start.8 = (bf16[2,1,64,512]{3,2,0,1:T(8,128)(2,1)S(1)}, bf16[2,1,64,512]{3,2,0,1:T(8,128)(2,1)S(1)}, u32[]{:S(2)}, u32[]{:S(2)}) collective-permute-start(bf16[2,1,64,512]{3,2,0,1:T(8,128)(2,1)S(1)} %maximum_bitcast_fusion.2), channel_id=1, source_target_pairs={{0,4},{1,5},{2,6},{3,7},{4,0},{5,1},{6,2},{7,3},{8,12},{9,13},{10,... | collective-permute-start | bytes 393224 | tf_op jit(solution)/shard_map/ppermute | solution.py:345
  35.0 19.7 %collective-permute-start.9 = (bf16[2,1,64,512]{3,2,0,1:T(8,128)(2,1)S(1)}, bf16[2,1,64,512]{3,2,0,1:T(8,128)(2,1)S(1)}, u32[]{:S(2)}, u32[]{:S(2)}) collective-permute-start(bf16[2,1,64,512]{3,2,0,1:T(8,128)(2,1)S(1)} %maximum_bitcast_fusion.3), channel_id=1, source_target_pairs={{0,6},{1,7},{2,4},{3,5},{4,2},{5,3},{6,0},{7,1},{8,14},{9,15},{10,... | collective-permute-start | bytes 393224 | tf_op jit(solution)/shard_map/ppermute | solution.py:345
  54.6 1.0 copy-start.1
  54.6 1.1 copy-start.5
  55.7 14.8 %collective-permute-start.10 = (bf16[4,1,64,512]{3,2,1,0:T(8,128)(2,1)S(1)}, bf16[4,1,64,512]{3,2,1,0:T(8,128)(2,1)S(1)}, u32[]{:S(2)}, u32[]{:S(2)}) collective-permute-start(bf16[4,1,64,512]{3,2,1,0:T(8,128)(2,1)S(1)} %dynamic-slice_bitcast_fusion), channel_id=1, source_target_pairs={{0,1},{1,0},{2,3},{3,2},{4,5},{5,4},{6,7},{7,6},{8,9},{9,8},{10,11... | collective-permute-start | bytes 786440 | tf_op jit(solution)/shard_map/ppermute | solution.py:345
  69.0 0.8 copy-start.3
  69.8 0.7 copy-start.7
  70.5 1.2 %copy-start = (bf16[2,1,512,512]{3,2,0,1:T(8,128)(2,1)S(1)}, bf16[2,1,512,512]{3,2,0,1:T(8,128)(2,1)}, u32[]{:S(2)}) copy-start(bf16[2,1,512,512]{3,2,0,1:T(8,128)(2,1)} %all-gather.3.cloned.1.call-done) | copy-start | bytes 3145732
  71.8 1.2 %copy-start.2 = (bf16[512,1024]{1,0:T(8,128)(2,1)S(1)}, bf16[512,1024]{1,0:T(8,128)(2,1)}, u32[]{:S(2)}) copy-start(bf16[512,1024]{1,0:T(8,128)(2,1)} %copy-done.1) | copy-start | bytes 3145732
  73.0 1.0 copy-start.4
  74.0 0.9 copy-start.6
  75.0 0.9 copy-start.8
Sparse Core Ops, SparseCore 0:
  21.4 31.9 all-gather.2

commit v3 on v2

--- a/solution.py
+++ b/solution.py
@@ -10,6 +10,7 @@
 PANELS = 2
 NB = 128
 WB = 256
+GRANT = 32 << 20
 f32 = jnp.float32
 bf16 = jnp.bfloat16
 TRANS_B = (((1,), (1,)), ((), ()))
@@ -178,8 +179,7 @@
             place(x_ref, s * block, me ^ (2 * m + 1), piece, other_ref[m, s])
     amp = amp_ref[0]
     sq_row = half_norm_rows(x_ref[...])
-    halves = nz_ref[...].astype(f32)
-    noise = halves[:, 0] + halves[:, 1] + halves[:, 2]
+    noise = nz_ref[...]
     for i in range(n // NB):
         o = i * NB
         xi = x_ref[o : o + NB, :]
@@ -207,20 +207,25 @@
 
 
 def bulk_kernel(at_ref, amp_ref, *refs):
-    (rows_ref, mine_ref, other_ref, x_ref, uh0_ref, ul0_ref, inv0_ref, uh1_ref, ul1_ref, inv1_ref, nz_ref) = refs[:11]
-    out_ref, c_ref, ph_ref, pl_ref, wh_ref, wl_ref = refs[11:]
+    lead_refs, refs = refs[:8], refs[8:]
+    x_ref, uh0_ref, ul0_ref, inv0_ref, uh1_ref, ul1_ref, inv1_ref, nz_ref = lead_refs
+    count = len(refs) - 10
+    near_refs, other_ref, out_ref = refs[:count], refs[count], refs[count + 1]
+    r_ref, c_ref, ph_ref, pl_ref, zh_ref, zl_ref, wh_ref, wl_ref = refs[count + 2 :]
     n = x_ref.shape[0]
     split_at = uh0_ref.shape[0]
-    steps, _, _, piece = mine_ref.shape[:4]
-    nrows, block, _ = rows_ref.shape
+    nrows, block = nz_ref.shape
+    piece = other_ref.shape[2]
     ncols = c_ref.shape[0] // block
     row_at, me, row_n, col_n = at_ref[0], at_ref[1], at_ref[2], at_ref[3]
-    core = me & 1
     amp = amp_ref[0]
-    for m in range(steps):
+    for m in range(count):
+        for a in range(nrows):
+            place(r_ref, a * block, me ^ (2 * m), piece, near_refs[m][a])
+            place(r_ref, a * block, me ^ (2 * m + 1), piece, other_ref[m, a])
         for b in range(ncols):
-            place(c_ref, b * block, me ^ (2 * m), piece, mine_ref[m, core, b])
-            place(c_ref, b * block, me ^ (2 * m + 1), piece, other_ref[m, b])
+            place(c_ref, b * block, me ^ (2 * m), piece, near_refs[m][nrows + ncols + b])
+            place(c_ref, b * block, me ^ (2 * m + 1), piece, other_ref[m, nrows + b])
 
     def upper(r0, r1, c0, c1):
         parts = []
@@ -237,7 +242,8 @@
         d = split_at // NB
         return inv0_ref[k] if k < d else inv1_ref[k - d]
 
-    for q in range(n // WB):
+    steps = n // WB
+    for q in range(steps):
         top, low = inverse(2 * q), inverse(2 * q + 1)
         s = q * WB
         corner = dot_tn(*upper(s, s + NB, s + NB, s + WB), *split(top))
@@ -246,90 +252,97 @@
         full = jnp.concatenate([jnp.concatenate([top, zero], 1), jnp.concatenate([corner, low], 1)], 0)
         wh_ref[q], wl_ref[q] = split(full)
     lead_sq = half_norm_rows(x_ref[...])
+
+    def kernel_entries(x, sq, q):
+        s = q * WB
+        cross = lax.dot_general(x, x_ref[s : s + WB, :], TRANS_B, preferred_element_type=f32)
+        return amp * jnp.exp(cross - sq - lead_sq[:, s : s + WB])
+
+    def forward(x, hi_ref, lo_ref, rows, last):
+        sq = half_norm_cols(x, WB)
+        for q in range(last):
+            s = q * WB
+            acc = kernel_entries(x, sq, q)
+            if q:
+                acc = acc - dot_nn(hi_ref[rows, 0:s], lo_ref[rows, 0:s], *upper(0, s, s, s + WB))
+            hi_ref[rows, s : s + WB], lo_ref[rows, s : s + WB] = split(dot_nt(*split(acc), wh_ref[q], wl_ref[q]))
+
     chunk = 256
-
-    def solve(xb, o):
-        sq = half_norm_cols(xb, WB)
-        for q in range(n // WB):
-            s = q * WB
-            cross = lax.dot_general(xb, x_ref[s : s + WB, :], TRANS_B, preferred_element_type=f32)
-            acc = amp * jnp.exp(cross - sq - lead_sq[:, s : s + WB])
-            if q:
-                acc = acc - dot_nn(
-                    ph_ref[pl.ds(o, chunk), 0:s], pl_ref[pl.ds(o, chunk), 0:s], *upper(0, s, s, s + WB)
-                )
-            hi, lo = split(dot_nt(*split(acc), wh_ref[q], wl_ref[q]))
-            ph_ref[pl.ds(o, chunk), s : s + WB] = hi
-            pl_ref[pl.ds(o, chunk), s : s + WB] = lo
-
-    parts = block // chunk
-
-    def solve_rows(step, carry):
-        a = step // parts
-
-        @pl.when(a * row_n + row_at >= PANELS)
-        def _():
-            h = pl.multiple_of((step % parts) * chunk, chunk)
-            solve(rows_ref[a, pl.ds(h, chunk), :], pl.multiple_of(step * chunk, chunk))
-
-        return carry
-
-    def solve_cols(step, carry):
-        @pl.when((step // parts) * col_n + me >= PANELS)
-        def _():
-            h = pl.multiple_of(step * chunk, chunk)
-            solve(c_ref[pl.ds(h, chunk), :], pl.multiple_of(nrows * block + step * chunk, chunk))
-
-        return carry
-
-    lax.fori_loop(0, nrows * parts, solve_rows, 0)
-    lax.fori_loop(0, ncols * parts, solve_cols, 0)
     for b in range(ncols):
         j = b * col_n + me
-        fo = (nrows + b) * block
-        xc = c_ref[b * block : (b + 1) * block, :]
-        col_sq = half_norm_rows(xc)
-        for a in range(nrows):
-            i = a * row_n + row_at
-
-            @pl.when((i >= PANELS) & (j >= PANELS))
-            def _():
-                for h in range(0, block, chunk):
-                    o = a * block + h
-                    xr = rows_ref[a, h : h + chunk, :]
-                    cross = lax.dot_general(xr, xc, TRANS_B, preferred_element_type=f32)
-                    k = amp * jnp.exp(cross - half_norm_cols(xr, block) - col_sq)
-                    row_id = lax.broadcasted_iota(jnp.int32, (chunk, block), 0) + h
-                    col_id = lax.broadcasted_iota(jnp.int32, (chunk, block), 1)
-                    on_diag = (row_id == col_id) & (i == j)
-                    k = k + jnp.where(on_diag, jnp.broadcast_to(nz_ref[a : a + 1, :], (chunk, block)), 0.0)
-                    k = k - dot_nt(
-                        ph_ref[o : o + chunk, :],
-                        pl_ref[o : o + chunk, :],
-                        ph_ref[fo : fo + block, :],
-                        pl_ref[fo : fo + block, :],
+        cols = slice(b * block, (b + 1) * block)
+
+        @pl.when(j >= PANELS)
+        def _():
+            xc = c_ref[cols, :]
+            everyone = slice(0, block)
+            for h in range(0, nrows * block, chunk):
+                xr = r_ref[h : h + chunk, :]
+                sq = half_norm_cols(xr, WB)
+                for q in range(steps):
+                    s = q * WB
+                    ph_ref[h : h + chunk, s : s + WB], pl_ref[h : h + chunk, s : s + WB] = split(
+                        kernel_entries(xr, sq, q)
                     )
-                    store_block(out_ref, a, b, h, ncols, k)
-
-            for s in range(PANELS):
-                w = s * block
-
-                @pl.when((i >= PANELS) & (j == s))
+            forward(xc, zh_ref, zl_ref, everyone, steps)
+            for q in range(steps - 1, -1, -1):
+                s = q * WB
+                e = s + WB
+                hi, lo = zh_ref[:, s:e], zl_ref[:, s:e]
+                if q < steps - 1:
+                    acc = hi.astype(f32) + lo.astype(f32)
+                    acc = acc - dot_nt(zh_ref[:, e:], zl_ref[:, e:], *upper(s, e, e, n))
+                    hi, lo = split(acc)
+                zh_ref[:, s:e], zl_ref[:, s:e] = split(dot_nn(hi, lo, wh_ref[q], wl_ref[q]))
+            col_sq = half_norm_rows(xc)
+            for a in range(nrows):
+                i = a * row_n + row_at
+
+                @pl.when(i >= PANELS)
                 def _():
-                    rows = slice(a * block, (a + 1) * block)
+                    for h in range(0, block, chunk):
+                        o = a * block + h
+                        xr = r_ref[o : o + chunk, :]
+                        cross = lax.dot_general(xr, xc, TRANS_B, preferred_element_type=f32)
+                        k = amp * jnp.exp(cross - half_norm_cols(xr, block) - col_sq)
+                        row_id = lax.broadcasted_iota(jnp.int32, (chunk, block), 0) + h
+                        col_id = lax.broadcasted_iota(jnp.int32, (chunk, block), 1)
+                        on_diag = (row_id == col_id) & (i == j)
+                        k = k + jnp.where(on_diag, jnp.broadcast_to(nz_ref[a : a + 1, :], (chunk, block)), 0.0)
+                        k = k - dot_nt(
+                            ph_ref[o : o + chunk, :], pl_ref[o : o + chunk, :], zh_ref[...], zl_ref[...]
+                        )
+                        store_block(out_ref, a, b, h, ncols, k)
+
+                @pl.when(i < PANELS)
+                def _():
+                    store_block(out_ref, a, b, 0, ncols, jnp.zeros((block, block), f32))
+
+        if b:
+            continue
+        for s in range(PANELS):
+            w = s * block
+            for a in range(nrows):
+                i = a * row_n + row_at
+                rows = slice(a * block, (a + 1) * block)
+
+                @pl.when((j == s) & (i >= PANELS))
+                def _():
+                    forward(r_ref[rows, :], ph_ref, pl_ref, rows, (w + block) // WB)
                     hi, lo = ph_ref[rows, w : w + block], pl_ref[rows, w : w + block]
                     store_block(out_ref, a, b, 0, ncols, hi.astype(f32) + lo.astype(f32))
 
-                @pl.when((i == s) & (j > s))
-                def _():
-                    store_block(out_ref, a, b, 0, ncols, jnp.zeros((block, block), f32))
-
-                for v in range(s + 1):
-
-                    @pl.when((i == s) & (j == v))
+                if a:
+                    continue
+                for v in range(PANELS):
+
+                    @pl.when((j == s) & (i == v))
                     def _():
-                        hi, lo = upper(v * block, (v + 1) * block, w, w + block)
-                        u = (hi.astype(f32) + lo.astype(f32)).T
+                        if v < s:
+                            u = jnp.zeros((block, block), f32)
+                        else:
+                            hi, lo = upper(w, w + block, v * block, (v + 1) * block)
+                            u = (hi.astype(f32) + lo.astype(f32)).T
                         if v == s:
                             row_id = lax.broadcasted_iota(jnp.int32, (block, block), 0)
                             col_id = lax.broadcasted_iota(jnp.int32, (block, block), 1)
@@ -350,14 +363,6 @@
     for k in range(1, len(options)):
         out = jnp.where(index == k, options[k], out)
     return out
-
-
-def split3(x):
-    hi, rest = x.astype(bf16), x
-    rest = x - lax.reduce_precision(x, 8, 7)
-    mid = rest.astype(bf16)
-    low = (rest - lax.reduce_precision(rest, 8, 7)).astype(bf16)
-    return jnp.stack([hi, mid, low])
 
 
 def local(features, amplitude, noise):
@@ -371,31 +376,27 @@
     n = PANELS * block
     mine = features.reshape(nrows, piece, width)
     noise_rows = noise.reshape(nrows, block)
-    rows = lax.all_gather(mine, "col", axis=1, tiled=True)
-    extra = split3(noise_rows[0]).reshape(-1, width)
-    extra = jnp.pad(extra, ((0, -extra.shape[0] % 16), (0, 0)))
-    parcel = jnp.concatenate([mine.reshape(-1, width), extra], 0)
-    plane = [parcel] + [exchange(parcel, "row", k) for k in range(1, row_n)]
-    lead = jnp.stack([choose(row_at ^ s, [p[:piece] for p in plane]) for s in range(PANELS)])
-    lead_noise = jnp.stack([choose(row_at ^ s, [p[nrows * piece :] for p in plane]) for s in range(PANELS)])
-    lead_noise = lead_noise[:, : 3 * block // width].reshape(PANELS, 3, block)
-    near = jnp.stack([lead] + [exchange(lead, "col", k) for k in range(2, col_n, 2)])
+    plane = [mine] + [exchange(mine, "row", k) for k in range(1, row_n)]
+    lead = jnp.stack([choose(row_at ^ s, [p[0] for p in plane]) for s in range(PANELS)])
+    noise_rows, lead = lax.optimization_barrier((noise_rows, lead))
+    near = [lead] + [exchange(lead, "col", k) for k in range(2, col_n, 2)]
+    noises = [noise_rows] + [exchange(noise_rows, "row", k) for k in range(1, row_n)]
+    lead_noise = jnp.stack([choose(row_at ^ s, [p[0] for p in noises]) for s in range(PANELS)])
+    near = jnp.stack(near)
     other = exchange(near, "col", 1)
-    near, other, everything = lax.optimization_barrier((near, other, jnp.stack(plane)))
-
-    def for_chip(to):
-        out = []
-        for core in range(2):
+    everything, near = lax.optimization_barrier((jnp.stack(plane), near))
+    core = col_at & 1
+
+    def parcel(to):
+        out = [mine]
+        for to_core in (1 - core, core):
             for b in range(ncols):
-                number = b * col_n + (to & ~1) + core
-                out.append(
-                    lax.dynamic_slice(
-                        everything, (row_at ^ (number % row_n), (number // row_n) * piece, 0), (1, piece, width)
-                    )
-                )
-        return jnp.concatenate(out, 0).reshape(2, ncols, piece, width)
-
-    cols_near = [for_chip(col_at)] + [exchange(for_chip(col_at ^ k), "col", k) for k in range(2, col_n, 2)]
+                number = b * col_n + (to & ~1) + to_core
+                at = (row_at ^ (number & (row_n - 1)), number // row_n, 0, 0)
+                out.append(lax.dynamic_slice(everything, at, (1, 1, piece, width)).reshape(1, piece, width))
+        return jnp.concatenate(out, 0)
+
+    parcels = [parcel(col_at)] + [exchange(parcel(col_at ^ k), "col", k) for k in range(2, col_n, 2)]
     at = jnp.stack([row_at, col_at, jnp.int32(row_n), jnp.int32(col_n)])
     first = n // NB // 2
     n1 = n - first * NB
@@ -411,14 +412,12 @@
         in_specs=[SMEM, SMEM, VMEM, VMEM, VMEM],
         out_specs=[VMEM] * 5,
         scratch_shapes=[pltpu.VMEM((n, n), f32)],
-        compiler_params=pltpu.CompilerParams(vmem_limit_bytes=20 << 20),
+        compiler_params=pltpu.CompilerParams(vmem_limit_bytes=GRANT),
         cost_estimate=pl.CostEstimate(flops=20_000_000_000, bytes_accessed=8_000_000, transcendentals=0),
         name="first",
     )(at, amplitude, near, other, lead_noise)
-    cols_near = jnp.stack(cols_near)
-    cols_near, rest = lax.optimization_barrier((cols_near, rest))
-    core = col_at & 1
-    cols_other = exchange(lax.dynamic_index_in_dim(cols_near, 1 - core, 1, keepdims=False), "col", 1)
+    parcels, rest = lax.optimization_barrier((parcels, rest))
+    passed = exchange(jnp.stack([p[: nrows + ncols] for p in parcels]), "col", 1)
     uh1, ul1, inv1 = pl.pallas_call(
         second_kernel,
         out_shape=[
@@ -429,26 +428,30 @@
         in_specs=[VMEM],
         out_specs=[VMEM] * 3,
         scratch_shapes=[pltpu.VMEM((n1, n1), f32)],
-        compiler_params=pltpu.CompilerParams(vmem_limit_bytes=20 << 20),
+        compiler_params=pltpu.CompilerParams(vmem_limit_bytes=GRANT),
         cost_estimate=pl.CostEstimate(flops=20_000_000_000, bytes_accessed=8_000_000, transcendentals=0),
         name="second",
     )(rest)
+    half = pltpu.VMEM((block, n), bf16)
     out = pl.pallas_call(
         bulk_kernel,
         out_shape=jax.ShapeDtypeStruct((nrows * block * ncols * (block // NB), NB), f32),
-        in_specs=[SMEM, SMEM] + [VMEM] * 11,
+        in_specs=[SMEM, SMEM] + [VMEM] * (9 + len(parcels)),
         out_specs=VMEM,
         scratch_shapes=[
+            pltpu.VMEM((nrows * block, width), bf16),
             pltpu.VMEM((ncols * block, width), bf16),
-            pltpu.VMEM(((nrows + ncols) * block, n), bf16),
-            pltpu.VMEM(((nrows + ncols) * block, n), bf16),
+            pltpu.VMEM((nrows * block, n), bf16),
+            pltpu.VMEM((nrows * block, n), bf16),
+            half,
+            half,
             pltpu.VMEM((n // WB, WB, WB), bf16),
             pltpu.VMEM((n // WB, WB, WB), bf16),
         ],
-        compiler_params=pltpu.CompilerParams(vmem_limit_bytes=36 << 20),
+        compiler_params=pltpu.CompilerParams(vmem_limit_bytes=GRANT),
         cost_estimate=pl.CostEstimate(flops=12_000_000_000, bytes_accessed=8_000_000, transcendentals=0),
         name="bulk",
-    )(at, amplitude, rows, cols_near, cols_other, points, uh0, ul0, inv0, uh1, ul1, inv1, noise_rows)
+    )(at, amplitude, points, uh0, ul0, inv0, uh1, ul1, inv1, noise_rows, *parcels, passed)
     return out.reshape(nrows, 1, block, ncols, 1, block)
 
 

time: 110 us -> 82.8 us (0.75)
  between operations: 14.6 us -> 0.87 us
  local copies, waits for them, and re-layouts: 9.26 us -> 0.85 us
  Pallas kernels: 55.3 us -> 49.6 us
  starting transfers between devices: 15.8 us -> 17.8 us
    unnamed x19 -> x3, local copies, waits for them, and re-layouts: 8.53 us -> 0.73 us
    pallas_call x1, Pallas kernels: 25.5 us -> 19.8 us  [local(): pl.pallas_call(bulk_kernel, out_shape=jax.ShapeDtypeStruct((nrows * block...]
    ppermute x11 -> x14, starting transfers between devices: 15.8 us -> 17.8 us  [exchange(): lax.ppermute(x, axis, [(i, i ^ k) for i in range(lax.axis_size(axis))])]
    ppermute x11 -> x14, waiting for transfers between devices: 10.5 us -> 10.3 us  [exchange(): lax.ppermute(x, axis, [(i, i ^ k) for i in range(lax.axis_size(axis))])]
  transfers between devices with their start and end apart: 12 -> 14, of which waited for: 4 -> 4; matrix products, arithmetic and copies ran while one was open for 1% -> 2% of each run, Pallas kernels for 27% -> 36%
where the time goes in v3:
time: 82.8 us; the launch traced here: 81.6 us
  Pallas kernels  49.6 us (60%)
  starting transfers between devices  17.8 us (21%)
  waiting for transfers between devices  10.3 us (12%)
  other arithmetic  2.2 us (3%)
  between operations  0.87 us (1%)
  local copies, waits for them, and re-layouts  0.85 us (1%)
    pallas_call x1, Pallas kernels, local(): pl.pallas_call(bulk_kernel, out_shape=jax.ShapeDtypeStruct((nrows * block...  19.8 us
    ppermute x14, starting transfers between devices, exchange(): lax.ppermute(x, axis, [(i, i ^ k) for i in range(lax.axis_size(axis))])  17.8 us
    pallas_call x1, Pallas kernels, local(): pl.pallas_call(first_kernel, out_shape=[jax.ShapeDtypeStruct((n, width),...  17.5 us
    pallas_call x1, Pallas kernels, local(): pl.pallas_call(second_kernel, out_shape=[jax.ShapeDtypeStruct((n1, n1), b...  12.3 us
    ppermute x14, waiting for transfers between devices, exchange(): lax.ppermute(x, axis, [(i, i ^ k) for i in range(lax.axis_size(axis))])  10.3 us
  transfers between devices with their start and end apart: 14, of which 4 were waited for; matrix products, arithmetic and copies ran while one was open for 2% of the time, Pallas kernels for 36%

profile of v3, /device:TPU:31, one launch (start us, length us, event | category | flops | bytes accessed | tf_op | source)
XLA Modules:
  0.0 81.6 jit_solution(10040891571151412537)
XLA Ops:
  0.0 0.2 collective-permute-start.2
  0.2 1.2 %collective-permute-start.1 = (bf16[2,64,512]{2,1,0:T(8,128)(2,1)}, bf16[2,64,512]{2,1,0:T(8,128)(2,1)S(1)}, u32[]{:S(2)}, u32[]{:S(2)}) collective-permute-start(bf16[2,64,512]{2,1,0:T(8,128)(2,1)} %bitcast.56), channel_id=1, source_target_pairs={{0,16},{8,24},{16,0},{24,8},{1,17},{9,25},{17,1},{25,9},{2,18},{10... | collective-permute-start | bytes 393224 | tf_op jit(solution)/shard_map/ppermute | solution.py:358
  1.4 1.2 %collective-permute-start = (bf16[2,64,512]{2,1,0:T(8,128)(2,1)}, bf16[2,64,512]{2,1,0:T(8,128)(2,1)S(1)}, u32[]{:S(2)}, u32[]{:S(2)}) collective-permute-start(bf16[2,64,512]{2,1,0:T(8,128)(2,1)} %bitcast.57), channel_id=1, source_target_pairs={{0,8},{8,0},{16,24},{24,16},{1,9},{9,1},{17,25},{25,17},{2,10},{10... | collective-permute-start | bytes 393224 | tf_op jit(solution)/shard_map/ppermute | solution.py:358
  2.6 0.0 copy-start
  2.7 0.7 copy.7
  3.4 0.1 pad_add_fusion.at_ref
  3.5 2.1 %collective-permute-done.2 = bf16[2,64,512]{2,1,0:T(8,128)(2,1)S(1)} collective-permute-done((bf16[2,64,512]{2,1,0:T(8,128)(2,1)}, bf16[2,64,512]{2,1,0:T(8,128)(2,1)S(1)}, u32[]{:S(2)}, u32[]{:S(2)}) %collective-permute-start.2) | collective-permute-done | bytes 131104 | tf_op jit(solution)/shard_map/ppermute | solution.py:358
  5.6 2.3 %collective-permute-done.1 = bf16[2,64,512]{2,1,0:T(8,128)(2,1)S(1)} collective-permute-done((bf16[2,64,512]{2,1,0:T(8,128)(2,1)}, bf16[2,64,512]{2,1,0:T(8,128)(2,1)S(1)}, u32[]{:S(2)}, u32[]{:S(2)}) %collective-permute-start.1) | collective-permute-done | bytes 131104 | tf_op jit(solution)/shard_map/ppermute | solution.py:358
  7.9 0.0 collective-permute-done
  7.9 0.9 %fusion.5 = (bf16[1,64,512]{2,1,0:T(8,128)(2,1)S(1)}, bf16[1,64,512]{2,1,0:T(8,128)(2,1)S(1)}) fusion(pred[]{:T(512)S(6)} %eq.26, pred[]{:T(512)S(6)} %eq.25, pred[]{:T(512)S(6)} %eq.24, bf16[2,64,512]{2,1,0:T(8,128)(2,1)S(1)} %collective-permute-done, bf16[2,64,512]{2,1,0:T(8,128)(2,1)S(1)} %collective-permute-done.1, ...), kind=kLoop, calls=%fused_computation.19 | loop fusion | flops 196608 | bytes 393222 | tf_op jit(solution)/shard_map/jit(_where)/select_n | solution.py:364
  8.8 0.1 collective-permute-start.5
  8.9 1.3 %collective-permute-start.4 = (bf16[2,64,512]{2,1,0:T(8,128)(2,1)S(1)}, bf16[2,64,512]{2,1,0:T(8,128)(2,1)S(1)}, u32[]{:S(2)}, u32[]{:S(2)}) collective-permute-start(bf16[2,64,512]{2,1,0:T(8,128)(2,1)S(1)} %pad_maximum_fusion.7), channel_id=1, source_target_pairs={{0,4},{1,5},{2,6},{3,7},{4,0},{5,1},{6,2},{7,3},{8,12},{9,13},{10,... | collective-permute-start | bytes 393224 | tf_op jit(solution)/shard_map/ppermute | solution.py:358
  10.2 2.2 %collective-permute-start.3 = (bf16[2,64,512]{2,1,0:T(8,128)(2,1)S(1)}, bf16[2,64,512]{2,1,0:T(8,128)(2,1)S(1)}, u32[]{:S(2)}, u32[]{:S(2)}) collective-permute-start(bf16[2,64,512]{2,1,0:T(8,128)(2,1)S(1)} %pad_maximum_fusion.7), channel_id=1, source_target_pairs={{0,2},{1,3},{2,0},{3,1},{4,6},{5,7},{6,4},{7,5},{8,10},{9,11},{10,... | collective-permute-start | bytes 393224 | tf_op jit(solution)/shard_map/ppermute | solution.py:358
  13.1 1.8 %collective-permute-start.9 = (f32[2,512]{1,0:T(2,128)S(1)}, f32[2,512]{1,0:T(2,128)S(1)}, u32[]{:S(2)}, u32[]{:S(2)}) collective-permute-start(f32[2,512]{1,0:T(2,128)S(1)} %bitcast.50), channel_id=1, source_target_pairs={{0,8},{8,0},{16,24},{24,16},{1,9},{9,1},{17,25},{25,17},{2,10},{10... | collective-permute-start | bytes 12296 | tf_op jit(solution)/shard_map/ppermute | solution.py:358
  14.9 0.2 collective-permute-start.8
  15.1 1.0 %pad_maximum_fusion.1 = bf16[4,2,64,512]{3,2,1,0:T(8,128)(2,1)S(1)} fusion(bf16[1,2,64,512]{3,2,1,0:T(8,128)(2,1)S(1)} %bitcast.61, bf16[1,2,64,512]{3,2,1,0:T(8,128)(2,1)S(1)} %bitcast.62, bf16[1,2,64,512]{3,2,1,0:T(8,128)(2,1)S(1)} %bitcast.63, bf16[1,2,64,512]{3,2,1,0:T(8,128)(2,1)} %bitcast.58), kind=kLoop, calls=%fused_computation.1 | loop fusion | flops 786432 | bytes 1048576 | tf_op jit(solution)/shard_map/stack | solution.py:387
  16.1 0.0 collective-permute-done.5
  16.1 1.1 %collective-permute-start.7 = (f32[2,512]{1,0:T(2,128)S(1)}, f32[2,512]{1,0:T(2,128)S(1)}, u32[]{:S(2)}, u32[]{:S(2)}) collective-permute-start(f32[2,512]{1,0:T(2,128)S(1)} %bitcast.52), channel_id=1, source_target_pairs={{0,24},{8,16},{16,8},{24,0},{1,25},{9,17},{17,9},{25,1},{2,26},{10... | collective-permute-start | bytes 12296 | tf_op jit(solution)/shard_map/ppermute | solution.py:358
  17.2 3.4 %collective-permute-done.4 = bf16[2,64,512]{2,1,0:T(8,128)(2,1)S(1)} collective-permute-done((bf16[2,64,512]{2,1,0:T(8,128)(2,1)S(1)}, bf16[2,64,512]{2,1,0:T(8,128)(2,1)S(1)}, u32[]{:S(2)}, u32[]{:S(2)}) %collective-permute-start.4) | collective-permute-done | bytes 131104 | tf_op jit(solution)/shard_map/ppermute | solution.py:358
  20.6 0.0 collective-permute-done.3
  20.6 0.1 pad_maximum_fusion.2.mine_ref
  20.7 2.5 %collective-permute-start.6 = (bf16[4,2,64,512]{3,2,1,0:T(8,128)(2,1)S(1)}, bf16[4,2,64,512]{3,2,1,0:T(8,128)(2,1)S(1)}, u32[]{:S(2)}, u32[]{:S(2)}) collective-permute-start(bf16[4,2,64,512]{3,2,1,0:T(8,128)(2,1)S(1)} %pad_maximum_fusion.2.mine_ref), channel_id=1, source_target_pairs={{0,1},{1,0},{2,3},{3,2},{4,5},{5,4},{6,7},{7,6},{8,9},{9,8},{10,11... | collective-permute-start | bytes 1572872 | tf_op jit(solution)/shard_map/ppermute | solution.py:358
  23.2 0.0 collective-permute-done.9
  23.2 0.0 collective-permute-done.8
  23.2 0.0 collective-permute-done.7
  23.3 0.1 dynamic-slice_bitcast_fusion.1
  23.3 0.0 copy-done
  23.3 0.1 fusion.3
  23.4 1.1 %collective-permute-start.12 = (bf16[4,64,512]{2,1,0:T(8,128)(2,1)S(1)}, bf16[4,64,512]{2,1,0:T(8,128)(2,1)S(1)}, u32[]{:S(2)}, u32[]{:S(2)}) collective-permute-start(bf16[4,64,512]{2,1,0:T(8,128)(2,1)S(1)} %get-tuple-element.49), channel_id=1, source_target_pairs={{0,6},{1,7},{2,4},{3,5},{4,2},{5,3},{6,0},{7,1},{8,14},{9,15},{10,... | collective-permute-start | bytes 786440 | tf_op jit(solution)/shard_map/ppermute | solution.py:358
  24.6 0.0 collective-permute-start.10
  24.6 2.5 %collective-permute-start.11 = (bf16[4,64,512]{2,1,0:T(8,128)(2,1)S(1)}, bf16[4,64,512]{2,1,0:T(8,128)(2,1)S(1)}, u32[]{:S(2)}, u32[]{:S(2)}) collective-permute-start(bf16[4,64,512]{2,1,0:T(8,128)(2,1)S(1)} %get-tuple-element.51), channel_id=1, source_target_pairs={{0,4},{1,5},{2,6},{3,7},{4,0},{5,1},{6,2},{7,3},{8,12},{9,13},{10,... | collective-permute-start | bytes 786440 | tf_op jit(solution)/shard_map/ppermute | solution.py:358
  27.0 0.0 collective-permute-done.6.other_ref
  27.0 17.5 %first.1 = (bf16[1024,512]{1,0:T(8,128)(2,1)S(1)}, bf16[512,1024]{1,0:T(8,128)(2,1)S(1)}, bf16[512,1024]{1,0:T(8,128)(2,1)S(1)}, f32[4,128,128]{2,1,0:T(8,128)S(1)}, f32[512,512]{1,0:T(8,128)S(1)}) custom-call(s32[4]{0:T(128)S(1)} %pad_add_fusion.at_ref, f32[1]{0:T(128)S(6)} %copy.8.amp_ref, bf16[4,2,64,512]{3,2,1,0:T(8,128)(2,1)S(1)} %pad_maximum_fusion.2.mine_ref, ...), custom_call_target="tpu_custom_call" | custom-call | flops 20000000000 | bytes 8000000 | tf_op jit(solution)/shard_map/first/pallas_call | solution.py:403
  44.5 0.0 collective-permute-done.12.refs_11_
  44.5 0.0 collective-permute-done.10.refs_9_
  44.5 2.5 %collective-permute-done.11.refs_10_ = bf16[4,64,512]{2,1,0:T(8,128)(2,1)S(1)} collective-permute-done((bf16[4,64,512]{2,1,0:T(8,128)(2,1)S(1)}, bf16[4,64,512]{2,1,0:T(8,128)(2,1)S(1)}, u32[]{:S(2)}, u32[]{:S(2)}) %collective-permute-start.11) | collective-permute-done | bytes 262176 | tf_op jit(solution)/shard_map/ppermute | solution.py:358
  47.1 0.1 pad_maximum_fusion
  47.2 2.3 %collective-permute-start.13 = (bf16[4,3,64,512]{3,2,1,0:T(8,128)(2,1)S(1)}, bf16[4,3,64,512]{3,2,1,0:T(8,128)(2,1)S(1)}, u32[]{:S(2)}, u32[]{:S(2)}) collective-permute-start(bf16[4,3,64,512]{3,2,1,0:T(8,128)(2,1)S(1)} %pad_maximum_fusion), channel_id=1, source_target_pairs={{0,1},{1,0},{2,3},{3,2},{4,5},{5,4},{6,7},{7,6},{8,9},{9,8},{10,11... | collective-permute-start | bytes 2359304 | tf_op jit(solution)/shard_map/ppermute | solution.py:358
  49.5 12.3 %second.1 = (bf16[512,512]{1,0:T(8,128)(2,1)S(1)}, bf16[512,512]{1,0:T(8,128)(2,1)S(1)}, f32[4,128,128]{2,1,0:T(8,128)S(1)}) custom-call(f32[512,512]{1,0:T(8,128)S(1)} %get-tuple-element.31.rest_ref), custom_call_target="tpu_custom_call" | custom-call | flops 20000000000 | bytes 8000000 | tf_op jit(solution)/shard_map/second/pallas_call | solution.py:421
  61.7 0.0 collective-permute-done.13.refs_12_
  61.7 19.8 %bulk.1 = f32[4096,128]{1,0:T(8,128)} custom-call(s32[4]{0:T(128)S(1)} %pad_add_fusion.at_ref, f32[1]{0:T(128)S(6)} %copy.8.amp_ref, bf16[1024,512]{1,0:T(8,128)(2,1)S(1)} %get-tuple-element.25.refs_0_, bf16[512,1024]{1,0:T(8,128)(2,1)S(1)} %get-tuple-element.26.refs_1_, bf16[512,1024]{1,0:T(8,128)(2,1)S(1)} %get-tuple-element.27.refs_2_, ...), custom_call_target="tpu_custom_call" | custom-call | flops 12000000000 | bytes 8000000 | tf_op jit(solution)/shard_map/bulk/pallas_call | solution.py:436
  (5 shorter events, 0.1 us)
Async XLA Ops:
  0.0 5.6 %collective-permute-start.2 = (bf16[2,64,512]{2,1,0:T(8,128)(2,1)}, bf16[2,64,512]{2,1,0:T(8,128)(2,1)S(1)}, u32[]{:S(2)}, u32[]{:S(2)}) collective-permute-start(bf16[2,64,512]{2,1,0:T(8,128)(2,1)} %bitcast.55), channel_id=1, source_target_pairs={{0,24},{8,16},{16,8},{24,0},{1,25},{9,17},{17,9},{25,1},{2,26},{10... | collective-permute-start | bytes 393224 | tf_op jit(solution)/shard_map/ppermute | solution.py:358
  0.2 7.7 %collective-permute-start.1 = (bf16[2,64,512]{2,1,0:T(8,128)(2,1)}, bf16[2,64,512]{2,1,0:T(8,128)(2,1)S(1)}, u32[]{:S(2)}, u32[]{:S(2)}) collective-permute-start(bf16[2,64,512]{2,1,0:T(8,128)(2,1)} %bitcast.56), channel_id=1, source_target_pairs={{0,16},{8,24},{16,0},{24,8},{1,17},{9,25},{17,1},{25,9},{2,18},{10... | collective-permute-start | bytes 393224 | tf_op jit(solution)/shard_map/ppermute | solution.py:358
  1.4 6.4 %collective-permute-start = (bf16[2,64,512]{2,1,0:T(8,128)(2,1)}, bf16[2,64,512]{2,1,0:T(8,128)(2,1)S(1)}, u32[]{:S(2)}, u32[]{:S(2)}) collective-permute-start(bf16[2,64,512]{2,1,0:T(8,128)(2,1)} %bitcast.57), channel_id=1, source_target_pairs={{0,8},{8,0},{16,24},{24,16},{1,9},{9,1},{17,25},{25,17},{2,10},{10... | collective-permute-start | bytes 393224 | tf_op jit(solution)/shard_map/ppermute | solution.py:358
  2.6 20.7 %copy-start = (bf16[2,1,64,512]{3,2,1,0:T(8,128)(2,1)S(1)}, bf16[2,1,64,512]{3,2,1,0:T(8,128)(2,1)}, u32[]{:S(2)}) copy-start(bf16[2,1,64,512]{3,2,1,0:T(8,128)(2,1)} %param.3) | copy-start | bytes 393220
  8.8 7.3 %collective-permute-start.5 = (bf16[2,64,512]{2,1,0:T(8,128)(2,1)S(1)}, bf16[2,64,512]{2,1,0:T(8,128)(2,1)S(1)}, u32[]{:S(2)}, u32[]{:S(2)}) collective-permute-start(bf16[2,64,512]{2,1,0:T(8,128)(2,1)S(1)} %pad_maximum_fusion.7), channel_id=1, source_target_pairs={{0,6},{1,7},{2,4},{3,5},{4,2},{5,3},{6,0},{7,1},{8,14},{9,15},{10,... | collective-permute-start | bytes 393224 | tf_op jit(solution)/shard_map/ppermute | solution.py:358
  8.9 11.7 %collective-permute-start.4 = (bf16[2,64,512]{2,1,0:T(8,128)(2,1)S(1)}, bf16[2,64,512]{2,1,0:T(8,128)(2,1)S(1)}, u32[]{:S(2)}, u32[]{:S(2)}) collective-permute-start(bf16[2,64,512]{2,1,0:T(8,128)(2,1)S(1)} %pad_maximum_fusion.7), channel_id=1, source_target_pairs={{0,4},{1,5},{2,6},{3,7},{4,0},{5,1},{6,2},{7,3},{8,12},{9,13},{10,... | collective-permute-start | bytes 393224 | tf_op jit(solution)/shard_map/ppermute | solution.py:358
  10.2 10.4 %collective-permute-start.3 = (bf16[2,64,512]{2,1,0:T(8,128)(2,1)S(1)}, bf16[2,64,512]{2,1,0:T(8,128)(2,1)S(1)}, u32[]{:S(2)}, u32[]{:S(2)}) collective-permute-start(bf16[2,64,512]{2,1,0:T(8,128)(2,1)S(1)} %pad_maximum_fusion.7), channel_id=1, source_target_pairs={{0,2},{1,3},{2,0},{3,1},{4,6},{5,7},{6,4},{7,5},{8,10},{9,11},{10,... | collective-permute-start | bytes 393224 | tf_op jit(solution)/shard_map/ppermute | solution.py:358
  13.1 10.1 %collective-permute-start.9 = (f32[2,512]{1,0:T(2,128)S(1)}, f32[2,512]{1,0:T(2,128)S(1)}, u32[]{:S(2)}, u32[]{:S(2)}) collective-permute-start(f32[2,512]{1,0:T(2,128)S(1)} %bitcast.50), channel_id=1, source_target_pairs={{0,8},{8,0},{16,24},{24,16},{1,9},{9,1},{17,25},{25,17},{2,10},{10... | collective-permute-start | bytes 12296 | tf_op jit(solution)/shard_map/ppermute | solution.py:358
  14.9 8.3 %collective-permute-start.8 = (f32[2,512]{1,0:T(2,128)S(1)}, f32[2,512]{1,0:T(2,128)S(1)}, u32[]{:S(2)}, u32[]{:S(2)}) collective-permute-start(f32[2,512]{1,0:T(2,128)S(1)} %bitcast.51), channel_id=1, source_target_pairs={{0,16},{8,24},{16,0},{24,8},{1,17},{9,25},{17,1},{25,9},{2,18},{10... | collective-permute-start | bytes 12296 | tf_op jit(solution)/shard_map/ppermute | solution.py:358
  16.1 7.1 %collective-permute-start.7 = (f32[2,512]{1,0:T(2,128)S(1)}, f32[2,512]{1,0:T(2,128)S(1)}, u32[]{:S(2)}, u32[]{:S(2)}) collective-permute-start(f32[2,512]{1,0:T(2,128)S(1)} %bitcast.52), channel_id=1, source_target_pairs={{0,24},{8,16},{16,8},{24,0},{1,25},{9,17},{17,9},{25,1},{2,26},{10... | collective-permute-start | bytes 12296 | tf_op jit(solution)/shard_map/ppermute | solution.py:358
  20.7 6.4 %collective-permute-start.6 = (bf16[4,2,64,512]{3,2,1,0:T(8,128)(2,1)S(1)}, bf16[4,2,64,512]{3,2,1,0:T(8,128)(2,1)S(1)}, u32[]{:S(2)}, u32[]{:S(2)}) collective-permute-start(bf16[4,2,64,512]{3,2,1,0:T(8,128)(2,1)S(1)} %pad_maximum_fusion.2.mine_ref), channel_id=1, source_target_pairs={{0,1},{1,0},{2,3},{3,2},{4,5},{5,4},{6,7},{7,6},{8,9},{9,8},{10,11... | collective-permute-start | bytes 1572872 | tf_op jit(solution)/shard_map/ppermute | solution.py:358
  23.4 21.1 %collective-permute-start.12 = (bf16[4,64,512]{2,1,0:T(8,128)(2,1)S(1)}, bf16[4,64,512]{2,1,0:T(8,128)(2,1)S(1)}, u32[]{:S(2)}, u32[]{:S(2)}) collective-permute-start(bf16[4,64,512]{2,1,0:T(8,128)(2,1)S(1)} %get-tuple-element.49), channel_id=1, source_target_pairs={{0,6},{1,7},{2,4},{3,5},{4,2},{5,3},{6,0},{7,1},{8,14},{9,15},{10,... | collective-permute-start | bytes 786440 | tf_op jit(solution)/shard_map/ppermute | solution.py:358
  24.6 20.0 %collective-permute-start.10 = (bf16[4,64,512]{2,1,0:T(8,128)(2,1)S(1)}, bf16[4,64,512]{2,1,0:T(8,128)(2,1)S(1)}, u32[]{:S(2)}, u32[]{:S(2)}) collective-permute-start(bf16[4,64,512]{2,1,0:T(8,128)(2,1)S(1)} %get-tuple-element.50), channel_id=1, source_target_pairs={{0,2},{1,3},{2,0},{3,1},{4,6},{5,7},{6,4},{7,5},{8,10},{9,11},{10,... | collective-permute-start | bytes 786440 | tf_op jit(solution)/shard_map/ppermute | solution.py:358
  24.6 22.4 %collective-permute-start.11 = (bf16[4,64,512]{2,1,0:T(8,128)(2,1)S(1)}, bf16[4,64,512]{2,1,0:T(8,128)(2,1)S(1)}, u32[]{:S(2)}, u32[]{:S(2)}) collective-permute-start(bf16[4,64,512]{2,1,0:T(8,128)(2,1)S(1)} %get-tuple-element.51), channel_id=1, source_target_pairs={{0,4},{1,5},{2,6},{3,7},{4,0},{5,1},{6,2},{7,3},{8,12},{9,13},{10,... | collective-permute-start | bytes 786440 | tf_op jit(solution)/shard_map/ppermute | solution.py:358
  47.2 14.6 %collective-permute-start.13 = (bf16[4,3,64,512]{3,2,1,0:T(8,128)(2,1)S(1)}, bf16[4,3,64,512]{3,2,1,0:T(8,128)(2,1)S(1)}, u32[]{:S(2)}, u32[]{:S(2)}) collective-permute-start(bf16[4,3,64,512]{3,2,1,0:T(8,128)(2,1)S(1)} %pad_maximum_fusion), channel_id=1, source_target_pairs={{0,1},{1,0},{2,3},{3,2},{4,5},{5,4},{6,7},{7,6},{8,9},{9,8},{10,11... | collective-permute-start | bytes 2359304 | tf_op jit(solution)/shard_map/ppermute | solution.py:358

commit v4 on v3

v4 whole, which is shorter than its diff:
```python
import functools

import jax
import jax.numpy as jnp
from jax import lax
from jax.experimental import pallas as pl
from jax.experimental.pallas import tpu as pltpu
from jax.sharding import PartitionSpec as P

PANELS = 2
NB = 128
WB = 256
GRANT = 30 << 20
UPDATE_ROWS = 256
FIRST = 5
f32 = jnp.float32
bf16 = jnp.bfloat16
TRANS_B = (((1,), (1,)), ((), ()))
TRANS_A = (((0,), (0,)), ((), ()))


def split(x):
    hi = x.astype(bf16)
    return hi, (x - hi.astype(f32)).astype(bf16)


def dot_nn(ah, al, bh, bl):
    return jnp.dot(
        jnp.concatenate([ah, ah, al], 1), jnp.concatenate([bh, bl, bh], 0), preferred_element_type=f32
    )


def dot_nt(ah, al, bh, bl):
    return lax.dot_general(
        jnp.concatenate([ah, ah, al], 1), jnp.concatenate([bh, bl, bh], 1), TRANS_B, preferred_element_type=f32
    )


def dot_tn(ah, al, bh, bl):
    return lax.dot_general(
        jnp.concatenate([ah, ah, al], 0), jnp.concatenate([bh, bl, bh], 0), TRANS_A, preferred_element_type=f32
    )


def spread(x):
    return jnp.broadcast_to(x, (8, NB))


def tree_sum(xs):
    while len(xs) > 1:
        xs = [xs[i] + xs[i + 1] if i + 1 < len(xs) else xs[i] for i in range(0, len(xs), 2)]
    return xs[0]


def factor_tile(t, rows, cols, lane, sub):
    scaled, ratio, inverses, pivots = [], {}, [], None
    for j in range(8):
        pivot = spread(cols[j][j : j + 1, :])
        inv = 1.0 / pivot
        inverses.append(inv)
        pivots = pivot if j == 0 else jnp.where(sub == j, pivot, pivots)
        below = jnp.where(sub > j, cols[j], 0.0)
        for k in range(j + 1, 8):
            entry = spread(cols[k][j : j + 1, :])
            cols[k] = cols[k] - (below * entry) * inv
            ratio[j, k] = entry * inv
        row = spread(rows[j : j + 1, :]) * inv
        row = jnp.where(lane == 8 * t + j, 1.0 + inv, row)
        scaled.append(row)
        if j < 7:
            rows = rows - below * row
    return rows, lax.rsqrt(pivots), scaled, ratio, inverses


def factor_block(tiles, store_u, store_l):
    tiles = list(tiles)
    n = len(tiles)
    lane = lax.broadcasted_iota(jnp.int32, (8, NB), 1)
    sub = lax.broadcasted_iota(jnp.int32, (8, NB), 0)
    cols = [spread(tiles[0][:, k : k + 1]) for k in range(8)]
    for t in range(n):
        last = t + 1 == n
        if not last:
            near = [spread(tiles[t + 1][:, 8 * t + k : 8 * t + k + 1]) for k in range(8)]
            ahead = [spread(tiles[t + 1][:, 8 * t + 8 + k : 8 * t + 9 + k]) for k in range(8)]
        far = {i: [spread(tiles[i][:, 8 * t + k : 8 * t + k + 1]) for k in range(8)] for i in range(t + 2, n)}
        rows, root, scaled, ratio, inverses = factor_tile(t, tiles[t], cols, lane, sub)
        if not last:
            for j in range(8):
                part = near[j] * inverses[j]
                for k in range(j + 1, 8):
                    near[k] = near[k] - near[j] * ratio[j, k]
                for k in range(8):
                    ahead[k] = ahead[k] - near[j] * spread(part[k : k + 1, :])
                tiles[t + 1] = tiles[t + 1] - near[j] * scaled[j]
            cols = ahead
        back = list(scaled)
        for j in range(6, -1, -1):
            for k in range(7, j, -1):
                back[j] = back[j] - ratio[j, k] * back[k]
        for i in range(t + 2, n):
            tiles[i] = tiles[i] - tree_sum([far[i][j] * back[j] for j in range(8)])
        final = rows * root
        diff = lane - sub - 8 * t
        store_u(t, jnp.where(diff >= 0, final, 0.0))
        store_l(t, jnp.where(diff < 0, final, jnp.where(diff == 0, root, 0.0)))


def half_norm_rows(x):
    xf = x.astype(f32)
    hi, lo = split(xf * xf)
    ones = jnp.ones((8, x.shape[1]), bf16)
    total = lax.dot_general(ones, hi, TRANS_B, preferred_element_type=f32)
    total = total + lax.dot_general(ones, lo, TRANS_B, preferred_element_type=f32)
    return 0.5 * total[0:1]


def half_norm_cols(x, width):
    xf = x.astype(f32)
    hi, lo = split(xf * xf)
    ones = jnp.ones((NB, x.shape[1]), bf16)
    total = lax.dot_general(hi, ones, TRANS_B, preferred_element_type=f32)
    total = 0.5 * (total + lax.dot_general(lo, ones, TRANS_B, preferred_element_type=f32))
    return jnp.concatenate([total] * (width // NB), 1)


def diagonal(n):
    return lax.broadcasted_iota(jnp.int32, (n, n), 0) == lax.broadcasted_iota(jnp.int32, (n, n), 1)


def place(x_ref, base, piece_at, piece, value):
    at = pl.multiple_of(base + piece_at * piece, piece)
    x_ref[pl.ds(at, piece), :] = value


def factor_panels(a_ref, u_ref, wh_ref, wl_ref, inv_ref, row0, count, block):
    n = a_ref.shape[1]

    def panel(p, carry):
        r = pl.multiple_of(p * NB, NB)
        o = pl.multiple_of(row0 + p * NB, NB)
        d = a_ref[pl.ds(r, NB), pl.ds(o, NB)]

        def store_u(t, v):
            u_ref[pl.ds(pl.multiple_of(r + 8 * t, 8), 8), pl.ds(o, NB)] = v

        def store_l(t, v):
            inv_ref[8 * t : 8 * t + 8, :] = v

        factor_block([d[8 * t : 8 * t + 8] for t in range(NB // 8)], store_u, store_l)
        for k in range(count):

            @pl.when(p == k)
            def _():
                lr = k * NB
                rows = slice(lr, lr + NB)
                s = row0 + lr
                e = s + NB
                ih, il = split(inv_ref[...])
                parts = ([a_ref[rows, :s]] if s else []) + ([a_ref[rows, e:]] if e < n else [])
                row = dot_nn(ih, il, *split(jnp.concatenate(parts, 1)))
                hi, lo = split(row)
                for w_ref, w, diag in ((wh_ref, hi, ih), (wl_ref, lo, il)):
                    if s:
                        w_ref[rows, :s] = w[:, :s]
                    w_ref[rows, s:e] = diag
                    end = (s // block + 1) * block
                    if e < end:
                        w_ref[rows, e:end] = jnp.zeros((NB, end - e), bf16)
                if e < n:
                    u_ref[rows, e:] = row[:, s:]
                    right_h = jnp.concatenate(([hi[:, :s]] if s else []) + [ih, hi[:, s:]], 1)
                    right_l = jnp.concatenate(([lo[:, :s]] if s else []) + [il, lo[:, s:]], 1)
                    for i in range(0, n - e, UPDATE_ROWS):
                        f = min(i + UPDATE_ROWS, n - e)
                        change = dot_tn(hi[:, s + i : s + f], lo[:, s + i : s + f], right_h, right_l)
                        q = slice(lr + NB + i, lr + NB + f)
                        if s:
                            a_ref[q, :s] = a_ref[q, :s] - change[:, :s]
                        a_ref[q, s:e] = -change[:, s:e]
                        a_ref[q, e:] = a_ref[q, e:] - change[:, e:]

        return carry

    lax.fori_loop(0, count, panel, 0)


def first_kernel(at_ref, amp_ref, mine_ref, other_ref, nz_ref, x_ref, u_ref, wh_ref, wl_ref, rest_ref, a_ref, inv_ref):
    n = a_ref.shape[0]
    steps, panels, piece = mine_ref.shape[:3]
    block = n // panels
    me = at_ref[1]
    for m in range(steps):
        for s in range(panels):
            place(x_ref, s * block, me ^ (2 * m), piece, mine_ref[m, s])
            place(x_ref, s * block, me ^ (2 * m + 1), piece, other_ref[m, s])
    amp = amp_ref[0]
    sq_row = half_norm_rows(x_ref[...])
    noise = nz_ref[...]
    for o in range(0, n, WB):
        xi = x_ref[o : o + WB, :]
        cross = lax.dot_general(xi, x_ref[o:, :], TRANS_B, preferred_element_type=f32)
        k = amp * jnp.exp(cross - half_norm_cols(xi, n - o) - sq_row[:, o:])
        a_ref[o : o + WB, o:] = k
        row = noise[o // block : o // block + 1, o % block : o % block + WB]
        a_ref[o : o + WB, o : o + WB] = k[:, :WB] + jnp.where(diagonal(WB), jnp.broadcast_to(row, (WB, WB)), 0.0)
    count = u_ref.shape[0] // NB
    factor_panels(a_ref, u_ref, wh_ref, wl_ref, inv_ref, 0, count, block)
    rest_ref[...] = a_ref[count * NB :, :]


def second_kernel(rest_ref, u_ref, wh_ref, wl_ref, a_ref, inv_ref):
    n1, n = rest_ref.shape
    a_ref[...] = rest_ref[...]
    factor_panels(a_ref, u_ref, wh_ref, wl_ref, inv_ref, n - n1, n1 // NB, n // PANELS)


def store_block(out_ref, a, b, row, ncols, value):
    rows, block = value.shape
    per = block // NB
    for q in range(per):
        at = ((a * block + row) * ncols + b) * per + q
        out_ref[pl.ds(at, rows, stride=ncols * per), :] = value[:, q * NB : (q + 1) * NB]


def bulk_kernel(at_ref, amp_ref, *refs):
    x_ref, u0_ref, wh0_ref, wl0_ref, u1_ref, wh1_ref, wl1_ref, nz_ref = refs[:8]
    refs = refs[8:]
    count = len(refs) - 10
    near_refs, other_ref, out_ref = refs[:count], refs[count], refs[count + 1]
    r_ref, c_ref, kh_ref, kl_ref, ph_ref, pl_ref, zh_ref, zl_ref = refs[count + 2 :]
    n = x_ref.shape[0]
    split_at = u0_ref.shape[0]
    nrows, block = nz_ref.shape
    piece = other_ref.shape[2]
    ncols = c_ref.shape[0] // block
    row_at, me, row_n, col_n = at_ref[0], at_ref[1], at_ref[2], at_ref[3]
    amp = amp_ref[0]
    for m in range(count):
        for a in range(nrows):
            place(r_ref, a * block, me ^ (2 * m), piece, near_refs[m][a])
            place(r_ref, a * block, me ^ (2 * m + 1), piece, other_ref[m, a])
        for b in range(ncols):
            place(c_ref, b * block, me ^ (2 * m), piece, near_refs[m][nrows + ncols + b])
            place(c_ref, b * block, me ^ (2 * m + 1), piece, other_ref[m, nrows + b])

    def pick(first_ref, second_ref, r0, r1, c0, c1):
        parts = []
        if r0 < split_at:
            parts.append(first_ref[r0 : min(r1, split_at), c0:c1])
        if r1 > split_at:
            parts.append(second_ref[max(r0, split_at) - split_at : r1 - split_at, c0:c1])
        return jnp.concatenate(parts, 0) if len(parts) > 1 else parts[0]

    def inverse(r0, r1, c0, c1):
        return pick(wh0_ref, wh1_ref, r0, r1, c0, c1), pick(wl0_ref, wl1_ref, r0, r1, c0, c1)

    lead_sq = half_norm_rows(x_ref[...])

    def entries(x):
        cross = lax.dot_general(x, x_ref[...], TRANS_B, preferred_element_type=f32)
        return split(amp * jnp.exp(cross - half_norm_cols(x, n) - lead_sq))

    for a in range(nrows):
        rows = slice(a * block, (a + 1) * block)
        kh_ref[rows, :], kl_ref[rows, :] = entries(r_ref[rows, :])
    for b in range(ncols):
        j = b * col_n + me
        cols = slice(b * block, (b + 1) * block)

        @pl.when(j >= PANELS)
        def _():
            xc = c_ref[cols, :]
            zh_ref[...], zl_ref[...] = entries(xc)
            for s in range(0, n, block):
                e = s + block
                panel = dot_nt(zh_ref[:, :e], zl_ref[:, :e], *inverse(s, e, 0, e))
                ph_ref[:, s:e], pl_ref[:, s:e] = split(panel)
            for s in range(0, n, block):
                e = s + block
                solved = dot_nn(ph_ref[:, s:], pl_ref[:, s:], *inverse(s, n, s, e))
                zh_ref[:, s:e], zl_ref[:, s:e] = split(solved)
            col_sq = half_norm_rows(xc)
            for a in range(nrows):
                i = a * row_n + row_at
                rows = slice(a * block, (a + 1) * block)

                @pl.when(i >= PANELS)
                def _():
                    xr = r_ref[rows, :]
                    cross = lax.dot_general(xr, xc, TRANS_B, preferred_element_type=f32)
                    k = amp * jnp.exp(cross - half_norm_cols(xr, block) - col_sq)
                    on_diag = diagonal(block) & (i == j)
                    k = k + jnp.where(on_diag, jnp.broadcast_to(nz_ref[a : a + 1, :], (block, block)), 0.0)
                    k = k - dot_nt(kh_ref[rows, :], kl_ref[rows, :], zh_ref[...], zl_ref[...])
                    store_block(out_ref, a, b, 0, ncols, k)

                @pl.when(i < PANELS)
                def _():
                    store_block(out_ref, a, b, 0, ncols, jnp.zeros((block, block), f32))

        if b:
            continue
        for s in range(PANELS):
            w = s * block
            for a in range(nrows):
                i = a * row_n + row_at
                rows = slice(a * block, (a + 1) * block)

                @pl.when((j == s) & (i >= PANELS))
                def _():
                    e = w + block
                    panel = dot_nt(kh_ref[rows, :e], kl_ref[rows, :e], *inverse(w, e, 0, e))
                    store_block(out_ref, a, b, 0, ncols, panel)

                if a:
                    continue
                for v in range(PANELS):

                    @pl.when((j == s) & (i == v))
                    def _():
                        if v < s:
                            u = jnp.zeros((block, block), f32)
                        else:
                            u = pick(u0_ref, u1_ref, w, w + block, v * block, (v + 1) * block).T
                        if v == s:
                            row_id = lax.broadcasted_iota(jnp.int32, (block, block), 0)
                            col_id = lax.broadcasted_iota(jnp.int32, (block, block), 1)
                            u = jnp.where(row_id >= col_id, u, 0.0)
                        store_block(out_ref, a, b, 0, ncols, u)


SMEM = pl.BlockSpec(memory_space=pltpu.SMEM)
VMEM = pl.BlockSpec(memory_space=pltpu.VMEM)


def exchange(x, axis, k):
    return lax.ppermute(x, axis, [(i, i ^ k) for i in range(lax.axis_size(axis))])


def choose(index, options):
    out = options[0]
    for k in range(1, len(options)):
        out = jnp.where(index == k, options[k], out)
    return out


def local(features, amplitude, noise):
    row_n = lax.axis_size("row")
    col_n = lax.axis_size("col")
    row_at = lax.axis_index("row")
    col_at = lax.axis_index("col")
    nrows, _, piece, width = features.shape
    block = piece * col_n
    ncols = nrows * row_n // col_n
    n = PANELS * block
    mine = features.reshape(nrows, piece, width)
    noise_rows = noise.reshape(nrows, block)
    plane = [mine] + [exchange(mine, "row", k) for k in range(1, row_n)]
    lead = jnp.stack([choose(row_at ^ s, [p[0] for p in plane]) for s in range(PANELS)])
    noise_rows, lead = lax.optimization_barrier((noise_rows, lead))
    near = [lead] + [exchange(lead, "col", k) for k in range(2, col_n, 2)]
    noises = [noise_rows] + [exchange(noise_rows, "row", k) for k in range(1, row_n)]
    lead_noise = jnp.stack([choose(row_at ^ s, [p[0] for p in noises]) for s in range(PANELS)])
    near = jnp.stack(near)
    other = exchange(near, "col", 1)
    everything, near = lax.optimization_barrier((jnp.stack(plane), near))
    core = col_at & 1

    def parcel(to):
        out = [mine]
        for to_core in (1 - core, core):
            for b in range(ncols):
                number = b * col_n + (to & ~1) + to_core
                at = (row_at ^ (number & (row_n - 1)), number // row_n, 0, 0)
                out.append(lax.dynamic_slice(everything, at, (1, 1, piece, width)).reshape(1, piece, width))
        return jnp.concatenate(out, 0)

    parcels = [parcel(col_at)] + [exchange(parcel(col_at ^ k), "col", k) for k in range(2, col_n, 2)]
    at = jnp.stack([row_at, col_at, jnp.int32(row_n), jnp.int32(col_n)])
    first = FIRST * n // NB // 8 * NB
    n1 = n - first
    params = pltpu.CompilerParams(vmem_limit_bytes=GRANT)
    cost = pl.CostEstimate(flops=20_000_000_000, bytes_accessed=8_000_000, transcendentals=0)
    square = pltpu.VMEM((NB, NB), f32)

    def factor_shapes(rows):
        half = jax.ShapeDtypeStruct((rows, n), bf16)
        return [jax.ShapeDtypeStruct((rows, n), f32), half, half]

    points, u0, wh0, wl0, rest = pl.pallas_call(
        first_kernel,
        out_shape=[jax.ShapeDtypeStruct((n, width), bf16)]
        + factor_shapes(first)
        + [jax.ShapeDtypeStruct((n1, n), f32)],
        in_specs=[SMEM, SMEM, VMEM, VMEM, VMEM],
        out_specs=[VMEM] * 5,
        scratch_shapes=[pltpu.VMEM((n, n), f32), square],
        compiler_params=params,
        cost_estimate=cost,
        name="first",
    )(at, amplitude, near, other, lead_noise)
    parcels, rest = lax.optimization_barrier((parcels, rest))
    passed = exchange(jnp.stack([p[: nrows + ncols] for p in parcels]), "col", 1)
    u1, wh1, wl1 = pl.pallas_call(
        second_kernel,
        out_shape=factor_shapes(n1),
        in_specs=[VMEM],
        out_specs=[VMEM] * 3,
        scratch_shapes=[pltpu.VMEM((n1, n), f32), square],
        compiler_params=params,
        cost_estimate=cost,
        name="second",
    )(rest)
    half = pltpu.VMEM((block, n), bf16)
    tall = pltpu.VMEM((nrows * block, n), bf16)
    out = pl.pallas_call(
        bulk_kernel,
        out_shape=jax.ShapeDtypeStruct((nrows * block * ncols * (block // NB), NB), f32),
        in_specs=[SMEM, SMEM] + [VMEM] * (9 + len(parcels)),
        out_specs=VMEM,
        scratch_shapes=[
            pltpu.VMEM((nrows * block, width), bf16),
            pltpu.VMEM((ncols * block, width), bf16),
            tall,
            tall,
            half,
            half,
            half,
            half,
        ],
        compiler_params=params,
        cost_estimate=cost,
        name="bulk",
    )(at, amplitude, points, u0, wh0, wl0, u1, wh1, wl1, noise_rows, *parcels, passed)
    return out.reshape(nrows, 1, block, ncols, 1, block)


def solution(mesh):
    return jax.shard_map(
        local,
        mesh=mesh,
        in_specs=(P(None, "row", "col", None), P(), P(None, "row", None)),
        out_specs=P(None, "row", None, None, "col", None),
        check_vma=False,
    )
```

time: 82.8 us -> 80.6 us (0.973)
  the two profiles are of different devices: /device:TPU:31 before, /device:TPU:21 now
where the time goes in v4:
time: 80.6 us; the launch traced here: 80.3 us
  Pallas kernels  49 us (61%)
  starting transfers between devices  18.2 us (23%)
  waiting for transfers between devices  9.25 us (11%)
  other arithmetic  2.27 us (3%)
  between operations  0.86 us (1%)
  local copies, waits for them, and re-layouts  0.81 us (1%)
    pallas_call x1, Pallas kernels, local(): pl.pallas_call(first_kernel, out_shape=[jax.ShapeDtypeStruct((n, width),...  22 us
    ppermute x14, starting transfers between devices, exchange(): lax.ppermute(x, axis, [(i, i ^ k) for i in range(lax.axis_size(axis))])  18.2 us
    pallas_call x1, Pallas kernels, local(): pl.pallas_call(bulk_kernel, out_shape=jax.ShapeDtypeStruct((nrows * block...  17.1 us
    pallas_call x1, Pallas kernels, local(): pl.pallas_call(second_kernel, out_shape=factor_shapes(n1), in_specs=[VMEM...  9.84 us
    ppermute x14, waiting for transfers between devices, exchange(): lax.ppermute(x, axis, [(i, i ^ k) for i in range(lax.axis_size(axis))])  9.25 us
  transfers between devices with their start and end apart: 14, of which 4 were waited for; matrix products, arithmetic and copies ran while one was open for 3% of the time, Pallas kernels for 40%

profile of v4, /device:TPU:21, one launch (start us, length us, event | category | flops | bytes accessed | tf_op | source)
XLA Modules:
  0.0 80.3 jit_solution(13206973361028140774)
XLA Ops:
  0.0 1.2 %collective-permute-start.2 = (bf16[2,64,512]{2,1,0:T(8,128)(2,1)}, bf16[2,64,512]{2,1,0:T(8,128)(2,1)S(1)}, u32[]{:S(2)}, u32[]{:S(2)}) collective-permute-start(bf16[2,64,512]{2,1,0:T(8,128)(2,1)} %bitcast.55), channel_id=1, source_target_pairs={{0,24},{8,16},{16,8},{24,0},{1,25},{9,17},{17,9},{25,1},{2,26},{10... | collective-permute-start | bytes 393224 | tf_op jit(solution)/shard_map/ppermute | solution.py:338
  1.2 1.2 %collective-permute-start.1 = (bf16[2,64,512]{2,1,0:T(8,128)(2,1)}, bf16[2,64,512]{2,1,0:T(8,128)(2,1)S(1)}, u32[]{:S(2)}, u32[]{:S(2)}) collective-permute-start(bf16[2,64,512]{2,1,0:T(8,128)(2,1)} %bitcast.56), channel_id=1, source_target_pairs={{0,16},{8,24},{16,0},{24,8},{1,17},{9,25},{17,1},{25,9},{2,18},{10... | collective-permute-start | bytes 393224 | tf_op jit(solution)/shard_map/ppermute | solution.py:338
  2.4 0.3 collective-permute-start
  2.7 0.7 copy.7
  3.3 0.1 pad_add_fusion.at_ref
  3.4 2.1 %collective-permute-done.2 = bf16[2,64,512]{2,1,0:T(8,128)(2,1)S(1)} collective-permute-done((bf16[2,64,512]{2,1,0:T(8,128)(2,1)}, bf16[2,64,512]{2,1,0:T(8,128)(2,1)S(1)}, u32[]{:S(2)}, u32[]{:S(2)}) %collective-permute-start.2) | collective-permute-done | bytes 131104 | tf_op jit(solution)/shard_map/ppermute | solution.py:338
  5.5 3.9 %collective-permute-done.1 = bf16[2,64,512]{2,1,0:T(8,128)(2,1)S(1)} collective-permute-done((bf16[2,64,512]{2,1,0:T(8,128)(2,1)}, bf16[2,64,512]{2,1,0:T(8,128)(2,1)S(1)}, u32[]{:S(2)}, u32[]{:S(2)}) %collective-permute-start.1) | collective-permute-done | bytes 131104 | tf_op jit(solution)/shard_map/ppermute | solution.py:338
  9.3 0.0 collective-permute-done
  9.3 0.9 %fusion.5 = (bf16[1,64,512]{2,1,0:T(8,128)(2,1)S(1)}, bf16[1,64,512]{2,1,0:T(8,128)(2,1)S(1)}) fusion(pred[]{:T(512)S(6)} %eq.26, pred[]{:T(512)S(6)} %eq.25, pred[]{:T(512)S(6)} %eq.24, bf16[2,64,512]{2,1,0:T(8,128)(2,1)S(1)} %collective-permute-done, bf16[2,64,512]{2,1,0:T(8,128)(2,1)S(1)} %collective-permute-done.1, ...), kind=kLoop, calls=%fused_computation.19 | loop fusion | flops 196608 | bytes 393222 | tf_op jit(solution)/shard_map/jit(_where)/select_n | solution.py:344
  10.2 0.2 collective-permute-start.5
  10.5 3.2 %collective-permute-start.4 = (bf16[2,64,512]{2,1,0:T(8,128)(2,1)S(1)}, bf16[2,64,512]{2,1,0:T(8,128)(2,1)S(1)}, u32[]{:S(2)}, u32[]{:S(2)}) collective-permute-start(bf16[2,64,512]{2,1,0:T(8,128)(2,1)S(1)} %pad_maximum_fusion.7), channel_id=1, source_target_pairs={{0,4},{1,5},{2,6},{3,7},{4,0},{5,1},{6,2},{7,3},{8,12},{9,13},{10,... | collective-permute-start | bytes 393224 | tf_op jit(solution)/shard_map/ppermute | solution.py:338
  13.7 0.0 collective-permute-start.3
  14.4 0.1 collective-permute-start.9
  14.5 1.4 %collective-permute-start.8 = (f32[2,512]{1,0:T(2,128)S(1)}, f32[2,512]{1,0:T(2,128)S(1)}, u32[]{:S(2)}, u32[]{:S(2)}) collective-permute-start(f32[2,512]{1,0:T(2,128)S(1)} %bitcast.51), channel_id=1, source_target_pairs={{0,16},{8,24},{16,0},{24,8},{1,17},{9,25},{17,1},{25,9},{2,18},{10... | collective-permute-start | bytes 12296 | tf_op jit(solution)/shard_map/ppermute | solution.py:338
  15.9 0.0 copy-start
  15.9 1.0 %pad_maximum_fusion.1 = bf16[4,2,64,512]{3,2,1,0:T(8,128)(2,1)S(1)} fusion(bf16[1,2,64,512]{3,2,1,0:T(8,128)(2,1)S(1)} %bitcast.61, bf16[1,2,64,512]{3,2,1,0:T(8,128)(2,1)S(1)} %bitcast.62, bf16[1,2,64,512]{3,2,1,0:T(8,128)(2,1)S(1)} %bitcast.63, bf16[1,2,64,512]{3,2,1,0:T(8,128)(2,1)} %bitcast.58), kind=kLoop, calls=%fused_computation.1 | loop fusion | flops 786432 | bytes 1048576 | tf_op jit(solution)/shard_map/stack | solution.py:367
  16.9 1.1 %collective-permute-done.5 = bf16[2,64,512]{2,1,0:T(8,128)(2,1)S(1)} collective-permute-done((bf16[2,64,512]{2,1,0:T(8,128)(2,1)S(1)}, bf16[2,64,512]{2,1,0:T(8,128)(2,1)S(1)}, u32[]{:S(2)}, u32[]{:S(2)}) %collective-permute-start.5) | collective-permute-done | bytes 131104 | tf_op jit(solution)/shard_map/ppermute | solution.py:338
  18.1 1.0 %collective-permute-start.7 = (f32[2,512]{1,0:T(2,128)S(1)}, f32[2,512]{1,0:T(2,128)S(1)}, u32[]{:S(2)}, u32[]{:S(2)}) collective-permute-start(f32[2,512]{1,0:T(2,128)S(1)} %bitcast.52), channel_id=1, source_target_pairs={{0,24},{8,16},{16,8},{24,0},{1,25},{9,17},{17,9},{25,1},{2,26},{10... | collective-permute-start | bytes 12296 | tf_op jit(solution)/shard_map/ppermute | solution.py:338
  19.1 2.2 %collective-permute-done.4 = bf16[2,64,512]{2,1,0:T(8,128)(2,1)S(1)} collective-permute-done((bf16[2,64,512]{2,1,0:T(8,128)(2,1)S(1)}, bf16[2,64,512]{2,1,0:T(8,128)(2,1)S(1)}, u32[]{:S(2)}, u32[]{:S(2)}) %collective-permute-start.4) | collective-permute-done | bytes 131104 | tf_op jit(solution)/shard_map/ppermute | solution.py:338
  21.3 0.0 collective-permute-done.3
  21.3 0.1 pad_maximum_fusion.2.mine_ref
  21.4 3.1 %collective-permute-start.6 = (bf16[4,2,64,512]{3,2,1,0:T(8,128)(2,1)S(1)}, bf16[4,2,64,512]{3,2,1,0:T(8,128)(2,1)S(1)}, u32[]{:S(2)}, u32[]{:S(2)}) collective-permute-start(bf16[4,2,64,512]{3,2,1,0:T(8,128)(2,1)S(1)} %pad_maximum_fusion.2.mine_ref), channel_id=1, source_target_pairs={{0,1},{1,0},{2,3},{3,2},{4,5},{5,4},{6,7},{7,6},{8,9},{9,8},{10,11... | collective-permute-start | bytes 1572872 | tf_op jit(solution)/shard_map/ppermute | solution.py:338
  24.5 0.0 collective-permute-done.9
  24.5 0.0 collective-permute-done.8
  24.5 0.0 collective-permute-done.7
  24.5 0.1 dynamic-slice_bitcast_fusion.1
  24.6 0.0 copy-done
  24.6 0.1 fusion.3
  24.7 0.1 collective-permute-start.12
  24.8 2.5 %collective-permute-start.10 = (bf16[4,64,512]{2,1,0:T(8,128)(2,1)S(1)}, bf16[4,64,512]{2,1,0:T(8,128)(2,1)S(1)}, u32[]{:S(2)}, u32[]{:S(2)}) collective-permute-start(bf16[4,64,512]{2,1,0:T(8,128)(2,1)S(1)} %get-tuple-element.50), channel_id=1, source_target_pairs={{0,2},{1,3},{2,0},{3,1},{4,6},{5,7},{6,4},{7,5},{8,10},{9,11},{10,... | collective-permute-start | bytes 786440 | tf_op jit(solution)/shard_map/ppermute | solution.py:338
  27.3 1.0 %collective-permute-start.11 = (bf16[4,64,512]{2,1,0:T(8,128)(2,1)S(1)}, bf16[4,64,512]{2,1,0:T(8,128)(2,1)S(1)}, u32[]{:S(2)}, u32[]{:S(2)}) collective-permute-start(bf16[4,64,512]{2,1,0:T(8,128)(2,1)S(1)} %get-tuple-element.51), channel_id=1, source_target_pairs={{0,4},{1,5},{2,6},{3,7},{4,0},{5,1},{6,2},{7,3},{8,12},{9,13},{10,... | collective-permute-start | bytes 786440 | tf_op jit(solution)/shard_map/ppermute | solution.py:338
  28.4 0.0 collective-permute-done.6.other_ref
  28.4 22.0 %first.1 = (bf16[1024,512]{1,0:T(8,128)(2,1)S(1)}, f32[640,1024]{1,0:T(8,128)S(1)}, bf16[640,1024]{1,0:T(8,128)(2,1)S(1)}, bf16[640,1024]{1,0:T(8,128)(2,1)S(1)}, f32[384,1024]{1,0:T(8,128)S(1)}) custom-call(s32[4]{0:T(128)S(1)} %pad_add_fusion.at_ref, f32[1]{0:T(128)S(6)} %copy.8.amp_ref, bf16[4,2,64,512]{3,2,1,0:T(8,128)(2,1)S(1)} %pad_maximum_fusion.2.mine_ref, ...), custom_call_target="tpu_custom_call" | custom-call | flops 20000000000 | bytes 8000000 | tf_op jit(solution)/shard_map/first/pallas_call | solution.py:391
  50.4 0.0 collective-permute-done.12.refs_11_
  50.4 0.0 collective-permute-done.10.refs_9_
  50.4 0.0 collective-permute-done.11.refs_10_
  50.5 0.1 pad_maximum_fusion
  50.6 2.8 %collective-permute-start.13 = (bf16[4,3,64,512]{3,2,1,0:T(8,128)(2,1)S(1)}, bf16[4,3,64,512]{3,2,1,0:T(8,128)(2,1)S(1)}, u32[]{:S(2)}, u32[]{:S(2)}) collective-permute-start(bf16[4,3,64,512]{3,2,1,0:T(8,128)(2,1)S(1)} %pad_maximum_fusion), channel_id=1, source_target_pairs={{0,1},{1,0},{2,3},{3,2},{4,5},{5,4},{6,7},{7,6},{8,9},{9,8},{10,11... | collective-permute-start | bytes 2359304 | tf_op jit(solution)/shard_map/ppermute | solution.py:338
  53.3 9.8 %second.1 = (f32[384,1024]{1,0:T(8,128)S(1)}, bf16[384,1024]{1,0:T(8,128)(2,1)S(1)}, bf16[384,1024]{1,0:T(8,128)(2,1)S(1)}) custom-call(f32[384,1024]{1,0:T(8,128)S(1)} %get-tuple-element.31.rest_ref), custom_call_target="tpu_custom_call" | custom-call | flops 20000000000 | bytes 8000000 | tf_op jit(solution)/shard_map/second/pallas_call | solution.py:405
  63.2 0.0 collective-permute-done.13.refs_12_
  63.2 17.1 %bulk.1 = f32[4096,128]{1,0:T(8,128)} custom-call(s32[4]{0:T(128)S(1)} %pad_add_fusion.at_ref, f32[1]{0:T(128)S(6)} %copy.8.amp_ref, bf16[1024,512]{1,0:T(8,128)(2,1)S(1)} %get-tuple-element.25.refs_0_, f32[640,1024]{1,0:T(8,128)S(1)} %get-tuple-element.26.refs_1_, bf16[640,1024]{1,0:T(8,128)(2,1)S(1)} %get-tuple-element.27.refs_2_, ...), custom_call_target="tpu_custom_call" | custom-call | flops 20000000000 | bytes 8000000 | tf_op jit(solution)/shard_map/bulk/pallas_call | solution.py:417
  (5 shorter events, 0.1 us)
Async XLA Ops:
  0.0 5.5 %collective-permute-start.2 = (bf16[2,64,512]{2,1,0:T(8,128)(2,1)}, bf16[2,64,512]{2,1,0:T(8,128)(2,1)S(1)}, u32[]{:S(2)}, u32[]{:S(2)}) collective-permute-start(bf16[2,64,512]{2,1,0:T(8,128)(2,1)} %bitcast.55), channel_id=1, source_target_pairs={{0,24},{8,16},{16,8},{24,0},{1,25},{9,17},{17,9},{25,1},{2,26},{10... | collective-permute-start | bytes 393224 | tf_op jit(solution)/shard_map/ppermute | solution.py:338
  1.2 8.2 %collective-permute-start.1 = (bf16[2,64,512]{2,1,0:T(8,128)(2,1)}, bf16[2,64,512]{2,1,0:T(8,128)(2,1)S(1)}, u32[]{:S(2)}, u32[]{:S(2)}) collective-permute-start(bf16[2,64,512]{2,1,0:T(8,128)(2,1)} %bitcast.56), channel_id=1, source_target_pairs={{0,16},{8,24},{16,0},{24,8},{1,17},{9,25},{17,1},{25,9},{2,18},{10... | collective-permute-start | bytes 393224 | tf_op jit(solution)/shard_map/ppermute | solution.py:338
  2.4 6.9 %collective-permute-start = (bf16[2,64,512]{2,1,0:T(8,128)(2,1)}, bf16[2,64,512]{2,1,0:T(8,128)(2,1)S(1)}, u32[]{:S(2)}, u32[]{:S(2)}) collective-permute-start(bf16[2,64,512]{2,1,0:T(8,128)(2,1)} %bitcast.57), channel_id=1, source_target_pairs={{0,8},{8,0},{16,24},{24,16},{1,9},{9,1},{17,25},{25,17},{2,10},{10... | collective-permute-start | bytes 393224 | tf_op jit(solution)/shard_map/ppermute | solution.py:338
  10.2 7.8 %collective-permute-start.5 = (bf16[2,64,512]{2,1,0:T(8,128)(2,1)S(1)}, bf16[2,64,512]{2,1,0:T(8,128)(2,1)S(1)}, u32[]{:S(2)}, u32[]{:S(2)}) collective-permute-start(bf16[2,64,512]{2,1,0:T(8,128)(2,1)S(1)} %pad_maximum_fusion.7), channel_id=1, source_target_pairs={{0,6},{1,7},{2,4},{3,5},{4,2},{5,3},{6,0},{7,1},{8,14},{9,15},{10,... | collective-permute-start | bytes 393224 | tf_op jit(solution)/shard_map/ppermute | solution.py:338
  10.5 10.8 %collective-permute-start.4 = (bf16[2,64,512]{2,1,0:T(8,128)(2,1)S(1)}, bf16[2,64,512]{2,1,0:T(8,128)(2,1)S(1)}, u32[]{:S(2)}, u32[]{:S(2)}) collective-permute-start(bf16[2,64,512]{2,1,0:T(8,128)(2,1)S(1)} %pad_maximum_fusion.7), channel_id=1, source_target_pairs={{0,4},{1,5},{2,6},{3,7},{4,0},{5,1},{6,2},{7,3},{8,12},{9,13},{10,... | collective-permute-start | bytes 393224 | tf_op jit(solution)/shard_map/ppermute | solution.py:338
  13.7 7.6 %collective-permute-start.3 = (bf16[2,64,512]{2,1,0:T(8,128)(2,1)S(1)}, bf16[2,64,512]{2,1,0:T(8,128)(2,1)S(1)}, u32[]{:S(2)}, u32[]{:S(2)}) collective-permute-start(bf16[2,64,512]{2,1,0:T(8,128)(2,1)S(1)} %pad_maximum_fusion.7), channel_id=1, source_target_pairs={{0,2},{1,3},{2,0},{3,1},{4,6},{5,7},{6,4},{7,5},{8,10},{9,11},{10,... | collective-permute-start | bytes 393224 | tf_op jit(solution)/shard_map/ppermute | solution.py:338
  14.4 10.1 %collective-permute-start.9 = (f32[2,512]{1,0:T(2,128)S(1)}, f32[2,512]{1,0:T(2,128)S(1)}, u32[]{:S(2)}, u32[]{:S(2)}) collective-permute-start(f32[2,512]{1,0:T(2,128)S(1)} %bitcast.50), channel_id=1, source_target_pairs={{0,8},{8,0},{16,24},{24,16},{1,9},{9,1},{17,25},{25,17},{2,10},{10... | collective-permute-start | bytes 12296 | tf_op jit(solution)/shard_map/ppermute | solution.py:338
  14.5 10.0 %collective-permute-start.8 = (f32[2,512]{1,0:T(2,128)S(1)}, f32[2,512]{1,0:T(2,128)S(1)}, u32[]{:S(2)}, u32[]{:S(2)}) collective-permute-start(f32[2,512]{1,0:T(2,128)S(1)} %bitcast.51), channel_id=1, source_target_pairs={{0,16},{8,24},{16,0},{24,8},{1,17},{9,25},{17,1},{25,9},{2,18},{10... | collective-permute-start | bytes 12296 | tf_op jit(solution)/shard_map/ppermute | solution.py:338
  15.9 8.7 %copy-start = (bf16[2,1,64,512]{3,2,1,0:T(8,128)(2,1)S(1)}, bf16[2,1,64,512]{3,2,1,0:T(8,128)(2,1)}, u32[]{:S(2)}) copy-start(bf16[2,1,64,512]{3,2,1,0:T(8,128)(2,1)} %param.3) | copy-start | bytes 393220
  18.1 6.4 %collective-permute-start.7 = (f32[2,512]{1,0:T(2,128)S(1)}, f32[2,512]{1,0:T(2,128)S(1)}, u32[]{:S(2)}, u32[]{:S(2)}) collective-permute-start(f32[2,512]{1,0:T(2,128)S(1)} %bitcast.52), channel_id=1, source_target_pairs={{0,24},{8,16},{16,8},{24,0},{1,25},{9,17},{17,9},{25,1},{2,26},{10... | collective-permute-start | bytes 12296 | tf_op jit(solution)/shard_map/ppermute | solution.py:338
  21.4 7.0 %collective-permute-start.6 = (bf16[4,2,64,512]{3,2,1,0:T(8,128)(2,1)S(1)}, bf16[4,2,64,512]{3,2,1,0:T(8,128)(2,1)S(1)}, u32[]{:S(2)}, u32[]{:S(2)}) collective-permute-start(bf16[4,2,64,512]{3,2,1,0:T(8,128)(2,1)S(1)} %pad_maximum_fusion.2.mine_ref), channel_id=1, source_target_pairs={{0,1},{1,0},{2,3},{3,2},{4,5},{5,4},{6,7},{7,6},{8,9},{9,8},{10,11... | collective-permute-start | bytes 1572872 | tf_op jit(solution)/shard_map/ppermute | solution.py:338
  24.7 25.7 %collective-permute-start.12 = (bf16[4,64,512]{2,1,0:T(8,128)(2,1)S(1)}, bf16[4,64,512]{2,1,0:T(8,128)(2,1)S(1)}, u32[]{:S(2)}, u32[]{:S(2)}) collective-permute-start(bf16[4,64,512]{2,1,0:T(8,128)(2,1)S(1)} %get-tuple-element.49), channel_id=1, source_target_pairs={{0,6},{1,7},{2,4},{3,5},{4,2},{5,3},{6,0},{7,1},{8,14},{9,15},{10,... | collective-permute-start | bytes 786440 | tf_op jit(solution)/shard_map/ppermute | solution.py:338
  24.8 25.6 %collective-permute-start.10 = (bf16[4,64,512]{2,1,0:T(8,128)(2,1)S(1)}, bf16[4,64,512]{2,1,0:T(8,128)(2,1)S(1)}, u32[]{:S(2)}, u32[]{:S(2)}) collective-permute-start(bf16[4,64,512]{2,1,0:T(8,128)(2,1)S(1)} %get-tuple-element.50), channel_id=1, source_target_pairs={{0,2},{1,3},{2,0},{3,1},{4,6},{5,7},{6,4},{7,5},{8,10},{9,11},{10,... | collective-permute-start | bytes 786440 | tf_op jit(solution)/shard_map/ppermute | solution.py:338
  27.3 23.1 %collective-permute-start.11 = (bf16[4,64,512]{2,1,0:T(8,128)(2,1)S(1)}, bf16[4,64,512]{2,1,0:T(8,128)(2,1)S(1)}, u32[]{:S(2)}, u32[]{:S(2)}) collective-permute-start(bf16[4,64,512]{2,1,0:T(8,128)(2,1)S(1)} %get-tuple-element.51), channel_id=1, source_target_pairs={{0,4},{1,5},{2,6},{3,7},{4,0},{5,1},{6,2},{7,3},{8,12},{9,13},{10,... | collective-permute-start | bytes 786440 | tf_op jit(solution)/shard_map/ppermute | solution.py:338
  50.6 12.6 %collective-permute-start.13 = (bf16[4,3,64,512]{3,2,1,0:T(8,128)(2,1)S(1)}, bf16[4,3,64,512]{3,2,1,0:T(8,128)(2,1)S(1)}, u32[]{:S(2)}, u32[]{:S(2)}) collective-permute-start(bf16[4,3,64,512]{3,2,1,0:T(8,128)(2,1)S(1)} %pad_maximum_fusion), channel_id=1, source_target_pairs={{0,1},{1,0},{2,3},{3,2},{4,5},{5,4},{6,7},{7,6},{8,9},{9,8},{10,11... | collective-permute-start | bytes 2359304 | tf_op jit(solution)/shard_map/ppermute | solution.py:338

commit v5 on v4

--- a/solution.py
+++ b/solution.py
@@ -13,6 +13,7 @@
 GRANT = 30 << 20
 UPDATE_ROWS = 256
 FIRST = 5
+GROUP = 4
 f32 = jnp.float32
 bf16 = jnp.bfloat16
 TRANS_B = (((1,), (1,)), ((), ()))
@@ -59,17 +60,20 @@
         inv = 1.0 / pivot
         inverses.append(inv)
         pivots = pivot if j == 0 else jnp.where(sub == j, pivot, pivots)
-        below = jnp.where(sub > j, cols[j], 0.0)
         for k in range(j + 1, 8):
             entry = spread(cols[k][j : j + 1, :])
-            cols[k] = cols[k] - (below * entry) * inv
             ratio[j, k] = entry * inv
+            cols[k] = cols[k] - ((cols[j] * entry) * inv if k == j + 1 else cols[j] * ratio[j, k])
         row = spread(rows[j : j + 1, :]) * inv
         row = jnp.where(lane == 8 * t + j, 1.0 + inv, row)
         scaled.append(row)
         if j < 7:
-            rows = rows - below * row
+            rows = rows - jnp.where(sub > j, cols[j], 0.0) * row
     return rows, lax.rsqrt(pivots), scaled, ratio, inverses
+
+
+def lane_columns(tile, first):
+    return [spread(tile[:, first + k : first + k + 1]) for k in range(8)]
 
 
 def factor_block(tiles, store_u, store_l):
@@ -77,33 +81,46 @@
     n = len(tiles)
     lane = lax.broadcasted_iota(jnp.int32, (8, NB), 1)
     sub = lax.broadcasted_iota(jnp.int32, (8, NB), 0)
-    cols = [spread(tiles[0][:, k : k + 1]) for k in range(8)]
-    for t in range(n):
-        last = t + 1 == n
-        if not last:
-            near = [spread(tiles[t + 1][:, 8 * t + k : 8 * t + k + 1]) for k in range(8)]
-            ahead = [spread(tiles[t + 1][:, 8 * t + 8 + k : 8 * t + 9 + k]) for k in range(8)]
-        far = {i: [spread(tiles[i][:, 8 * t + k : 8 * t + k + 1]) for k in range(8)] for i in range(t + 2, n)}
-        rows, root, scaled, ratio, inverses = factor_tile(t, tiles[t], cols, lane, sub)
-        if not last:
-            for j in range(8):
-                part = near[j] * inverses[j]
-                for k in range(j + 1, 8):
-                    near[k] = near[k] - near[j] * ratio[j, k]
-                for k in range(8):
-                    ahead[k] = ahead[k] - near[j] * spread(part[k : k + 1, :])
-                tiles[t + 1] = tiles[t + 1] - near[j] * scaled[j]
-            cols = ahead
-        back = list(scaled)
-        for j in range(6, -1, -1):
-            for k in range(7, j, -1):
-                back[j] = back[j] - ratio[j, k] * back[k]
-        for i in range(t + 2, n):
-            tiles[i] = tiles[i] - tree_sum([far[i][j] * back[j] for j in range(8)])
-        final = rows * root
-        diff = lane - sub - 8 * t
-        store_u(t, jnp.where(diff >= 0, final, 0.0))
-        store_l(t, jnp.where(diff < 0, final, jnp.where(diff == 0, root, 0.0)))
+    cols = lane_columns(tiles[0], 0)
+    for g in range(0, n, GROUP):
+        end = g + GROUP
+        window = min(n, end + 1)
+        left, right = [], []
+        for t in range(g, end):
+            last = t + 1 == window
+            if not last:
+                near = lane_columns(tiles[t + 1], 8 * t)
+                ahead = lane_columns(tiles[t + 1], 8 * t + 8)
+            far = {i: lane_columns(tiles[i], 8 * t) for i in range(t + 2, window)}
+            rows, root, scaled, ratio, inverses = factor_tile(t, tiles[t], cols, lane, sub)
+            if not last:
+                for j in range(8):
+                    part = near[j] * inverses[j]
+                    for k in range(j + 1, 8):
+                        near[k] = near[k] - near[j] * ratio[j, k]
+                    for k in range(8):
+                        ahead[k] = ahead[k] - near[j] * spread(part[k : k + 1, :])
+                    tiles[t + 1] = tiles[t + 1] - near[j] * scaled[j]
+                cols = ahead
+            if far:
+                back = list(scaled)
+                for j in range(6, -1, -1):
+                    for k in range(7, j, -1):
+                        back[j] = back[j] - ratio[j, k] * back[k]
+                for i in far:
+                    tiles[i] = tiles[i] - tree_sum([far[i][j] * back[j] for j in range(8)])
+            final = rows * root
+            diff = lane - sub - 8 * t
+            lower = jnp.where(diff < 0, final, jnp.where(diff == 0, root, 0.0))
+            store_u(t, jnp.where(diff >= 0, final, 0.0))
+            store_l(t, lower)
+            left.append(final)
+            right.append(jnp.where(lane >= 8 * end, final, lower))
+        if window < n:
+            change = dot_tn(*split(jnp.concatenate(left, 0)), *split(jnp.concatenate(right, 0)))
+            keep = (lane < 8 * g) | (lane >= 8 * end)
+            for i in range(window, n):
+                tiles[i] = jnp.where(keep, tiles[i], 0.0) - change[8 * i : 8 * i + 8]
 
 
 def half_norm_rows(x):
@@ -360,11 +377,9 @@
     lead = jnp.stack([choose(row_at ^ s, [p[0] for p in plane]) for s in range(PANELS)])
     noise_rows, lead = lax.optimization_barrier((noise_rows, lead))
     near = [lead] + [exchange(lead, "col", k) for k in range(2, col_n, 2)]
+    everything, near[1] = lax.optimization_barrier((jnp.stack(plane), near[1]))
     noises = [noise_rows] + [exchange(noise_rows, "row", k) for k in range(1, row_n)]
     lead_noise = jnp.stack([choose(row_at ^ s, [p[0] for p in noises]) for s in range(PANELS)])
-    near = jnp.stack(near)
-    other = exchange(near, "col", 1)
-    everything, near = lax.optimization_barrier((jnp.stack(plane), near))
     core = col_at & 1
 
     def parcel(to):
@@ -377,6 +392,8 @@
         return jnp.concatenate(out, 0)
 
     parcels = [parcel(col_at)] + [exchange(parcel(col_at ^ k), "col", k) for k in range(2, col_n, 2)]
+    near = jnp.stack(near)
+    other = exchange(near, "col", 1)
     at = jnp.stack([row_at, col_at, jnp.int32(row_n), jnp.int32(col_n)])
     first = FIRST * n // NB // 8 * NB
     n1 = n - first
@@ -397,7 +414,7 @@
         out_specs=[VMEM] * 5,
         scratch_shapes=[pltpu.VMEM((n, n), f32), square],
         compiler_params=params,
-        cost_estimate=cost,
+        cost_estimate=pl.CostEstimate(flops=1_000_000, bytes_accessed=1_000_000, transcendentals=0),
         name="first",
     )(at, amplitude, near, other, lead_noise)
     parcels, rest = lax.optimization_barrier((parcels, rest))

time: 80.6 us -> 75.2 us (0.933)
  the two profiles are of different devices: /device:TPU:21 before, /device:TPU:31 now
where the time goes in v5:
time: 75.2 us; the launch traced here: 75 us
  Pallas kernels  46 us (61%)
  starting transfers between devices  14.9 us (20%)
  waiting for transfers between devices  10.1 us (13%)
  other arithmetic  2.27 us (3%)
  between operations  0.86 us (1%)
  local copies, waits for them, and re-layouts  0.78 us (1%)
    pallas_call x1, Pallas kernels, local(): pl.pallas_call(first_kernel, out_shape=[jax.ShapeDtypeStruct((n, width),...  20.1 us
    pallas_call x1, Pallas kernels, local(): pl.pallas_call(bulk_kernel, out_shape=jax.ShapeDtypeStruct((nrows * block...  17.2 us
    ppermute x14, starting transfers between devices, exchange(): lax.ppermute(x, axis, [(i, i ^ k) for i in range(lax.axis_size(axis))])  14.9 us
    ppermute x14, waiting for transfers between devices, exchange(): lax.ppermute(x, axis, [(i, i ^ k) for i in range(lax.axis_size(axis))])  10.1 us
    pallas_call x1, Pallas kernels, local(): pl.pallas_call(second_kernel, out_shape=factor_shapes(n1), in_specs=[VMEM...  8.73 us
  transfers between devices with their start and end apart: 14, of which 4 were waited for; matrix products, arithmetic and copies ran while one was open for 3% of the time, Pallas kernels for 38%

profile of v5, /device:TPU:31, one launch (start us, length us, event | category | flops | bytes accessed | tf_op | source)
XLA Modules:
  0.0 75.0 jit_solution(14737825746722608946)
XLA Ops:
  0.0 0.3 collective-permute-start.2
  0.3 0.2 collective-permute-start.1
  0.5 2.2 %collective-permute-start = (bf16[2,64,512]{2,1,0:T(8,128)(2,1)}, bf16[2,64,512]{2,1,0:T(8,128)(2,1)S(1)}, u32[]{:S(2)}, u32[]{:S(2)}) collective-permute-start(bf16[2,64,512]{2,1,0:T(8,128)(2,1)} %bitcast.57), channel_id=1, source_target_pairs={{0,24},{8,16},{16,8},{24,0},{1,25},{9,17},{17,9},{25,1},{2,26},{10... | collective-permute-start | bytes 393224 | tf_op jit(solution)/shard_map/ppermute | solution.py:355
  2.7 0.7 copy.7
  3.3 0.1 pad_add_fusion.at_ref
  3.4 1.2 %collective-permute-done.2 = bf16[2,64,512]{2,1,0:T(8,128)(2,1)S(1)} collective-permute-done((bf16[2,64,512]{2,1,0:T(8,128)(2,1)}, bf16[2,64,512]{2,1,0:T(8,128)(2,1)S(1)}, u32[]{:S(2)}, u32[]{:S(2)}) %collective-permute-start.2) | collective-permute-done | bytes 131104 | tf_op jit(solution)/shard_map/ppermute | solution.py:355
  4.6 0.1 collective-permute-done.1
  4.6 2.7 %collective-permute-done = bf16[2,64,512]{2,1,0:T(8,128)(2,1)S(1)} collective-permute-done((bf16[2,64,512]{2,1,0:T(8,128)(2,1)}, bf16[2,64,512]{2,1,0:T(8,128)(2,1)S(1)}, u32[]{:S(2)}, u32[]{:S(2)}) %collective-permute-start) | collective-permute-done | bytes 131104 | tf_op jit(solution)/shard_map/ppermute | solution.py:355
  7.3 0.9 %fusion.5 = (bf16[1,64,512]{2,1,0:T(8,128)(2,1)S(1)}, bf16[1,64,512]{2,1,0:T(8,128)(2,1)S(1)}) fusion(pred[]{:T(512)S(6)} %eq.26, pred[]{:T(512)S(6)} %eq.25, pred[]{:T(512)S(6)} %eq.24, bf16[2,64,512]{2,1,0:T(8,128)(2,1)S(1)} %collective-permute-done.2, bf16[2,64,512]{2,1,0:T(8,128)(2,1)S(1)} %collective-permute-done.1, ...), kind=kLoop, calls=%fused_computation.19 | loop fusion | flops 196608 | bytes 393222 | tf_op jit(solution)/shard_map/jit(_where)/select_n | solution.py:361
  8.2 0.2 collective-permute-start.3
  8.5 1.1 %collective-permute-start.5 = (bf16[2,64,512]{2,1,0:T(8,128)(2,1)S(1)}, bf16[2,64,512]{2,1,0:T(8,128)(2,1)S(1)}, u32[]{:S(2)}, u32[]{:S(2)}) collective-permute-start(bf16[2,64,512]{2,1,0:T(8,128)(2,1)S(1)} %pad_maximum_fusion.7), channel_id=1, source_target_pairs={{0,6},{1,7},{2,4},{3,5},{4,2},{5,3},{6,0},{7,1},{8,14},{9,15},{10,... | collective-permute-start | bytes 393224 | tf_op jit(solution)/shard_map/ppermute | solution.py:355
  9.5 1.4 %collective-permute-start.4 = (bf16[2,64,512]{2,1,0:T(8,128)(2,1)S(1)}, bf16[2,64,512]{2,1,0:T(8,128)(2,1)S(1)}, u32[]{:S(2)}, u32[]{:S(2)}) collective-permute-start(bf16[2,64,512]{2,1,0:T(8,128)(2,1)S(1)} %pad_maximum_fusion.7), channel_id=1, source_target_pairs={{0,4},{1,5},{2,6},{3,7},{4,0},{5,1},{6,2},{7,3},{8,12},{9,13},{10,... | collective-permute-start | bytes 393224 | tf_op jit(solution)/shard_map/ppermute | solution.py:355
  11.6 0.2 collective-permute-start.9
  11.8 1.2 %collective-permute-start.8 = (f32[2,512]{1,0:T(2,128)S(1)}, f32[2,512]{1,0:T(2,128)S(1)}, u32[]{:S(2)}, u32[]{:S(2)}) collective-permute-start(f32[2,512]{1,0:T(2,128)S(1)} %bitcast.51), channel_id=1, source_target_pairs={{0,16},{8,24},{16,0},{24,8},{1,17},{9,25},{17,1},{25,9},{2,18},{10... | collective-permute-start | bytes 12296 | tf_op jit(solution)/shard_map/ppermute | solution.py:355
  13.1 0.0 copy-start
  13.1 1.0 %pad_maximum_fusion.1 = bf16[4,2,64,512]{3,2,1,0:T(8,128)(2,1)S(1)} fusion(bf16[1,2,64,512]{3,2,1,0:T(8,128)(2,1)S(1)} %bitcast.63, bf16[1,2,64,512]{3,2,1,0:T(8,128)(2,1)S(1)} %bitcast.62, bf16[1,2,64,512]{3,2,1,0:T(8,128)(2,1)S(1)} %bitcast.61, bf16[1,2,64,512]{3,2,1,0:T(8,128)(2,1)} %bitcast.58), kind=kLoop, calls=%fused_computation.1 | loop fusion | flops 786432 | bytes 1048576 | tf_op jit(solution)/shard_map/stack | solution.py:380
  14.1 0.0 collective-permute-done.3
  14.1 1.4 %collective-permute-start.7 = (f32[2,512]{1,0:T(2,128)S(1)}, f32[2,512]{1,0:T(2,128)S(1)}, u32[]{:S(2)}, u32[]{:S(2)}) collective-permute-start(f32[2,512]{1,0:T(2,128)S(1)} %bitcast.52), channel_id=1, source_target_pairs={{0,24},{8,16},{16,8},{24,0},{1,25},{9,17},{17,9},{25,1},{2,26},{10... | collective-permute-start | bytes 12296 | tf_op jit(solution)/shard_map/ppermute | solution.py:355
  15.5 0.0 collective-permute-done.5
  15.5 6.2 %collective-permute-done.4 = bf16[2,64,512]{2,1,0:T(8,128)(2,1)S(1)} collective-permute-done((bf16[2,64,512]{2,1,0:T(8,128)(2,1)S(1)}, bf16[2,64,512]{2,1,0:T(8,128)(2,1)S(1)}, u32[]{:S(2)}, u32[]{:S(2)}) %collective-permute-start.4) | collective-permute-done | bytes 131104 | tf_op jit(solution)/shard_map/ppermute | solution.py:355
  21.7 0.1 pad_maximum_fusion.2.mine_ref
  21.7 2.2 %collective-permute-start.6 = (bf16[4,2,64,512]{3,2,1,0:T(8,128)(2,1)S(1)}, bf16[4,2,64,512]{3,2,1,0:T(8,128)(2,1)S(1)}, u32[]{:S(2)}, u32[]{:S(2)}) collective-permute-start(bf16[4,2,64,512]{3,2,1,0:T(8,128)(2,1)S(1)} %pad_maximum_fusion.2.mine_ref), channel_id=1, source_target_pairs={{0,1},{1,0},{2,3},{3,2},{4,5},{5,4},{6,7},{7,6},{8,9},{9,8},{10,11... | collective-permute-start | bytes 1572872 | tf_op jit(solution)/shard_map/ppermute | solution.py:355
  24.0 0.0 copy-done
  24.0 0.1 fusion.3
  24.1 1.0 %collective-permute-start.12 = (bf16[4,64,512]{2,1,0:T(8,128)(2,1)S(1)}, bf16[4,64,512]{2,1,0:T(8,128)(2,1)S(1)}, u32[]{:S(2)}, u32[]{:S(2)}) collective-permute-start(bf16[4,64,512]{2,1,0:T(8,128)(2,1)S(1)} %get-tuple-element.49), channel_id=1, source_target_pairs={{0,6},{1,7},{2,4},{3,5},{4,2},{5,3},{6,0},{7,1},{8,14},{9,15},{10,... | collective-permute-start | bytes 786440 | tf_op jit(solution)/shard_map/ppermute | solution.py:355
  25.1 0.0 collective-permute-done.9
  25.1 0.0 collective-permute-start.10
  25.1 0.0 collective-permute-done.8
  25.1 2.6 %collective-permute-start.11 = (bf16[4,64,512]{2,1,0:T(8,128)(2,1)S(1)}, bf16[4,64,512]{2,1,0:T(8,128)(2,1)S(1)}, u32[]{:S(2)}, u32[]{:S(2)}) collective-permute-start(bf16[4,64,512]{2,1,0:T(8,128)(2,1)S(1)} %get-tuple-element.51), channel_id=1, source_target_pairs={{0,4},{1,5},{2,6},{3,7},{4,0},{5,1},{6,2},{7,3},{8,12},{9,13},{10,... | collective-permute-start | bytes 786440 | tf_op jit(solution)/shard_map/ppermute | solution.py:355
  27.7 0.0 collective-permute-done.7
  27.7 0.0 collective-permute-done.6.other_ref
  27.7 20.1 %first.1 = (bf16[1024,512]{1,0:T(8,128)(2,1)S(1)}, f32[640,1024]{1,0:T(8,128)S(1)}, bf16[640,1024]{1,0:T(8,128)(2,1)S(1)}, bf16[640,1024]{1,0:T(8,128)(2,1)S(1)}, f32[384,1024]{1,0:T(8,128)S(1)}) custom-call(s32[4]{0:T(128)S(1)} %pad_add_fusion.at_ref, f32[1]{0:T(128)S(6)} %copy.8.amp_ref, bf16[4,2,64,512]{3,2,1,0:T(8,128)(2,1)S(1)} %pad_maximum_fusion.2.mine_ref, ...), custom_call_target="tpu_custom_call" | custom-call | flops 1000000 | bytes 1000000 | tf_op jit(solution)/shard_map/first/pallas_call | solution.py:408
  47.9 0.0 collective-permute-done.12.refs_11_
  47.9 0.0 collective-permute-done.10.refs_9_
  47.9 0.0 collective-permute-done.11.refs_10_
  48.0 0.1 pad_maximum_fusion
  48.1 0.9 %collective-permute-start.13 = (bf16[4,3,64,512]{3,2,1,0:T(8,128)(2,1)S(1)}, bf16[4,3,64,512]{3,2,1,0:T(8,128)(2,1)S(1)}, u32[]{:S(2)}, u32[]{:S(2)}) collective-permute-start(bf16[4,3,64,512]{3,2,1,0:T(8,128)(2,1)S(1)} %pad_maximum_fusion), channel_id=1, source_target_pairs={{0,1},{1,0},{2,3},{3,2},{4,5},{5,4},{6,7},{7,6},{8,9},{9,8},{10,11... | collective-permute-start | bytes 2359304 | tf_op jit(solution)/shard_map/ppermute | solution.py:355
  49.0 8.7 %second.1 = (f32[384,1024]{1,0:T(8,128)S(1)}, bf16[384,1024]{1,0:T(8,128)(2,1)S(1)}, bf16[384,1024]{1,0:T(8,128)(2,1)S(1)}) custom-call(f32[384,1024]{1,0:T(8,128)S(1)} %get-tuple-element.31.rest_ref), custom_call_target="tpu_custom_call" | custom-call | flops 20000000000 | bytes 8000000 | tf_op jit(solution)/shard_map/second/pallas_call | solution.py:422
  57.8 0.0 collective-permute-done.13.refs_12_
  57.8 17.2 %bulk.1 = f32[4096,128]{1,0:T(8,128)} custom-call(s32[4]{0:T(128)S(1)} %pad_add_fusion.at_ref, f32[1]{0:T(128)S(6)} %copy.8.amp_ref, bf16[1024,512]{1,0:T(8,128)(2,1)S(1)} %get-tuple-element.25.refs_0_, f32[640,1024]{1,0:T(8,128)S(1)} %get-tuple-element.26.refs_1_, bf16[640,1024]{1,0:T(8,128)(2,1)S(1)} %get-tuple-element.27.refs_2_, ...), custom_call_target="tpu_custom_call" | custom-call | flops 20000000000 | bytes 8000000 | tf_op jit(solution)/shard_map/bulk/pallas_call | solution.py:434
  (6 shorter events, 0.1 us)
Async XLA Ops:
  0.0 4.6 %collective-permute-start.2 = (bf16[2,64,512]{2,1,0:T(8,128)(2,1)}, bf16[2,64,512]{2,1,0:T(8,128)(2,1)S(1)}, u32[]{:S(2)}, u32[]{:S(2)}) collective-permute-start(bf16[2,64,512]{2,1,0:T(8,128)(2,1)} %bitcast.55), channel_id=1, source_target_pairs={{0,8},{8,0},{16,24},{24,16},{1,9},{9,1},{17,25},{25,17},{2,10},{10... | collective-permute-start | bytes 393224 | tf_op jit(solution)/shard_map/ppermute | solution.py:355
  0.3 4.4 %collective-permute-start.1 = (bf16[2,64,512]{2,1,0:T(8,128)(2,1)}, bf16[2,64,512]{2,1,0:T(8,128)(2,1)S(1)}, u32[]{:S(2)}, u32[]{:S(2)}) collective-permute-start(bf16[2,64,512]{2,1,0:T(8,128)(2,1)} %bitcast.56), channel_id=1, source_target_pairs={{0,16},{8,24},{16,0},{24,8},{1,17},{9,25},{17,1},{25,9},{2,18},{10... | collective-permute-start | bytes 393224 | tf_op jit(solution)/shard_map/ppermute | solution.py:355
  0.5 6.8 %collective-permute-start = (bf16[2,64,512]{2,1,0:T(8,128)(2,1)}, bf16[2,64,512]{2,1,0:T(8,128)(2,1)S(1)}, u32[]{:S(2)}, u32[]{:S(2)}) collective-permute-start(bf16[2,64,512]{2,1,0:T(8,128)(2,1)} %bitcast.57), channel_id=1, source_target_pairs={{0,24},{8,16},{16,8},{24,0},{1,25},{9,17},{17,9},{25,1},{2,26},{10... | collective-permute-start | bytes 393224 | tf_op jit(solution)/shard_map/ppermute | solution.py:355
  8.2 5.9 %collective-permute-start.3 = (bf16[2,64,512]{2,1,0:T(8,128)(2,1)S(1)}, bf16[2,64,512]{2,1,0:T(8,128)(2,1)S(1)}, u32[]{:S(2)}, u32[]{:S(2)}) collective-permute-start(bf16[2,64,512]{2,1,0:T(8,128)(2,1)S(1)} %pad_maximum_fusion.7), channel_id=1, source_target_pairs={{0,2},{1,3},{2,0},{3,1},{4,6},{5,7},{6,4},{7,5},{8,10},{9,11},{10,... | collective-permute-start | bytes 393224 | tf_op jit(solution)/shard_map/ppermute | solution.py:355
  8.5 7.0 %collective-permute-start.5 = (bf16[2,64,512]{2,1,0:T(8,128)(2,1)S(1)}, bf16[2,64,512]{2,1,0:T(8,128)(2,1)S(1)}, u32[]{:S(2)}, u32[]{:S(2)}) collective-permute-start(bf16[2,64,512]{2,1,0:T(8,128)(2,1)S(1)} %pad_maximum_fusion.7), channel_id=1, source_target_pairs={{0,6},{1,7},{2,4},{3,5},{4,2},{5,3},{6,0},{7,1},{8,14},{9,15},{10,... | collective-permute-start | bytes 393224 | tf_op jit(solution)/shard_map/ppermute | solution.py:355
  9.5 12.1 %collective-permute-start.4 = (bf16[2,64,512]{2,1,0:T(8,128)(2,1)S(1)}, bf16[2,64,512]{2,1,0:T(8,128)(2,1)S(1)}, u32[]{:S(2)}, u32[]{:S(2)}) collective-permute-start(bf16[2,64,512]{2,1,0:T(8,128)(2,1)S(1)} %pad_maximum_fusion.7), channel_id=1, source_target_pairs={{0,4},{1,5},{2,6},{3,7},{4,0},{5,1},{6,2},{7,3},{8,12},{9,13},{10,... | collective-permute-start | bytes 393224 | tf_op jit(solution)/shard_map/ppermute | solution.py:355
  11.6 13.4 %collective-permute-start.9 = (f32[2,512]{1,0:T(2,128)S(1)}, f32[2,512]{1,0:T(2,128)S(1)}, u32[]{:S(2)}, u32[]{:S(2)}) collective-permute-start(f32[2,512]{1,0:T(2,128)S(1)} %bitcast.50), channel_id=1, source_target_pairs={{0,8},{8,0},{16,24},{24,16},{1,9},{9,1},{17,25},{25,17},{2,10},{10... | collective-permute-start | bytes 12296 | tf_op jit(solution)/shard_map/ppermute | solution.py:355
  11.8 13.2 %collective-permute-start.8 = (f32[2,512]{1,0:T(2,128)S(1)}, f32[2,512]{1,0:T(2,128)S(1)}, u32[]{:S(2)}, u32[]{:S(2)}) collective-permute-start(f32[2,512]{1,0:T(2,128)S(1)} %bitcast.51), channel_id=1, source_target_pairs={{0,16},{8,24},{16,0},{24,8},{1,17},{9,25},{17,1},{25,9},{2,18},{10... | collective-permute-start | bytes 12296 | tf_op jit(solution)/shard_map/ppermute | solution.py:355
  13.1 10.9 %copy-start = (bf16[2,1,64,512]{3,2,1,0:T(8,128)(2,1)S(1)}, bf16[2,1,64,512]{3,2,1,0:T(8,128)(2,1)}, u32[]{:S(2)}) copy-start(bf16[2,1,64,512]{3,2,1,0:T(8,128)(2,1)} %param.3) | copy-start | bytes 393220
  14.1 13.6 %collective-permute-start.7 = (f32[2,512]{1,0:T(2,128)S(1)}, f32[2,512]{1,0:T(2,128)S(1)}, u32[]{:S(2)}, u32[]{:S(2)}) collective-permute-start(f32[2,512]{1,0:T(2,128)S(1)} %bitcast.52), channel_id=1, source_target_pairs={{0,24},{8,16},{16,8},{24,0},{1,25},{9,17},{17,9},{25,1},{2,26},{10... | collective-permute-start | bytes 12296 | tf_op jit(solution)/shard_map/ppermute | solution.py:355
  21.7 6.0 %collective-permute-start.6 = (bf16[4,2,64,512]{3,2,1,0:T(8,128)(2,1)S(1)}, bf16[4,2,64,512]{3,2,1,0:T(8,128)(2,1)S(1)}, u32[]{:S(2)}, u32[]{:S(2)}) collective-permute-start(bf16[4,2,64,512]{3,2,1,0:T(8,128)(2,1)S(1)} %pad_maximum_fusion.2.mine_ref), channel_id=1, source_target_pairs={{0,1},{1,0},{2,3},{3,2},{4,5},{5,4},{6,7},{7,6},{8,9},{9,8},{10,11... | collective-permute-start | bytes 1572872 | tf_op jit(solution)/shard_map/ppermute | solution.py:355
  24.1 23.8 %collective-permute-start.12 = (bf16[4,64,512]{2,1,0:T(8,128)(2,1)S(1)}, bf16[4,64,512]{2,1,0:T(8,128)(2,1)S(1)}, u32[]{:S(2)}, u32[]{:S(2)}) collective-permute-start(bf16[4,64,512]{2,1,0:T(8,128)(2,1)S(1)} %get-tuple-element.49), channel_id=1, source_target_pairs={{0,6},{1,7},{2,4},{3,5},{4,2},{5,3},{6,0},{7,1},{8,14},{9,15},{10,... | collective-permute-start | bytes 786440 | tf_op jit(solution)/shard_map/ppermute | solution.py:355
  25.1 22.8 %collective-permute-start.10 = (bf16[4,64,512]{2,1,0:T(8,128)(2,1)S(1)}, bf16[4,64,512]{2,1,0:T(8,128)(2,1)S(1)}, u32[]{:S(2)}, u32[]{:S(2)}) collective-permute-start(bf16[4,64,512]{2,1,0:T(8,128)(2,1)S(1)} %get-tuple-element.50), channel_id=1, source_target_pairs={{0,2},{1,3},{2,0},{3,1},{4,6},{5,7},{6,4},{7,5},{8,10},{9,11},{10,... | collective-permute-start | bytes 786440 | tf_op jit(solution)/shard_map/ppermute | solution.py:355
  25.1 22.8 %collective-permute-start.11 = (bf16[4,64,512]{2,1,0:T(8,128)(2,1)S(1)}, bf16[4,64,512]{2,1,0:T(8,128)(2,1)S(1)}, u32[]{:S(2)}, u32[]{:S(2)}) collective-permute-start(bf16[4,64,512]{2,1,0:T(8,128)(2,1)S(1)} %get-tuple-element.51), channel_id=1, source_target_pairs={{0,4},{1,5},{2,6},{3,7},{4,0},{5,1},{6,2},{7,3},{8,12},{9,13},{10,... | collective-permute-start | bytes 786440 | tf_op jit(solution)/shard_map/ppermute | solution.py:355
  48.1 9.7 %collective-permute-start.13 = (bf16[4,3,64,512]{3,2,1,0:T(8,128)(2,1)S(1)}, bf16[4,3,64,512]{3,2,1,0:T(8,128)(2,1)S(1)}, u32[]{:S(2)}, u32[]{:S(2)}) collective-permute-start(bf16[4,3,64,512]{3,2,1,0:T(8,128)(2,1)S(1)} %pad_maximum_fusion), channel_id=1, source_target_pairs={{0,1},{1,0},{2,3},{3,2},{4,5},{5,4},{6,7},{7,6},{8,9},{9,8},{10,11... | collective-permute-start | bytes 2359304 | tf_op jit(solution)/shard_map/ppermute | solution.py:355

commit v6 on v5

--- a/solution.py
+++ b/solution.py
@@ -123,22 +123,31 @@
                 tiles[i] = jnp.where(keep, tiles[i], 0.0) - change[8 * i : 8 * i + 8]
 
 
-def half_norm_rows(x):
-    xf = x.astype(f32)
-    hi, lo = split(xf * xf)
-    ones = jnp.ones((8, x.shape[1]), bf16)
-    total = lax.dot_general(ones, hi, TRANS_B, preferred_element_type=f32)
-    total = total + lax.dot_general(ones, lo, TRANS_B, preferred_element_type=f32)
-    return 0.5 * total[0:1]
-
-
-def half_norm_cols(x, width):
+def half_norms(x):
     xf = x.astype(f32)
     hi, lo = split(xf * xf)
     ones = jnp.ones((NB, x.shape[1]), bf16)
-    total = lax.dot_general(hi, ones, TRANS_B, preferred_element_type=f32)
-    total = 0.5 * (total + lax.dot_general(lo, ones, TRANS_B, preferred_element_type=f32))
-    return jnp.concatenate([total] * (width // NB), 1)
+    row = lax.dot_general(ones[:8], hi, TRANS_B, preferred_element_type=f32)
+    row = row + lax.dot_general(ones[:8], lo, TRANS_B, preferred_element_type=f32)
+    col = lax.dot_general(hi, ones, TRANS_B, preferred_element_type=f32)
+    col = col + lax.dot_general(lo, ones, TRANS_B, preferred_element_type=f32)
+    return 0.5 * row[0:1], 0.5 * col
+
+
+def half_norm_col(x):
+    xf = x.astype(f32)
+    hi, lo = split(xf * xf)
+    ones = jnp.ones((NB, x.shape[1]), bf16)
+    col = lax.dot_general(hi, ones, TRANS_B, preferred_element_type=f32)
+    return 0.5 * (col + lax.dot_general(lo, ones, TRANS_B, preferred_element_type=f32))
+
+
+def widen(col, width):
+    return jnp.concatenate([col] * (width // NB), 1)
+
+
+def log_row(amp, width):
+    return jnp.log(jnp.full((1, width), amp, f32))
 
 
 def diagonal(n):
@@ -202,7 +211,8 @@
     lax.fori_loop(0, count, panel, 0)
 
 
-def first_kernel(at_ref, amp_ref, mine_ref, other_ref, nz_ref, x_ref, u_ref, wh_ref, wl_ref, rest_ref, a_ref, inv_ref):
+def first_kernel(at_ref, amp_ref, mine_ref, other_ref, nz_ref, *refs):
+    x_ref, sq_ref, u_ref, wh_ref, wl_ref, rest_ref, a_ref, inv_ref, col_ref = refs
     n = a_ref.shape[0]
     steps, panels, piece = mine_ref.shape[:3]
     block = n // panels
@@ -211,13 +221,13 @@
         for s in range(panels):
             place(x_ref, s * block, me ^ (2 * m), piece, mine_ref[m, s])
             place(x_ref, s * block, me ^ (2 * m + 1), piece, other_ref[m, s])
-    amp = amp_ref[0]
-    sq_row = half_norm_rows(x_ref[...])
+    sq_row, col_ref[...] = half_norms(x_ref[...])
+    sq_row = sq_row - log_row(amp_ref[0], n)
+    sq_ref[...] = jnp.broadcast_to(sq_row, sq_ref.shape)
     noise = nz_ref[...]
     for o in range(0, n, WB):
-        xi = x_ref[o : o + WB, :]
-        cross = lax.dot_general(xi, x_ref[o:, :], TRANS_B, preferred_element_type=f32)
-        k = amp * jnp.exp(cross - half_norm_cols(xi, n - o) - sq_row[:, o:])
+        cross = lax.dot_general(x_ref[o : o + WB, :], x_ref[o:, :], TRANS_B, preferred_element_type=f32)
+        k = jnp.exp(cross - widen(col_ref[o : o + WB, :], n - o) - sq_row[:, o:])
         a_ref[o : o + WB, o:] = k
         row = noise[o // block : o // block + 1, o % block : o % block + WB]
         a_ref[o : o + WB, o : o + WB] = k[:, :WB] + jnp.where(diagonal(WB), jnp.broadcast_to(row, (WB, WB)), 0.0)
@@ -241,18 +251,17 @@
 
 
 def bulk_kernel(at_ref, amp_ref, *refs):
-    x_ref, u0_ref, wh0_ref, wl0_ref, u1_ref, wh1_ref, wl1_ref, nz_ref = refs[:8]
-    refs = refs[8:]
-    count = len(refs) - 10
+    x_ref, sq_ref, u0_ref, wh0_ref, wl0_ref, u1_ref, wh1_ref, wl1_ref, nz_ref = refs[:9]
+    refs = refs[9:]
+    count = len(refs) - 11
     near_refs, other_ref, out_ref = refs[:count], refs[count], refs[count + 1]
-    r_ref, c_ref, kh_ref, kl_ref, ph_ref, pl_ref, zh_ref, zl_ref = refs[count + 2 :]
+    r_ref, c_ref, kh_ref, kl_ref, ph_ref, pl_ref, zh_ref, zl_ref, col_ref = refs[count + 2 :]
     n = x_ref.shape[0]
     split_at = u0_ref.shape[0]
     nrows, block = nz_ref.shape
     piece = other_ref.shape[2]
     ncols = c_ref.shape[0] // block
     row_at, me, row_n, col_n = at_ref[0], at_ref[1], at_ref[2], at_ref[3]
-    amp = amp_ref[0]
     for m in range(count):
         for a in range(nrows):
             place(r_ref, a * block, me ^ (2 * m), piece, near_refs[m][a])
@@ -272,15 +281,16 @@
     def inverse(r0, r1, c0, c1):
         return pick(wh0_ref, wh1_ref, r0, r1, c0, c1), pick(wl0_ref, wl1_ref, r0, r1, c0, c1)
 
-    lead_sq = half_norm_rows(x_ref[...])
-
-    def entries(x):
+    lead_sq = sq_ref[0:1, :]
+
+    def entries(x, col):
         cross = lax.dot_general(x, x_ref[...], TRANS_B, preferred_element_type=f32)
-        return split(amp * jnp.exp(cross - half_norm_cols(x, n) - lead_sq))
+        return split(jnp.exp(cross - widen(col, n) - lead_sq))
 
     for a in range(nrows):
         rows = slice(a * block, (a + 1) * block)
-        kh_ref[rows, :], kl_ref[rows, :] = entries(r_ref[rows, :])
+        col_ref[rows, :] = half_norm_col(r_ref[rows, :])
+        kh_ref[rows, :], kl_ref[rows, :] = entries(r_ref[rows, :], col_ref[rows, :])
     for b in range(ncols):
         j = b * col_n + me
         cols = slice(b * block, (b + 1) * block)
@@ -288,7 +298,9 @@
         @pl.when(j >= PANELS)
         def _():
             xc = c_ref[cols, :]
-            zh_ref[...], zl_ref[...] = entries(xc)
+            col_sq, col = half_norms(xc)
+            col_sq = col_sq - log_row(amp_ref[0], block)
+            zh_ref[...], zl_ref[...] = entries(xc, col)
             for s in range(0, n, block):
                 e = s + block
                 panel = dot_nt(zh_ref[:, :e], zl_ref[:, :e], *inverse(s, e, 0, e))
@@ -297,7 +309,6 @@
                 e = s + block
                 solved = dot_nn(ph_ref[:, s:], pl_ref[:, s:], *inverse(s, n, s, e))
                 zh_ref[:, s:e], zl_ref[:, s:e] = split(solved)
-            col_sq = half_norm_rows(xc)
             for a in range(nrows):
                 i = a * row_n + row_at
                 rows = slice(a * block, (a + 1) * block)
@@ -306,7 +317,7 @@
                 def _():
                     xr = r_ref[rows, :]
                     cross = lax.dot_general(xr, xc, TRANS_B, preferred_element_type=f32)
-                    k = amp * jnp.exp(cross - half_norm_cols(xr, block) - col_sq)
+                    k = jnp.exp(cross - widen(col_ref[rows, :], block) - col_sq)
                     on_diag = diagonal(block) & (i == j)
                     k = k + jnp.where(on_diag, jnp.broadcast_to(nz_ref[a : a + 1, :], (block, block)), 0.0)
                     k = k - dot_nt(kh_ref[rows, :], kl_ref[rows, :], zh_ref[...], zl_ref[...])
@@ -405,14 +416,14 @@
         half = jax.ShapeDtypeStruct((rows, n), bf16)
         return [jax.ShapeDtypeStruct((rows, n), f32), half, half]
 
-    points, u0, wh0, wl0, rest = pl.pallas_call(
+    points, lead_sq, u0, wh0, wl0, rest = pl.pallas_call(
         first_kernel,
-        out_shape=[jax.ShapeDtypeStruct((n, width), bf16)]
+        out_shape=[jax.ShapeDtypeStruct((n, width), bf16), jax.ShapeDtypeStruct((8, n), f32)]
         + factor_shapes(first)
         + [jax.ShapeDtypeStruct((n1, n), f32)],
         in_specs=[SMEM, SMEM, VMEM, VMEM, VMEM],
-        out_specs=[VMEM] * 5,
-        scratch_shapes=[pltpu.VMEM((n, n), f32), square],
+        out_specs=[VMEM] * 6,
+        scratch_shapes=[pltpu.VMEM((n, n), f32), square, pltpu.VMEM((n, NB), f32)],
         compiler_params=params,
         cost_estimate=pl.CostEstimate(flops=1_000_000, bytes_accessed=1_000_000, transcendentals=0),
         name="first",
@@ -434,7 +445,7 @@
     out = pl.pallas_call(
         bulk_kernel,
         out_shape=jax.ShapeDtypeStruct((nrows * block * ncols * (block // NB), NB), f32),
-        in_specs=[SMEM, SMEM] + [VMEM] * (9 + len(parcels)),
+        in_specs=[SMEM, SMEM] + [VMEM] * (10 + len(parcels)),
         out_specs=VMEM,
         scratch_shapes=[
             pltpu.VMEM((nrows * block, width), bf16),
@@ -445,11 +456,12 @@
             half,
             half,
             half,
+            pltpu.VMEM((nrows * block, NB), f32),
         ],
         compiler_params=params,
         cost_estimate=cost,
         name="bulk",
-    )(at, amplitude, points, u0, wh0, wl0, u1, wh1, wl1, noise_rows, *parcels, passed)
+    )(at, amplitude, points, lead_sq, u0, wh0, wl0, u1, wh1, wl1, noise_rows, *parcels, passed)
     return out.reshape(nrows, 1, block, ncols, 1, block)
 
 

time: 75.2 us -> 72.5 us (0.964)
  Pallas kernels: 46 us -> 43.3 us
    pallas_call x1, Pallas kernels: 17.2 us -> 14.9 us  [local(): pl.pallas_call(bulk_kernel, out_shape=jax.ShapeDtypeStruct((nrows * block...]
  transfers between devices with their start and end apart: 14 -> 14, of which waited for: 4 -> 4; matrix products, arithmetic and copies ran while one was open for 3% -> 3% of each run, Pallas kernels for 38% -> 39%
where the time goes in v6:
time: 72.5 us; the launch traced here: 72.3 us
  Pallas kernels  43.3 us (60%)
  starting transfers between devices  14.9 us (21%)
  waiting for transfers between devices  10.1 us (14%)
  other arithmetic  2.27 us (3%)
  between operations  0.86 us (1%)
  local copies, waits for them, and re-layouts  0.78 us (1%)
    pallas_call x1, Pallas kernels, local(): pl.pallas_call(first_kernel, out_shape=[jax.ShapeDtypeStruct((n, width),...  19.9 us
    ppermute x14, starting transfers between devices, exchange(): lax.ppermute(x, axis, [(i, i ^ k) for i in range(lax.axis_size(axis))])  14.9 us
    pallas_call x1, Pallas kernels, local(): pl.pallas_call(bulk_kernel, out_shape=jax.ShapeDtypeStruct((nrows * block...  14.9 us
    ppermute x14, waiting for transfers between devices, exchange(): lax.ppermute(x, axis, [(i, i ^ k) for i in range(lax.axis_size(axis))])  10.1 us
    pallas_call x1, Pallas kernels, local(): pl.pallas_call(second_kernel, out_shape=factor_shapes(n1), in_specs=[VMEM...  8.5 us
  transfers between devices with their start and end apart: 14, of which 4 were waited for; matrix products, arithmetic and copies ran while one was open for 3% of the time, Pallas kernels for 39%

profile of v6, /device:TPU:31, one launch (start us, length us, event | category | flops | bytes accessed | tf_op | source)
XLA Modules:
  0.0 72.3 jit_solution(254189609053490792)
XLA Ops:
  0.0 0.3 collective-permute-start.2
  0.3 0.2 collective-permute-start.1
  0.5 2.2 %collective-permute-start = (bf16[2,64,512]{2,1,0:T(8,128)(2,1)}, bf16[2,64,512]{2,1,0:T(8,128)(2,1)S(1)}, u32[]{:S(2)}, u32[]{:S(2)}) collective-permute-start(bf16[2,64,512]{2,1,0:T(8,128)(2,1)} %bitcast.57), channel_id=1, source_target_pairs={{0,24},{8,16},{16,8},{24,0},{1,25},{9,17},{17,9},{25,1},{2,26},{10... | collective-permute-start | bytes 393224 | tf_op jit(solution)/shard_map/ppermute | solution.py:366
  2.7 0.7 copy.7
  3.3 0.1 pad_add_fusion.at_ref
  3.4 1.2 %collective-permute-done.2 = bf16[2,64,512]{2,1,0:T(8,128)(2,1)S(1)} collective-permute-done((bf16[2,64,512]{2,1,0:T(8,128)(2,1)}, bf16[2,64,512]{2,1,0:T(8,128)(2,1)S(1)}, u32[]{:S(2)}, u32[]{:S(2)}) %collective-permute-start.2) | collective-permute-done | bytes 131104 | tf_op jit(solution)/shard_map/ppermute | solution.py:366
  4.6 0.1 collective-permute-done.1
  4.6 2.7 %collective-permute-done = bf16[2,64,512]{2,1,0:T(8,128)(2,1)S(1)} collective-permute-done((bf16[2,64,512]{2,1,0:T(8,128)(2,1)}, bf16[2,64,512]{2,1,0:T(8,128)(2,1)S(1)}, u32[]{:S(2)}, u32[]{:S(2)}) %collective-permute-start) | collective-permute-done | bytes 131104 | tf_op jit(solution)/shard_map/ppermute | solution.py:366
  7.3 0.9 %fusion.5 = (bf16[1,64,512]{2,1,0:T(8,128)(2,1)S(1)}, bf16[1,64,512]{2,1,0:T(8,128)(2,1)S(1)}) fusion(pred[]{:T(512)S(6)} %eq.26, pred[]{:T(512)S(6)} %eq.25, pred[]{:T(512)S(6)} %eq.24, bf16[2,64,512]{2,1,0:T(8,128)(2,1)S(1)} %collective-permute-done.2, bf16[2,64,512]{2,1,0:T(8,128)(2,1)S(1)} %collective-permute-done.1, ...), kind=kLoop, calls=%fused_computation.19 | loop fusion | flops 196608 | bytes 393222 | tf_op jit(solution)/shard_map/jit(_where)/select_n | solution.py:372
  8.2 0.2 collective-permute-start.3
  8.5 1.1 %collective-permute-start.5 = (bf16[2,64,512]{2,1,0:T(8,128)(2,1)S(1)}, bf16[2,64,512]{2,1,0:T(8,128)(2,1)S(1)}, u32[]{:S(2)}, u32[]{:S(2)}) collective-permute-start(bf16[2,64,512]{2,1,0:T(8,128)(2,1)S(1)} %pad_maximum_fusion.7), channel_id=1, source_target_pairs={{0,6},{1,7},{2,4},{3,5},{4,2},{5,3},{6,0},{7,1},{8,14},{9,15},{10,... | collective-permute-start | bytes 393224 | tf_op jit(solution)/shard_map/ppermute | solution.py:366
  9.5 1.4 %collective-permute-start.4 = (bf16[2,64,512]{2,1,0:T(8,128)(2,1)S(1)}, bf16[2,64,512]{2,1,0:T(8,128)(2,1)S(1)}, u32[]{:S(2)}, u32[]{:S(2)}) collective-permute-start(bf16[2,64,512]{2,1,0:T(8,128)(2,1)S(1)} %pad_maximum_fusion.7), channel_id=1, source_target_pairs={{0,4},{1,5},{2,6},{3,7},{4,0},{5,1},{6,2},{7,3},{8,12},{9,13},{10,... | collective-permute-start | bytes 393224 | tf_op jit(solution)/shard_map/ppermute | solution.py:366
  11.6 0.2 collective-permute-start.9
  11.8 1.2 %collective-permute-start.8 = (f32[2,512]{1,0:T(2,128)S(1)}, f32[2,512]{1,0:T(2,128)S(1)}, u32[]{:S(2)}, u32[]{:S(2)}) collective-permute-start(f32[2,512]{1,0:T(2,128)S(1)} %bitcast.51), channel_id=1, source_target_pairs={{0,16},{8,24},{16,0},{24,8},{1,17},{9,25},{17,1},{25,9},{2,18},{10... | collective-permute-start | bytes 12296 | tf_op jit(solution)/shard_map/ppermute | solution.py:366
  13.1 0.0 copy-start
  13.1 1.0 %pad_maximum_fusion.1 = bf16[4,2,64,512]{3,2,1,0:T(8,128)(2,1)S(1)} fusion(bf16[1,2,64,512]{3,2,1,0:T(8,128)(2,1)S(1)} %bitcast.63, bf16[1,2,64,512]{3,2,1,0:T(8,128)(2,1)S(1)} %bitcast.62, bf16[1,2,64,512]{3,2,1,0:T(8,128)(2,1)S(1)} %bitcast.61, bf16[1,2,64,512]{3,2,1,0:T(8,128)(2,1)} %bitcast.58), kind=kLoop, calls=%fused_computation.1 | loop fusion | flops 786432 | bytes 1048576 | tf_op jit(solution)/shard_map/stack | solution.py:391
  14.1 0.0 collective-permute-done.3
  14.1 1.4 %collective-permute-start.7 = (f32[2,512]{1,0:T(2,128)S(1)}, f32[2,512]{1,0:T(2,128)S(1)}, u32[]{:S(2)}, u32[]{:S(2)}) collective-permute-start(f32[2,512]{1,0:T(2,128)S(1)} %bitcast.52), channel_id=1, source_target_pairs={{0,24},{8,16},{16,8},{24,0},{1,25},{9,17},{17,9},{25,1},{2,26},{10... | collective-permute-start | bytes 12296 | tf_op jit(solution)/shard_map/ppermute | solution.py:366
  15.5 0.0 collective-permute-done.5
  15.5 6.2 %collective-permute-done.4 = bf16[2,64,512]{2,1,0:T(8,128)(2,1)S(1)} collective-permute-done((bf16[2,64,512]{2,1,0:T(8,128)(2,1)S(1)}, bf16[2,64,512]{2,1,0:T(8,128)(2,1)S(1)}, u32[]{:S(2)}, u32[]{:S(2)}) %collective-permute-start.4) | collective-permute-done | bytes 131104 | tf_op jit(solution)/shard_map/ppermute | solution.py:366
  21.7 0.1 pad_maximum_fusion.2.mine_ref
  21.7 2.2 %collective-permute-start.6 = (bf16[4,2,64,512]{3,2,1,0:T(8,128)(2,1)S(1)}, bf16[4,2,64,512]{3,2,1,0:T(8,128)(2,1)S(1)}, u32[]{:S(2)}, u32[]{:S(2)}) collective-permute-start(bf16[4,2,64,512]{3,2,1,0:T(8,128)(2,1)S(1)} %pad_maximum_fusion.2.mine_ref), channel_id=1, source_target_pairs={{0,1},{1,0},{2,3},{3,2},{4,5},{5,4},{6,7},{7,6},{8,9},{9,8},{10,11... | collective-permute-start | bytes 1572872 | tf_op jit(solution)/shard_map/ppermute | solution.py:366
  24.0 0.0 copy-done
  24.0 0.1 fusion.3
  24.1 1.0 %collective-permute-start.12 = (bf16[4,64,512]{2,1,0:T(8,128)(2,1)S(1)}, bf16[4,64,512]{2,1,0:T(8,128)(2,1)S(1)}, u32[]{:S(2)}, u32[]{:S(2)}) collective-permute-start(bf16[4,64,512]{2,1,0:T(8,128)(2,1)S(1)} %get-tuple-element.51), channel_id=1, source_target_pairs={{0,6},{1,7},{2,4},{3,5},{4,2},{5,3},{6,0},{7,1},{8,14},{9,15},{10,... | collective-permute-start | bytes 786440 | tf_op jit(solution)/shard_map/ppermute | solution.py:366
  25.1 0.0 collective-permute-done.9
  25.1 0.0 collective-permute-start.10
  25.1 0.0 collective-permute-done.8
  25.1 2.6 %collective-permute-start.11 = (bf16[4,64,512]{2,1,0:T(8,128)(2,1)S(1)}, bf16[4,64,512]{2,1,0:T(8,128)(2,1)S(1)}, u32[]{:S(2)}, u32[]{:S(2)}) collective-permute-start(bf16[4,64,512]{2,1,0:T(8,128)(2,1)S(1)} %get-tuple-element.53), channel_id=1, source_target_pairs={{0,4},{1,5},{2,6},{3,7},{4,0},{5,1},{6,2},{7,3},{8,12},{9,13},{10,... | collective-permute-start | bytes 786440 | tf_op jit(solution)/shard_map/ppermute | solution.py:366
  27.7 0.0 collective-permute-done.7
  27.7 0.0 collective-permute-done.6.other_ref
  27.7 19.9 %first.1 = (bf16[1024,512]{1,0:T(8,128)(2,1)S(1)}, f32[8,1024]{1,0:T(8,128)S(1)}, f32[640,1024]{1,0:T(8,128)S(1)}, bf16[640,1024]{1,0:T(8,128)(2,1)S(1)}, bf16[6...) custom-call(s32[4]{0:T(128)S(1)} %pad_add_fusion.at_ref, f32[1]{0:T(128)S(6)} %copy.8.amp_ref, ...), custom_call_target="tpu_custom_call" | custom-call | flops 1000000 | bytes 1000000 | tf_op jit(solution)/shard_map/first/pallas_call | solution.py:419
  47.7 0.0 collective-permute-done.12.refs_12_
  47.7 0.0 collective-permute-done.10.refs_10_
  47.7 0.0 collective-permute-done.11.refs_11_
  47.8 0.1 pad_maximum_fusion
  47.9 1.0 %collective-permute-start.13 = (bf16[4,3,64,512]{3,2,1,0:T(8,128)(2,1)S(1)}, bf16[4,3,64,512]{3,2,1,0:T(8,128)(2,1)S(1)}, u32[]{:S(2)}, u32[]{:S(2)}) collective-permute-start(bf16[4,3,64,512]{3,2,1,0:T(8,128)(2,1)S(1)} %pad_maximum_fusion), channel_id=1, source_target_pairs={{0,1},{1,0},{2,3},{3,2},{4,5},{5,4},{6,7},{7,6},{8,9},{9,8},{10,11... | collective-permute-start | bytes 2359304 | tf_op jit(solution)/shard_map/ppermute | solution.py:366
  48.8 8.5 %second.1 = (f32[384,1024]{1,0:T(8,128)S(1)}, bf16[384,1024]{1,0:T(8,128)(2,1)S(1)}, bf16[384,1024]{1,0:T(8,128)(2,1)S(1)}) custom-call(f32[384,1024]{1,0:T(8,128)S(1)} %get-tuple-element.33.rest_ref), custom_call_target="tpu_custom_call" | custom-call | flops 20000000000 | bytes 8000000 | tf_op jit(solution)/shard_map/second/pallas_call | solution.py:433
  57.3 0.0 collective-permute-done.13.refs_13_
  57.4 14.9 %bulk.1 = f32[4096,128]{1,0:T(8,128)} custom-call(s32[4]{0:T(128)S(1)} %pad_add_fusion.at_ref, f32[1]{0:T(128)S(6)} %copy.8.amp_ref, bf16[1024,512]{1,0:T(8,128)(2,1)S(1)} %get-tuple-element.26.refs_0_, f32[8,1024]{1,0:T(8,128)S(1)} %get-tuple-element.27.refs_1_, f32[640,1024]{1,0:T(8,128)S(1)} %get-tuple-element.28.refs_2_, ...), custom_call_target="tpu_custom_call" | custom-call | flops 20000000000 | bytes 8000000 | tf_op jit(solution)/shard_map/bulk/pallas_call | solution.py:445
  (6 shorter events, 0.1 us)
Async XLA Ops:
  0.0 4.6 %collective-permute-start.2 = (bf16[2,64,512]{2,1,0:T(8,128)(2,1)}, bf16[2,64,512]{2,1,0:T(8,128)(2,1)S(1)}, u32[]{:S(2)}, u32[]{:S(2)}) collective-permute-start(bf16[2,64,512]{2,1,0:T(8,128)(2,1)} %bitcast.55), channel_id=1, source_target_pairs={{0,8},{8,0},{16,24},{24,16},{1,9},{9,1},{17,25},{25,17},{2,10},{10... | collective-permute-start | bytes 393224 | tf_op jit(solution)/shard_map/ppermute | solution.py:366
  0.3 4.4 %collective-permute-start.1 = (bf16[2,64,512]{2,1,0:T(8,128)(2,1)}, bf16[2,64,512]{2,1,0:T(8,128)(2,1)S(1)}, u32[]{:S(2)}, u32[]{:S(2)}) collective-permute-start(bf16[2,64,512]{2,1,0:T(8,128)(2,1)} %bitcast.56), channel_id=1, source_target_pairs={{0,16},{8,24},{16,0},{24,8},{1,17},{9,25},{17,1},{25,9},{2,18},{10... | collective-permute-start | bytes 393224 | tf_op jit(solution)/shard_map/ppermute | solution.py:366
  0.5 6.8 %collective-permute-start = (bf16[2,64,512]{2,1,0:T(8,128)(2,1)}, bf16[2,64,512]{2,1,0:T(8,128)(2,1)S(1)}, u32[]{:S(2)}, u32[]{:S(2)}) collective-permute-start(bf16[2,64,512]{2,1,0:T(8,128)(2,1)} %bitcast.57), channel_id=1, source_target_pairs={{0,24},{8,16},{16,8},{24,0},{1,25},{9,17},{17,9},{25,1},{2,26},{10... | collective-permute-start | bytes 393224 | tf_op jit(solution)/shard_map/ppermute | solution.py:366
  8.2 5.9 %collective-permute-start.3 = (bf16[2,64,512]{2,1,0:T(8,128)(2,1)S(1)}, bf16[2,64,512]{2,1,0:T(8,128)(2,1)S(1)}, u32[]{:S(2)}, u32[]{:S(2)}) collective-permute-start(bf16[2,64,512]{2,1,0:T(8,128)(2,1)S(1)} %pad_maximum_fusion.7), channel_id=1, source_target_pairs={{0,2},{1,3},{2,0},{3,1},{4,6},{5,7},{6,4},{7,5},{8,10},{9,11},{10,... | collective-permute-start | bytes 393224 | tf_op jit(solution)/shard_map/ppermute | solution.py:366
  8.5 7.0 %collective-permute-start.5 = (bf16[2,64,512]{2,1,0:T(8,128)(2,1)S(1)}, bf16[2,64,512]{2,1,0:T(8,128)(2,1)S(1)}, u32[]{:S(2)}, u32[]{:S(2)}) collective-permute-start(bf16[2,64,512]{2,1,0:T(8,128)(2,1)S(1)} %pad_maximum_fusion.7), channel_id=1, source_target_pairs={{0,6},{1,7},{2,4},{3,5},{4,2},{5,3},{6,0},{7,1},{8,14},{9,15},{10,... | collective-permute-start | bytes 393224 | tf_op jit(solution)/shard_map/ppermute | solution.py:366
  9.5 12.1 %collective-permute-start.4 = (bf16[2,64,512]{2,1,0:T(8,128)(2,1)S(1)}, bf16[2,64,512]{2,1,0:T(8,128)(2,1)S(1)}, u32[]{:S(2)}, u32[]{:S(2)}) collective-permute-start(bf16[2,64,512]{2,1,0:T(8,128)(2,1)S(1)} %pad_maximum_fusion.7), channel_id=1, source_target_pairs={{0,4},{1,5},{2,6},{3,7},{4,0},{5,1},{6,2},{7,3},{8,12},{9,13},{10,... | collective-permute-start | bytes 393224 | tf_op jit(solution)/shard_map/ppermute | solution.py:366
  11.6 13.4 %collective-permute-start.9 = (f32[2,512]{1,0:T(2,128)S(1)}, f32[2,512]{1,0:T(2,128)S(1)}, u32[]{:S(2)}, u32[]{:S(2)}) collective-permute-start(f32[2,512]{1,0:T(2,128)S(1)} %bitcast.50), channel_id=1, source_target_pairs={{0,8},{8,0},{16,24},{24,16},{1,9},{9,1},{17,25},{25,17},{2,10},{10... | collective-permute-start | bytes 12296 | tf_op jit(solution)/shard_map/ppermute | solution.py:366
  11.8 13.2 %collective-permute-start.8 = (f32[2,512]{1,0:T(2,128)S(1)}, f32[2,512]{1,0:T(2,128)S(1)}, u32[]{:S(2)}, u32[]{:S(2)}) collective-permute-start(f32[2,512]{1,0:T(2,128)S(1)} %bitcast.51), channel_id=1, source_target_pairs={{0,16},{8,24},{16,0},{24,8},{1,17},{9,25},{17,1},{25,9},{2,18},{10... | collective-permute-start | bytes 12296 | tf_op jit(solution)/shard_map/ppermute | solution.py:366
  13.1 10.9 %copy-start = (bf16[2,1,64,512]{3,2,1,0:T(8,128)(2,1)S(1)}, bf16[2,1,64,512]{3,2,1,0:T(8,128)(2,1)}, u32[]{:S(2)}) copy-start(bf16[2,1,64,512]{3,2,1,0:T(8,128)(2,1)} %param.3) | copy-start | bytes 393220
  14.1 13.6 %collective-permute-start.7 = (f32[2,512]{1,0:T(2,128)S(1)}, f32[2,512]{1,0:T(2,128)S(1)}, u32[]{:S(2)}, u32[]{:S(2)}) collective-permute-start(f32[2,512]{1,0:T(2,128)S(1)} %bitcast.52), channel_id=1, source_target_pairs={{0,24},{8,16},{16,8},{24,0},{1,25},{9,17},{17,9},{25,1},{2,26},{10... | collective-permute-start | bytes 12296 | tf_op jit(solution)/shard_map/ppermute | solution.py:366
  21.7 6.0 %collective-permute-start.6 = (bf16[4,2,64,512]{3,2,1,0:T(8,128)(2,1)S(1)}, bf16[4,2,64,512]{3,2,1,0:T(8,128)(2,1)S(1)}, u32[]{:S(2)}, u32[]{:S(2)}) collective-permute-start(bf16[4,2,64,512]{3,2,1,0:T(8,128)(2,1)S(1)} %pad_maximum_fusion.2.mine_ref), channel_id=1, source_target_pairs={{0,1},{1,0},{2,3},{3,2},{4,5},{5,4},{6,7},{7,6},{8,9},{9,8},{10,11... | collective-permute-start | bytes 1572872 | tf_op jit(solution)/shard_map/ppermute | solution.py:366
  24.1 23.6 %collective-permute-start.12 = (bf16[4,64,512]{2,1,0:T(8,128)(2,1)S(1)}, bf16[4,64,512]{2,1,0:T(8,128)(2,1)S(1)}, u32[]{:S(2)}, u32[]{:S(2)}) collective-permute-start(bf16[4,64,512]{2,1,0:T(8,128)(2,1)S(1)} %get-tuple-element.51), channel_id=1, source_target_pairs={{0,6},{1,7},{2,4},{3,5},{4,2},{5,3},{6,0},{7,1},{8,14},{9,15},{10,... | collective-permute-start | bytes 786440 | tf_op jit(solution)/shard_map/ppermute | solution.py:366
  25.1 22.6 %collective-permute-start.10 = (bf16[4,64,512]{2,1,0:T(8,128)(2,1)S(1)}, bf16[4,64,512]{2,1,0:T(8,128)(2,1)S(1)}, u32[]{:S(2)}, u32[]{:S(2)}) collective-permute-start(bf16[4,64,512]{2,1,0:T(8,128)(2,1)S(1)} %get-tuple-element.52), channel_id=1, source_target_pairs={{0,2},{1,3},{2,0},{3,1},{4,6},{5,7},{6,4},{7,5},{8,10},{9,11},{10,... | collective-permute-start | bytes 786440 | tf_op jit(solution)/shard_map/ppermute | solution.py:366
  25.1 22.6 %collective-permute-start.11 = (bf16[4,64,512]{2,1,0:T(8,128)(2,1)S(1)}, bf16[4,64,512]{2,1,0:T(8,128)(2,1)S(1)}, u32[]{:S(2)}, u32[]{:S(2)}) collective-permute-start(bf16[4,64,512]{2,1,0:T(8,128)(2,1)S(1)} %get-tuple-element.53), channel_id=1, source_target_pairs={{0,4},{1,5},{2,6},{3,7},{4,0},{5,1},{6,2},{7,3},{8,12},{9,13},{10,... | collective-permute-start | bytes 786440 | tf_op jit(solution)/shard_map/ppermute | solution.py:366
  47.9 9.5 %collective-permute-start.13 = (bf16[4,3,64,512]{3,2,1,0:T(8,128)(2,1)S(1)}, bf16[4,3,64,512]{3,2,1,0:T(8,128)(2,1)S(1)}, u32[]{:S(2)}, u32[]{:S(2)}) collective-permute-start(bf16[4,3,64,512]{3,2,1,0:T(8,128)(2,1)S(1)} %pad_maximum_fusion), channel_id=1, source_target_pairs={{0,1},{1,0},{2,3},{3,2},{4,5},{5,4},{6,7},{7,6},{8,9},{9,8},{10,11... | collective-permute-start | bytes 2359304 | tf_op jit(solution)/shard_map/ppermute | solution.py:366

commit v7 on v6

--- a/solution.py
+++ b/solution.py
@@ -12,7 +12,7 @@
 WB = 256
 GRANT = 30 << 20
 UPDATE_ROWS = 256
-FIRST = 5
+FIRST = 6
 GROUP = 4
 f32 = jnp.float32
 bf16 = jnp.bfloat16
@@ -76,12 +76,13 @@
     return [spread(tile[:, first + k : first + k + 1]) for k in range(8)]
 
 
-def factor_block(tiles, store_u, store_l):
+def factor_block(tiles):
     tiles = list(tiles)
     n = len(tiles)
     lane = lax.broadcasted_iota(jnp.int32, (8, NB), 1)
     sub = lax.broadcasted_iota(jnp.int32, (8, NB), 0)
     cols = lane_columns(tiles[0], 0)
+    uppers, lowers = [], []
     for g in range(0, n, GROUP):
         end = g + GROUP
         window = min(n, end + 1)
@@ -112,8 +113,8 @@
             final = rows * root
             diff = lane - sub - 8 * t
             lower = jnp.where(diff < 0, final, jnp.where(diff == 0, root, 0.0))
-            store_u(t, jnp.where(diff >= 0, final, 0.0))
-            store_l(t, lower)
+            uppers.append(jnp.where(diff >= 0, final, 0.0))
+            lowers.append(lower)
             left.append(final)
             right.append(jnp.where(lane >= 8 * end, final, lower))
         if window < n:
@@ -121,6 +122,7 @@
             keep = (lane < 8 * g) | (lane >= 8 * end)
             for i in range(window, n):
                 tiles[i] = jnp.where(keep, tiles[i], 0.0) - change[8 * i : 8 * i + 8]
+    return jnp.concatenate(uppers, 0), jnp.concatenate(lowers, 0)
 
 
 def half_norms(x):
@@ -159,60 +161,48 @@
     x_ref[pl.ds(at, piece), :] = value
 
 
-def factor_panels(a_ref, u_ref, wh_ref, wl_ref, inv_ref, row0, count, block):
+def factor_panels(a_ref, u_ref, wh_ref, wl_ref, row0, count, block):
     n = a_ref.shape[1]
-
-    def panel(p, carry):
-        r = pl.multiple_of(p * NB, NB)
-        o = pl.multiple_of(row0 + p * NB, NB)
-        d = a_ref[pl.ds(r, NB), pl.ds(o, NB)]
-
-        def store_u(t, v):
-            u_ref[pl.ds(pl.multiple_of(r + 8 * t, 8), 8), pl.ds(o, NB)] = v
-
-        def store_l(t, v):
-            inv_ref[8 * t : 8 * t + 8, :] = v
-
-        factor_block([d[8 * t : 8 * t + 8] for t in range(NB // 8)], store_u, store_l)
-        for k in range(count):
-
-            @pl.when(p == k)
-            def _():
-                lr = k * NB
-                rows = slice(lr, lr + NB)
-                s = row0 + lr
-                e = s + NB
-                ih, il = split(inv_ref[...])
-                parts = ([a_ref[rows, :s]] if s else []) + ([a_ref[rows, e:]] if e < n else [])
-                row = dot_nn(ih, il, *split(jnp.concatenate(parts, 1)))
-                hi, lo = split(row)
-                for w_ref, w, diag in ((wh_ref, hi, ih), (wl_ref, lo, il)):
-                    if s:
-                        w_ref[rows, :s] = w[:, :s]
-                    w_ref[rows, s:e] = diag
-                    end = (s // block + 1) * block
-                    if e < end:
-                        w_ref[rows, e:end] = jnp.zeros((NB, end - e), bf16)
-                if e < n:
-                    u_ref[rows, e:] = row[:, s:]
-                    right_h = jnp.concatenate(([hi[:, :s]] if s else []) + [ih, hi[:, s:]], 1)
-                    right_l = jnp.concatenate(([lo[:, :s]] if s else []) + [il, lo[:, s:]], 1)
-                    for i in range(0, n - e, UPDATE_ROWS):
-                        f = min(i + UPDATE_ROWS, n - e)
-                        change = dot_tn(hi[:, s + i : s + f], lo[:, s + i : s + f], right_h, right_l)
-                        q = slice(lr + NB + i, lr + NB + f)
-                        if s:
-                            a_ref[q, :s] = a_ref[q, :s] - change[:, :s]
-                        a_ref[q, s:e] = -change[:, s:e]
-                        a_ref[q, e:] = a_ref[q, e:] - change[:, e:]
-
-        return carry
-
-    lax.fori_loop(0, count, panel, 0)
+    for p in range(count):
+        rows = slice(p * NB, (p + 1) * NB)
+        s = row0 + p * NB
+        e = s + NB
+        d = a_ref[rows, s:e]
+        upper, lower = factor_block([d[8 * t : 8 * t + 8] for t in range(NB // 8)])
+        u_ref[rows, s:e] = upper
+        ih, il = split(lower)
+        parts = ([a_ref[rows, :s]] if s else []) + ([a_ref[rows, e:]] if e < n else [])
+        row = dot_nn(ih, il, *split(jnp.concatenate(parts, 1)))
+        hi, lo = split(row)
+        for w_ref, w, diag in ((wh_ref, hi, ih), (wl_ref, lo, il)):
+            if s:
+                w_ref[rows, :s] = w[:, :s]
+            w_ref[rows, s:e] = diag
+            end = (s // block + 1) * block
+            if e < end:
+                w_ref[rows, e:end] = jnp.zeros((NB, end - e), bf16)
+        if e == n:
+            break
+        u_ref[rows, e:] = row[:, s:]
+        done_h = jnp.concatenate(([hi[:, :s]] if s else []) + [ih], 1)
+        done_l = jnp.concatenate(([lo[:, :s]] if s else []) + [il], 1)
+        for i in range(0, n - e, UPDATE_ROWS):
+            f = min(i + UPDATE_ROWS, n - e)
+            change = dot_tn(
+                hi[:, s + i : s + f],
+                lo[:, s + i : s + f],
+                jnp.concatenate([done_h, hi[:, s + i :]], 1),
+                jnp.concatenate([done_l, lo[:, s + i :]], 1),
+            )
+            q = slice((p + 1) * NB + i, (p + 1) * NB + f)
+            if s:
+                a_ref[q, :s] = a_ref[q, :s] - change[:, :s]
+            a_ref[q, s:e] = -change[:, s:e]
+            a_ref[q, e + i :] = a_ref[q, e + i :] - change[:, e:]
 
 
 def first_kernel(at_ref, amp_ref, mine_ref, other_ref, nz_ref, *refs):
-    x_ref, sq_ref, u_ref, wh_ref, wl_ref, rest_ref, a_ref, inv_ref, col_ref = refs
+    x_ref, sq_ref, u_ref, wh_ref, wl_ref, rest_ref, a_ref, col_ref = refs
     n = a_ref.shape[0]
     steps, panels, piece = mine_ref.shape[:3]
     block = n // panels
@@ -232,14 +222,14 @@
         row = noise[o // block : o // block + 1, o % block : o % block + WB]
         a_ref[o : o + WB, o : o + WB] = k[:, :WB] + jnp.where(diagonal(WB), jnp.broadcast_to(row, (WB, WB)), 0.0)
     count = u_ref.shape[0] // NB
-    factor_panels(a_ref, u_ref, wh_ref, wl_ref, inv_ref, 0, count, block)
+    factor_panels(a_ref, u_ref, wh_ref, wl_ref, 0, count, block)
     rest_ref[...] = a_ref[count * NB :, :]
 
 
-def second_kernel(rest_ref, u_ref, wh_ref, wl_ref, a_ref, inv_ref):
+def second_kernel(rest_ref, u_ref, wh_ref, wl_ref, a_ref):
     n1, n = rest_ref.shape
     a_ref[...] = rest_ref[...]
-    factor_panels(a_ref, u_ref, wh_ref, wl_ref, inv_ref, n - n1, n1 // NB, n // PANELS)
+    factor_panels(a_ref, u_ref, wh_ref, wl_ref, n - n1, n1 // NB, n // PANELS)
 
 
 def store_block(out_ref, a, b, row, ncols, value):
@@ -410,7 +400,6 @@
     n1 = n - first
     params = pltpu.CompilerParams(vmem_limit_bytes=GRANT)
     cost = pl.CostEstimate(flops=20_000_000_000, bytes_accessed=8_000_000, transcendentals=0)
-    square = pltpu.VMEM((NB, NB), f32)
 
     def factor_shapes(rows):
         half = jax.ShapeDtypeStruct((rows, n), bf16)
@@ -423,7 +412,7 @@
         + [jax.ShapeDtypeStruct((n1, n), f32)],
         in_specs=[SMEM, SMEM, VMEM, VMEM, VMEM],
         out_specs=[VMEM] * 6,
-        scratch_shapes=[pltpu.VMEM((n, n), f32), square, pltpu.VMEM((n, NB), f32)],
+        scratch_shapes=[pltpu.VMEM((n, n), f32), pltpu.VMEM((n, NB), f32)],
         compiler_params=params,
         cost_estimate=pl.CostEstimate(flops=1_000_000, bytes_accessed=1_000_000, transcendentals=0),
         name="first",
@@ -435,7 +424,7 @@
         out_shape=factor_shapes(n1),
         in_specs=[VMEM],
         out_specs=[VMEM] * 3,
-        scratch_shapes=[pltpu.VMEM((n1, n), f32), square],
+        scratch_shapes=[pltpu.VMEM((n1, n), f32)],
         compiler_params=params,
         cost_estimate=cost,
         name="second",

time: 72.5 us -> 69.1 us (0.953)
  Pallas kernels: 43.3 us -> 39.9 us
    pallas_call x1, Pallas kernels: 8.5 us -> 5.25 us  [local(): pl.pallas_call(second_kernel, out_shape=factor_shapes(n1), in_specs=[VMEM...]
  transfers between devices with their start and end apart: 14 -> 14, of which waited for: 4 -> 4; matrix products, arithmetic and copies ran while one was open for 3% -> 3% of each run, Pallas kernels for 39% -> 36%
where the time goes in v7:
time: 69.1 us; the launch traced here: 68.9 us
  Pallas kernels  39.9 us (58%)
  starting transfers between devices  15 us (22%)
  waiting for transfers between devices  10.1 us (15%)
  other arithmetic  2.2 us (3%)
  between operations  0.86 us (1%)
  local copies, waits for them, and re-layouts  0.82 us (1%)
    pallas_call x1, Pallas kernels, local(): pl.pallas_call(first_kernel, out_shape=[jax.ShapeDtypeStruct((n, width),...  19.8 us
    ppermute x14, starting transfers between devices, exchange(): lax.ppermute(x, axis, [(i, i ^ k) for i in range(lax.axis_size(axis))])  15 us
    pallas_call x1, Pallas kernels, local(): pl.pallas_call(bulk_kernel, out_shape=jax.ShapeDtypeStruct((nrows * block...  14.9 us
    ppermute x14, waiting for transfers between devices, exchange(): lax.ppermute(x, axis, [(i, i ^ k) for i in range(lax.axis_size(axis))])  10.1 us
    pallas_call x1, Pallas kernels, local(): pl.pallas_call(second_kernel, out_shape=factor_shapes(n1), in_specs=[VMEM...  5.25 us
  transfers between devices with their start and end apart: 14, of which 4 were waited for; matrix products, arithmetic and copies ran while one was open for 3% of the time, Pallas kernels for 36%

profile of v7, /device:TPU:31, one launch (start us, length us, event | category | flops | bytes accessed | tf_op | source)
XLA Modules:
  0.0 68.9 jit_solution(8124702674594550663)
XLA Ops:
  0.0 0.3 collective-permute-start.2
  0.3 0.2 collective-permute-start.1
  0.5 2.2 %collective-permute-start = (bf16[2,64,512]{2,1,0:T(8,128)(2,1)}, bf16[2,64,512]{2,1,0:T(8,128)(2,1)S(1)}, u32[]{:S(2)}, u32[]{:S(2)}) collective-permute-start(bf16[2,64,512]{2,1,0:T(8,128)(2,1)} %bitcast.57), channel_id=1, source_target_pairs={{0,24},{8,16},{16,8},{24,0},{1,25},{9,17},{17,9},{25,1},{2,26},{10... | collective-permute-start | bytes 393224 | tf_op jit(solution)/shard_map/ppermute | solution.py:356
  2.7 0.0 copy-start
  2.7 0.7 %copy.7 = f32[2,1,512]{2,0,1:T(2,128)S(1)} copy(f32[2,1,512]{2,1,0:T(1,128)} %param.5) | data formatting | bytes 8192
  3.4 0.1 pad_add_fusion.at_ref
  3.5 1.1 %collective-permute-done.2 = bf16[2,64,512]{2,1,0:T(8,128)(2,1)S(1)} collective-permute-done((bf16[2,64,512]{2,1,0:T(8,128)(2,1)}, bf16[2,64,512]{2,1,0:T(8,128)(2,1)S(1)}, u32[]{:S(2)}, u32[]{:S(2)}) %collective-permute-start.2) | collective-permute-done | bytes 131104 | tf_op jit(solution)/shard_map/ppermute | solution.py:356
  4.6 0.1 collective-permute-done.1
  4.6 2.7 %collective-permute-done = bf16[2,64,512]{2,1,0:T(8,128)(2,1)S(1)} collective-permute-done((bf16[2,64,512]{2,1,0:T(8,128)(2,1)}, bf16[2,64,512]{2,1,0:T(8,128)(2,1)S(1)}, u32[]{:S(2)}, u32[]{:S(2)}) %collective-permute-start) | collective-permute-done | bytes 131104 | tf_op jit(solution)/shard_map/ppermute | solution.py:356
  7.3 0.9 %fusion.5 = (bf16[1,64,512]{2,1,0:T(8,128)(2,1)S(1)}, bf16[1,64,512]{2,1,0:T(8,128)(2,1)S(1)}) fusion(pred[]{:T(512)S(6)} %eq.26, pred[]{:T(512)S(6)} %eq.25, pred[]{:T(512)S(6)} %eq.24, bf16[2,64,512]{2,1,0:T(8,128)(2,1)S(1)} %collective-permute-done.2, bf16[2,64,512]{2,1,0:T(8,128)(2,1)S(1)} %collective-permute-done.1, ...), kind=kLoop, calls=%fused_computation.19 | loop fusion | flops 196608 | bytes 393222 | tf_op jit(solution)/shard_map/jit(_where)/select_n | solution.py:362
  8.2 0.2 collective-permute-start.3
  8.5 1.1 %collective-permute-start.5 = (bf16[2,64,512]{2,1,0:T(8,128)(2,1)S(1)}, bf16[2,64,512]{2,1,0:T(8,128)(2,1)S(1)}, u32[]{:S(2)}, u32[]{:S(2)}) collective-permute-start(bf16[2,64,512]{2,1,0:T(8,128)(2,1)S(1)} %pad_maximum_fusion.7), channel_id=1, source_target_pairs={{0,6},{1,7},{2,4},{3,5},{4,2},{5,3},{6,0},{7,1},{8,14},{9,15},{10,... | collective-permute-start | bytes 393224 | tf_op jit(solution)/shard_map/ppermute | solution.py:356
  9.5 1.4 %collective-permute-start.4 = (bf16[2,64,512]{2,1,0:T(8,128)(2,1)S(1)}, bf16[2,64,512]{2,1,0:T(8,128)(2,1)S(1)}, u32[]{:S(2)}, u32[]{:S(2)}) collective-permute-start(bf16[2,64,512]{2,1,0:T(8,128)(2,1)S(1)} %pad_maximum_fusion.7), channel_id=1, source_target_pairs={{0,4},{1,5},{2,6},{3,7},{4,0},{5,1},{6,2},{7,3},{8,12},{9,13},{10,... | collective-permute-start | bytes 393224 | tf_op jit(solution)/shard_map/ppermute | solution.py:356
  11.6 0.2 collective-permute-start.9
  11.8 1.2 %collective-permute-start.8 = (f32[2,512]{1,0:T(2,128)S(1)}, f32[2,512]{1,0:T(2,128)S(1)}, u32[]{:S(2)}, u32[]{:S(2)}) collective-permute-start(f32[2,512]{1,0:T(2,128)S(1)} %bitcast.51), channel_id=1, source_target_pairs={{0,16},{8,24},{16,0},{24,8},{1,17},{9,25},{17,1},{25,9},{2,18},{10... | collective-permute-start | bytes 12296 | tf_op jit(solution)/shard_map/ppermute | solution.py:356
  13.1 1.0 %pad_maximum_fusion.1 = bf16[4,2,64,512]{3,2,1,0:T(8,128)(2,1)S(1)} fusion(bf16[1,2,64,512]{3,2,1,0:T(8,128)(2,1)S(1)} %bitcast.63, bf16[1,2,64,512]{3,2,1,0:T(8,128)(2,1)S(1)} %bitcast.62, bf16[1,2,64,512]{3,2,1,0:T(8,128)(2,1)S(1)} %bitcast.61, bf16[1,2,64,512]{3,2,1,0:T(8,128)(2,1)} %bitcast.58), kind=kLoop, calls=%fused_computation.1 | loop fusion | flops 786432 | bytes 1048576 | tf_op jit(solution)/shard_map/stack | solution.py:381
  14.0 0.0 collective-permute-done.3
  14.0 1.4 %collective-permute-start.7 = (f32[2,512]{1,0:T(2,128)S(1)}, f32[2,512]{1,0:T(2,128)S(1)}, u32[]{:S(2)}, u32[]{:S(2)}) collective-permute-start(f32[2,512]{1,0:T(2,128)S(1)} %bitcast.52), channel_id=1, source_target_pairs={{0,24},{8,16},{16,8},{24,0},{1,25},{9,17},{17,9},{25,1},{2,26},{10... | collective-permute-start | bytes 12296 | tf_op jit(solution)/shard_map/ppermute | solution.py:356
  15.4 0.0 collective-permute-done.5
  15.4 6.2 %collective-permute-done.4 = bf16[2,64,512]{2,1,0:T(8,128)(2,1)S(1)} collective-permute-done((bf16[2,64,512]{2,1,0:T(8,128)(2,1)S(1)}, bf16[2,64,512]{2,1,0:T(8,128)(2,1)S(1)}, u32[]{:S(2)}, u32[]{:S(2)}) %collective-permute-start.4) | collective-permute-done | bytes 131104 | tf_op jit(solution)/shard_map/ppermute | solution.py:356
  21.6 0.1 pad_maximum_fusion.2.mine_ref
  21.7 2.3 %collective-permute-start.6 = (bf16[4,2,64,512]{3,2,1,0:T(8,128)(2,1)S(1)}, bf16[4,2,64,512]{3,2,1,0:T(8,128)(2,1)S(1)}, u32[]{:S(2)}, u32[]{:S(2)}) collective-permute-start(bf16[4,2,64,512]{3,2,1,0:T(8,128)(2,1)S(1)} %pad_maximum_fusion.2.mine_ref), channel_id=1, source_target_pairs={{0,1},{1,0},{2,3},{3,2},{4,5},{5,4},{6,7},{7,6},{8,9},{9,8},{10,11... | collective-permute-start | bytes 1572872 | tf_op jit(solution)/shard_map/ppermute | solution.py:356
  24.0 0.0 copy-done
  24.0 0.1 fusion.3
  24.1 1.0 %collective-permute-start.12 = (bf16[4,64,512]{2,1,0:T(8,128)(2,1)S(1)}, bf16[4,64,512]{2,1,0:T(8,128)(2,1)S(1)}, u32[]{:S(2)}, u32[]{:S(2)}) collective-permute-start(bf16[4,64,512]{2,1,0:T(8,128)(2,1)S(1)} %get-tuple-element.51), channel_id=1, source_target_pairs={{0,6},{1,7},{2,4},{3,5},{4,2},{5,3},{6,0},{7,1},{8,14},{9,15},{10,... | collective-permute-start | bytes 786440 | tf_op jit(solution)/shard_map/ppermute | solution.py:356
  25.1 0.0 collective-permute-done.9
  25.1 0.0 collective-permute-start.10
  25.1 0.0 collective-permute-done.8
  25.1 2.6 %collective-permute-start.11 = (bf16[4,64,512]{2,1,0:T(8,128)(2,1)S(1)}, bf16[4,64,512]{2,1,0:T(8,128)(2,1)S(1)}, u32[]{:S(2)}, u32[]{:S(2)}) collective-permute-start(bf16[4,64,512]{2,1,0:T(8,128)(2,1)S(1)} %get-tuple-element.53), channel_id=1, source_target_pairs={{0,4},{1,5},{2,6},{3,7},{4,0},{5,1},{6,2},{7,3},{8,12},{9,13},{10,... | collective-permute-start | bytes 786440 | tf_op jit(solution)/shard_map/ppermute | solution.py:356
  27.7 0.0 collective-permute-done.7
  27.7 0.0 collective-permute-done.6.other_ref
  27.7 19.8 %first.1 = (bf16[1024,512]{1,0:T(8,128)(2,1)S(1)}, f32[8,1024]{1,0:T(8,128)S(1)}, f32[768,1024]{1,0:T(8,128)S(1)}, bf16[768,1024]{1,0:T(8,128)(2,1)S(1)}, bf16[7...) custom-call(s32[4]{0:T(128)S(1)} %pad_add_fusion.at_ref, f32[1]{0:T(128)S(6)} %copy.8.amp_ref, ...), custom_call_target="tpu_custom_call" | custom-call | flops 1000000 | bytes 1000000 | tf_op jit(solution)/shard_map/first/pallas_call | solution.py:408
  47.6 0.0 collective-permute-done.12.refs_12_
  47.6 0.0 collective-permute-done.10.refs_10_
  47.6 0.0 collective-permute-done.11.refs_11_
  47.7 0.1 pad_maximum_fusion
  47.8 0.9 %collective-permute-start.13 = (bf16[4,3,64,512]{3,2,1,0:T(8,128)(2,1)S(1)}, bf16[4,3,64,512]{3,2,1,0:T(8,128)(2,1)S(1)}, u32[]{:S(2)}, u32[]{:S(2)}) collective-permute-start(bf16[4,3,64,512]{3,2,1,0:T(8,128)(2,1)S(1)} %pad_maximum_fusion), channel_id=1, source_target_pairs={{0,1},{1,0},{2,3},{3,2},{4,5},{5,4},{6,7},{7,6},{8,9},{9,8},{10,11... | collective-permute-start | bytes 2359304 | tf_op jit(solution)/shard_map/ppermute | solution.py:356
  48.7 5.3 %second.1 = (f32[256,1024]{1,0:T(8,128)S(1)}, bf16[256,1024]{1,0:T(8,128)(2,1)S(1)}, bf16[256,1024]{1,0:T(8,128)(2,1)S(1)}) custom-call(f32[256,1024]{1,0:T(8,128)S(1)} %get-tuple-element.33.rest_ref), custom_call_target="tpu_custom_call" | custom-call | flops 20000000000 | bytes 8000000 | tf_op jit(solution)/shard_map/second/pallas_call | solution.py:422
  54.0 0.0 collective-permute-done.13.refs_13_
  54.0 14.9 %bulk.1 = f32[4096,128]{1,0:T(8,128)} custom-call(s32[4]{0:T(128)S(1)} %pad_add_fusion.at_ref, f32[1]{0:T(128)S(6)} %copy.8.amp_ref, bf16[1024,512]{1,0:T(8,128)(2,1)S(1)} %get-tuple-element.26.refs_0_, f32[8,1024]{1,0:T(8,128)S(1)} %get-tuple-element.27.refs_1_, f32[768,1024]{1,0:T(8,128)S(1)} %get-tuple-element.28.refs_2_, ...), custom_call_target="tpu_custom_call" | custom-call | flops 20000000000 | bytes 8000000 | tf_op jit(solution)/shard_map/bulk/pallas_call | solution.py:434
  (6 shorter events, 0.1 us)
Async XLA Ops:
  0.0 4.6 %collective-permute-start.2 = (bf16[2,64,512]{2,1,0:T(8,128)(2,1)}, bf16[2,64,512]{2,1,0:T(8,128)(2,1)S(1)}, u32[]{:S(2)}, u32[]{:S(2)}) collective-permute-start(bf16[2,64,512]{2,1,0:T(8,128)(2,1)} %bitcast.55), channel_id=1, source_target_pairs={{0,8},{8,0},{16,24},{24,16},{1,9},{9,1},{17,25},{25,17},{2,10},{10... | collective-permute-start | bytes 393224 | tf_op jit(solution)/shard_map/ppermute | solution.py:356
  0.3 4.4 %collective-permute-start.1 = (bf16[2,64,512]{2,1,0:T(8,128)(2,1)}, bf16[2,64,512]{2,1,0:T(8,128)(2,1)S(1)}, u32[]{:S(2)}, u32[]{:S(2)}) collective-permute-start(bf16[2,64,512]{2,1,0:T(8,128)(2,1)} %bitcast.56), channel_id=1, source_target_pairs={{0,16},{8,24},{16,0},{24,8},{1,17},{9,25},{17,1},{25,9},{2,18},{10... | collective-permute-start | bytes 393224 | tf_op jit(solution)/shard_map/ppermute | solution.py:356
  0.5 6.8 %collective-permute-start = (bf16[2,64,512]{2,1,0:T(8,128)(2,1)}, bf16[2,64,512]{2,1,0:T(8,128)(2,1)S(1)}, u32[]{:S(2)}, u32[]{:S(2)}) collective-permute-start(bf16[2,64,512]{2,1,0:T(8,128)(2,1)} %bitcast.57), channel_id=1, source_target_pairs={{0,24},{8,16},{16,8},{24,0},{1,25},{9,17},{17,9},{25,1},{2,26},{10... | collective-permute-start | bytes 393224 | tf_op jit(solution)/shard_map/ppermute | solution.py:356
  2.7 21.3 %copy-start = (bf16[2,1,64,512]{3,2,1,0:T(8,128)(2,1)S(1)}, bf16[2,1,64,512]{3,2,1,0:T(8,128)(2,1)}, u32[]{:S(2)}) copy-start(bf16[2,1,64,512]{3,2,1,0:T(8,128)(2,1)} %param.3) | copy-start | bytes 393220
  8.2 5.8 %collective-permute-start.3 = (bf16[2,64,512]{2,1,0:T(8,128)(2,1)S(1)}, bf16[2,64,512]{2,1,0:T(8,128)(2,1)S(1)}, u32[]{:S(2)}, u32[]{:S(2)}) collective-permute-start(bf16[2,64,512]{2,1,0:T(8,128)(2,1)S(1)} %pad_maximum_fusion.7), channel_id=1, source_target_pairs={{0,2},{1,3},{2,0},{3,1},{4,6},{5,7},{6,4},{7,5},{8,10},{9,11},{10,... | collective-permute-start | bytes 393224 | tf_op jit(solution)/shard_map/ppermute | solution.py:356
  8.5 7.0 %collective-permute-start.5 = (bf16[2,64,512]{2,1,0:T(8,128)(2,1)S(1)}, bf16[2,64,512]{2,1,0:T(8,128)(2,1)S(1)}, u32[]{:S(2)}, u32[]{:S(2)}) collective-permute-start(bf16[2,64,512]{2,1,0:T(8,128)(2,1)S(1)} %pad_maximum_fusion.7), channel_id=1, source_target_pairs={{0,6},{1,7},{2,4},{3,5},{4,2},{5,3},{6,0},{7,1},{8,14},{9,15},{10,... | collective-permute-start | bytes 393224 | tf_op jit(solution)/shard_map/ppermute | solution.py:356
  9.5 12.1 %collective-permute-start.4 = (bf16[2,64,512]{2,1,0:T(8,128)(2,1)S(1)}, bf16[2,64,512]{2,1,0:T(8,128)(2,1)S(1)}, u32[]{:S(2)}, u32[]{:S(2)}) collective-permute-start(bf16[2,64,512]{2,1,0:T(8,128)(2,1)S(1)} %pad_maximum_fusion.7), channel_id=1, source_target_pairs={{0,4},{1,5},{2,6},{3,7},{4,0},{5,1},{6,2},{7,3},{8,12},{9,13},{10,... | collective-permute-start | bytes 393224 | tf_op jit(solution)/shard_map/ppermute | solution.py:356
  11.6 13.4 %collective-permute-start.9 = (f32[2,512]{1,0:T(2,128)S(1)}, f32[2,512]{1,0:T(2,128)S(1)}, u32[]{:S(2)}, u32[]{:S(2)}) collective-permute-start(f32[2,512]{1,0:T(2,128)S(1)} %bitcast.50), channel_id=1, source_target_pairs={{0,8},{8,0},{16,24},{24,16},{1,9},{9,1},{17,25},{25,17},{2,10},{10... | collective-permute-start | bytes 12296 | tf_op jit(solution)/shard_map/ppermute | solution.py:356
  11.8 13.2 %collective-permute-start.8 = (f32[2,512]{1,0:T(2,128)S(1)}, f32[2,512]{1,0:T(2,128)S(1)}, u32[]{:S(2)}, u32[]{:S(2)}) collective-permute-start(f32[2,512]{1,0:T(2,128)S(1)} %bitcast.51), channel_id=1, source_target_pairs={{0,16},{8,24},{16,0},{24,8},{1,17},{9,25},{17,1},{25,9},{2,18},{10... | collective-permute-start | bytes 12296 | tf_op jit(solution)/shard_map/ppermute | solution.py:356
  14.0 13.7 %collective-permute-start.7 = (f32[2,512]{1,0:T(2,128)S(1)}, f32[2,512]{1,0:T(2,128)S(1)}, u32[]{:S(2)}, u32[]{:S(2)}) collective-permute-start(f32[2,512]{1,0:T(2,128)S(1)} %bitcast.52), channel_id=1, source_target_pairs={{0,24},{8,16},{16,8},{24,0},{1,25},{9,17},{17,9},{25,1},{2,26},{10... | collective-permute-start | bytes 12296 | tf_op jit(solution)/shard_map/ppermute | solution.py:356
  21.7 6.1 %collective-permute-start.6 = (bf16[4,2,64,512]{3,2,1,0:T(8,128)(2,1)S(1)}, bf16[4,2,64,512]{3,2,1,0:T(8,128)(2,1)S(1)}, u32[]{:S(2)}, u32[]{:S(2)}) collective-permute-start(bf16[4,2,64,512]{3,2,1,0:T(8,128)(2,1)S(1)} %pad_maximum_fusion.2.mine_ref), channel_id=1, source_target_pairs={{0,1},{1,0},{2,3},{3,2},{4,5},{5,4},{6,7},{7,6},{8,9},{9,8},{10,11... | collective-permute-start | bytes 1572872 | tf_op jit(solution)/shard_map/ppermute | solution.py:356
  24.1 23.5 %collective-permute-start.12 = (bf16[4,64,512]{2,1,0:T(8,128)(2,1)S(1)}, bf16[4,64,512]{2,1,0:T(8,128)(2,1)S(1)}, u32[]{:S(2)}, u32[]{:S(2)}) collective-permute-start(bf16[4,64,512]{2,1,0:T(8,128)(2,1)S(1)} %get-tuple-element.51), channel_id=1, source_target_pairs={{0,6},{1,7},{2,4},{3,5},{4,2},{5,3},{6,0},{7,1},{8,14},{9,15},{10,... | collective-permute-start | bytes 786440 | tf_op jit(solution)/shard_map/ppermute | solution.py:356
  25.1 22.5 %collective-permute-start.10 = (bf16[4,64,512]{2,1,0:T(8,128)(2,1)S(1)}, bf16[4,64,512]{2,1,0:T(8,128)(2,1)S(1)}, u32[]{:S(2)}, u32[]{:S(2)}) collective-permute-start(bf16[4,64,512]{2,1,0:T(8,128)(2,1)S(1)} %get-tuple-element.52), channel_id=1, source_target_pairs={{0,2},{1,3},{2,0},{3,1},{4,6},{5,7},{6,4},{7,5},{8,10},{9,11},{10,... | collective-permute-start | bytes 786440 | tf_op jit(solution)/shard_map/ppermute | solution.py:356
  25.1 22.5 %collective-permute-start.11 = (bf16[4,64,512]{2,1,0:T(8,128)(2,1)S(1)}, bf16[4,64,512]{2,1,0:T(8,128)(2,1)S(1)}, u32[]{:S(2)}, u32[]{:S(2)}) collective-permute-start(bf16[4,64,512]{2,1,0:T(8,128)(2,1)S(1)} %get-tuple-element.53), channel_id=1, source_target_pairs={{0,4},{1,5},{2,6},{3,7},{4,0},{5,1},{6,2},{7,3},{8,12},{9,13},{10,... | collective-permute-start | bytes 786440 | tf_op jit(solution)/shard_map/ppermute | solution.py:356
  47.8 6.2 %collective-permute-start.13 = (bf16[4,3,64,512]{3,2,1,0:T(8,128)(2,1)S(1)}, bf16[4,3,64,512]{3,2,1,0:T(8,128)(2,1)S(1)}, u32[]{:S(2)}, u32[]{:S(2)}) collective-permute-start(bf16[4,3,64,512]{3,2,1,0:T(8,128)(2,1)S(1)} %pad_maximum_fusion), channel_id=1, source_target_pairs={{0,1},{1,0},{2,3},{3,2},{4,5},{5,4},{6,7},{7,6},{8,9},{9,8},{10,11... | collective-permute-start | bytes 2359304 | tf_op jit(solution)/shard_map/ppermute | solution.py:356

commit v8 on v7

--- a/solution.py
+++ b/solution.py
@@ -277,10 +277,12 @@
         cross = lax.dot_general(x, x_ref[...], TRANS_B, preferred_element_type=f32)
         return split(jnp.exp(cross - widen(col, n) - lead_sq))
 
-    for a in range(nrows):
-        rows = slice(a * block, (a + 1) * block)
-        col_ref[rows, :] = half_norm_col(r_ref[rows, :])
-        kh_ref[rows, :], kl_ref[rows, :] = entries(r_ref[rows, :], col_ref[rows, :])
+    def row_entries():
+        for a in range(nrows):
+            rows = slice(a * block, (a + 1) * block)
+            col_ref[rows, :] = half_norm_col(r_ref[rows, :])
+            kh_ref[rows, :], kl_ref[rows, :] = entries(r_ref[rows, :], col_ref[rows, :])
+
     for b in range(ncols):
         j = b * col_n + me
         cols = slice(b * block, (b + 1) * block)
@@ -291,6 +293,7 @@
             col_sq, col = half_norms(xc)
             col_sq = col_sq - log_row(amp_ref[0], block)
             zh_ref[...], zl_ref[...] = entries(xc, col)
+            row_entries()
             for s in range(0, n, block):
                 e = s + block
                 panel = dot_nt(zh_ref[:, :e], zl_ref[:, :e], *inverse(s, e, 0, e))
@@ -302,50 +305,54 @@
             for a in range(nrows):
                 i = a * row_n + row_at
                 rows = slice(a * block, (a + 1) * block)
-
-                @pl.when(i >= PANELS)
-                def _():
-                    xr = r_ref[rows, :]
-                    cross = lax.dot_general(xr, xc, TRANS_B, preferred_element_type=f32)
-                    k = jnp.exp(cross - widen(col_ref[rows, :], block) - col_sq)
-                    on_diag = diagonal(block) & (i == j)
-                    k = k + jnp.where(on_diag, jnp.broadcast_to(nz_ref[a : a + 1, :], (block, block)), 0.0)
-                    k = k - dot_nt(kh_ref[rows, :], kl_ref[rows, :], zh_ref[...], zl_ref[...])
-                    store_block(out_ref, a, b, 0, ncols, k)
-
-                @pl.when(i < PANELS)
-                def _():
-                    store_block(out_ref, a, b, 0, ncols, jnp.zeros((block, block), f32))
+                cross = lax.dot_general(r_ref[rows, :], xc, TRANS_B, preferred_element_type=f32)
+                k = jnp.exp(cross - widen(col_ref[rows, :], block) - col_sq)
+                on_diag = diagonal(block) & (i == j)
+                k = k + jnp.where(on_diag, jnp.broadcast_to(nz_ref[a : a + 1, :], (block, block)), 0.0)
+                k = k - dot_nt(kh_ref[rows, :], kl_ref[rows, :], zh_ref[...], zl_ref[...])
+                store_block(out_ref, a, b, 0, ncols, jnp.where(i >= PANELS, k, 0.0))
 
         if b:
             continue
+
+        @pl.when(j < PANELS)
+        def _():
+            def some_entries(step, carry):
+                o = pl.multiple_of(step * WB, WB)
+                x = r_ref[pl.ds(o, WB), :]
+                kh_ref[pl.ds(o, WB), :], kl_ref[pl.ds(o, WB), :] = entries(x, half_norm_col(x))
+                return carry
+
+            lax.fori_loop(0, nrows * block // WB, some_entries, 0)
+
         for s in range(PANELS):
             w = s * block
-            for a in range(nrows):
-                i = a * row_n + row_at
-                rows = slice(a * block, (a + 1) * block)
-
-                @pl.when((j == s) & (i >= PANELS))
+            e = w + block
+
+            @pl.when(j == s)
+            def _():
+                def some_rows(step, carry):
+                    o = pl.multiple_of(step * WB, WB)
+                    rows = pl.ds(o, WB)
+                    panel = dot_nt(kh_ref[rows, :e], kl_ref[rows, :e], *inverse(w, e, 0, e))
+                    store_block(out_ref, 0, b, o, ncols, panel)
+                    return carry
+
+                lax.fori_loop(0, nrows * block // WB, some_rows, 0)
+
+            for v in range(PANELS):
+
+                @pl.when((j == s) & (row_at == v))
                 def _():
-                    e = w + block
-                    panel = dot_nt(kh_ref[rows, :e], kl_ref[rows, :e], *inverse(w, e, 0, e))
-                    store_block(out_ref, a, b, 0, ncols, panel)
-
-                if a:
-                    continue
-                for v in range(PANELS):
-
-                    @pl.when((j == s) & (i == v))
-                    def _():
-                        if v < s:
-                            u = jnp.zeros((block, block), f32)
-                        else:
-                            u = pick(u0_ref, u1_ref, w, w + block, v * block, (v + 1) * block).T
-                        if v == s:
-                            row_id = lax.broadcasted_iota(jnp.int32, (block, block), 0)
-                            col_id = lax.broadcasted_iota(jnp.int32, (block, block), 1)
-                            u = jnp.where(row_id >= col_id, u, 0.0)
-                        store_block(out_ref, a, b, 0, ncols, u)
+                    if v < s:
+                        u = jnp.zeros((block, block), f32)
+                    else:
+                        u = pick(u0_ref, u1_ref, w, e, v * block, (v + 1) * block).T
+                    if v == s:
+                        row_id = lax.broadcasted_iota(jnp.int32, (block, block), 0)
+                        col_id = lax.broadcasted_iota(jnp.int32, (block, block), 1)
+                        u = jnp.where(row_id >= col_id, u, 0.0)
+                    store_block(out_ref, 0, b, 0, ncols, u)
 
 
 SMEM = pl.BlockSpec(memory_space=pltpu.SMEM)

time: 69.1 us -> 69.6 us (level); the launches traced: 68.9 us -> 68.4 us
  transfers between devices with their start and end apart: 14 -> 14, of which waited for: 4 -> 4; matrix products, arithmetic and copies ran while one was open for 3% -> 3% of each run, Pallas kernels for 36% -> 37%
where the time goes in v8:
time: 69.6 us; the launch traced here: 68.4 us
  Pallas kernels  39.5 us (57%)
  starting transfers between devices  15 us (22%)
  waiting for transfers between devices  10.1 us (15%)
  other arithmetic  2.2 us (3%)
  between operations  0.86 us (1%)
  local copies, waits for them, and re-layouts  0.82 us (1%)
    pallas_call x1, Pallas kernels, local(): pl.pallas_call(first_kernel, out_shape=[jax.ShapeDtypeStruct((n, width),...  19.8 us
    ppermute x14, starting transfers between devices, exchange(): lax.ppermute(x, axis, [(i, i ^ k) for i in range(lax.axis_size(axis))])  15 us
    pallas_call x1, Pallas kernels, local(): pl.pallas_call(bulk_kernel, out_shape=jax.ShapeDtypeStruct((nrows * block...  14.4 us
    ppermute x14, waiting for transfers between devices, exchange(): lax.ppermute(x, axis, [(i, i ^ k) for i in range(lax.axis_size(axis))])  10.1 us
    pallas_call x1, Pallas kernels, local(): pl.pallas_call(second_kernel, out_shape=factor_shapes(n1), in_specs=[VMEM...  5.25 us
  transfers between devices with their start and end apart: 14, of which 4 were waited for; matrix products, arithmetic and copies ran while one was open for 3% of the time, Pallas kernels for 37%

profile of v8, /device:TPU:31, one launch (start us, length us, event | category | flops | bytes accessed | tf_op | source)
XLA Modules:
  0.0 68.4 jit_solution(490645727811116401)
XLA Ops:
  0.0 0.3 collective-permute-start.2
  0.3 0.2 collective-permute-start.1
  0.5 2.2 %collective-permute-start = (bf16[2,64,512]{2,1,0:T(8,128)(2,1)}, bf16[2,64,512]{2,1,0:T(8,128)(2,1)S(1)}, u32[]{:S(2)}, u32[]{:S(2)}) collective-permute-start(bf16[2,64,512]{2,1,0:T(8,128)(2,1)} %bitcast.57), channel_id=1, source_target_pairs={{0,24},{8,16},{16,8},{24,0},{1,25},{9,17},{17,9},{25,1},{2,26},{10... | collective-permute-start | bytes 393224 | tf_op jit(solution)/shard_map/ppermute | solution.py:363
  2.7 0.0 copy-start
  2.7 0.7 %copy.7 = f32[2,1,512]{2,0,1:T(2,128)S(1)} copy(f32[2,1,512]{2,1,0:T(1,128)} %param.5) | data formatting | bytes 8192
  3.4 0.1 pad_add_fusion.at_ref
  3.5 1.1 %collective-permute-done.2 = bf16[2,64,512]{2,1,0:T(8,128)(2,1)S(1)} collective-permute-done((bf16[2,64,512]{2,1,0:T(8,128)(2,1)}, bf16[2,64,512]{2,1,0:T(8,128)(2,1)S(1)}, u32[]{:S(2)}, u32[]{:S(2)}) %collective-permute-start.2) | collective-permute-done | bytes 131104 | tf_op jit(solution)/shard_map/ppermute | solution.py:363
  4.6 0.1 collective-permute-done.1
  4.6 2.7 %collective-permute-done = bf16[2,64,512]{2,1,0:T(8,128)(2,1)S(1)} collective-permute-done((bf16[2,64,512]{2,1,0:T(8,128)(2,1)}, bf16[2,64,512]{2,1,0:T(8,128)(2,1)S(1)}, u32[]{:S(2)}, u32[]{:S(2)}) %collective-permute-start) | collective-permute-done | bytes 131104 | tf_op jit(solution)/shard_map/ppermute | solution.py:363
  7.3 0.9 %fusion.5 = (bf16[1,64,512]{2,1,0:T(8,128)(2,1)S(1)}, bf16[1,64,512]{2,1,0:T(8,128)(2,1)S(1)}) fusion(pred[]{:T(512)S(6)} %eq.26, pred[]{:T(512)S(6)} %eq.25, pred[]{:T(512)S(6)} %eq.24, bf16[2,64,512]{2,1,0:T(8,128)(2,1)S(1)} %collective-permute-done.2, bf16[2,64,512]{2,1,0:T(8,128)(2,1)S(1)} %collective-permute-done.1, ...), kind=kLoop, calls=%fused_computation.19 | loop fusion | flops 196608 | bytes 393222 | tf_op jit(solution)/shard_map/jit(_where)/select_n | solution.py:369
  8.2 0.2 collective-permute-start.3
  8.5 1.1 %collective-permute-start.5 = (bf16[2,64,512]{2,1,0:T(8,128)(2,1)S(1)}, bf16[2,64,512]{2,1,0:T(8,128)(2,1)S(1)}, u32[]{:S(2)}, u32[]{:S(2)}) collective-permute-start(bf16[2,64,512]{2,1,0:T(8,128)(2,1)S(1)} %pad_maximum_fusion.7), channel_id=1, source_target_pairs={{0,6},{1,7},{2,4},{3,5},{4,2},{5,3},{6,0},{7,1},{8,14},{9,15},{10,... | collective-permute-start | bytes 393224 | tf_op jit(solution)/shard_map/ppermute | solution.py:363
  9.5 1.4 %collective-permute-start.4 = (bf16[2,64,512]{2,1,0:T(8,128)(2,1)S(1)}, bf16[2,64,512]{2,1,0:T(8,128)(2,1)S(1)}, u32[]{:S(2)}, u32[]{:S(2)}) collective-permute-start(bf16[2,64,512]{2,1,0:T(8,128)(2,1)S(1)} %pad_maximum_fusion.7), channel_id=1, source_target_pairs={{0,4},{1,5},{2,6},{3,7},{4,0},{5,1},{6,2},{7,3},{8,12},{9,13},{10,... | collective-permute-start | bytes 393224 | tf_op jit(solution)/shard_map/ppermute | solution.py:363
  11.6 0.2 collective-permute-start.9
  11.8 1.2 %collective-permute-start.8 = (f32[2,512]{1,0:T(2,128)S(1)}, f32[2,512]{1,0:T(2,128)S(1)}, u32[]{:S(2)}, u32[]{:S(2)}) collective-permute-start(f32[2,512]{1,0:T(2,128)S(1)} %bitcast.51), channel_id=1, source_target_pairs={{0,16},{8,24},{16,0},{24,8},{1,17},{9,25},{17,1},{25,9},{2,18},{10... | collective-permute-start | bytes 12296 | tf_op jit(solution)/shard_map/ppermute | solution.py:363
  13.1 1.0 %pad_maximum_fusion.1 = bf16[4,2,64,512]{3,2,1,0:T(8,128)(2,1)S(1)} fusion(bf16[1,2,64,512]{3,2,1,0:T(8,128)(2,1)S(1)} %bitcast.63, bf16[1,2,64,512]{3,2,1,0:T(8,128)(2,1)S(1)} %bitcast.62, bf16[1,2,64,512]{3,2,1,0:T(8,128)(2,1)S(1)} %bitcast.61, bf16[1,2,64,512]{3,2,1,0:T(8,128)(2,1)} %bitcast.58), kind=kLoop, calls=%fused_computation.1 | loop fusion | flops 786432 | bytes 1048576 | tf_op jit(solution)/shard_map/stack | solution.py:388
  14.0 0.0 collective-permute-done.3
  14.0 1.4 %collective-permute-start.7 = (f32[2,512]{1,0:T(2,128)S(1)}, f32[2,512]{1,0:T(2,128)S(1)}, u32[]{:S(2)}, u32[]{:S(2)}) collective-permute-start(f32[2,512]{1,0:T(2,128)S(1)} %bitcast.52), channel_id=1, source_target_pairs={{0,24},{8,16},{16,8},{24,0},{1,25},{9,17},{17,9},{25,1},{2,26},{10... | collective-permute-start | bytes 12296 | tf_op jit(solution)/shard_map/ppermute | solution.py:363
  15.4 0.0 collective-permute-done.5
  15.4 6.2 %collective-permute-done.4 = bf16[2,64,512]{2,1,0:T(8,128)(2,1)S(1)} collective-permute-done((bf16[2,64,512]{2,1,0:T(8,128)(2,1)S(1)}, bf16[2,64,512]{2,1,0:T(8,128)(2,1)S(1)}, u32[]{:S(2)}, u32[]{:S(2)}) %collective-permute-start.4) | collective-permute-done | bytes 131104 | tf_op jit(solution)/shard_map/ppermute | solution.py:363
  21.6 0.1 pad_maximum_fusion.2.mine_ref
  21.7 2.3 %collective-permute-start.6 = (bf16[4,2,64,512]{3,2,1,0:T(8,128)(2,1)S(1)}, bf16[4,2,64,512]{3,2,1,0:T(8,128)(2,1)S(1)}, u32[]{:S(2)}, u32[]{:S(2)}) collective-permute-start(bf16[4,2,64,512]{3,2,1,0:T(8,128)(2,1)S(1)} %pad_maximum_fusion.2.mine_ref), channel_id=1, source_target_pairs={{0,1},{1,0},{2,3},{3,2},{4,5},{5,4},{6,7},{7,6},{8,9},{9,8},{10,11... | collective-permute-start | bytes 1572872 | tf_op jit(solution)/shard_map/ppermute | solution.py:363
  24.0 0.0 copy-done
  24.0 0.1 fusion.3
  24.1 1.0 %collective-permute-start.12 = (bf16[4,64,512]{2,1,0:T(8,128)(2,1)S(1)}, bf16[4,64,512]{2,1,0:T(8,128)(2,1)S(1)}, u32[]{:S(2)}, u32[]{:S(2)}) collective-permute-start(bf16[4,64,512]{2,1,0:T(8,128)(2,1)S(1)} %get-tuple-element.51), channel_id=1, source_target_pairs={{0,6},{1,7},{2,4},{3,5},{4,2},{5,3},{6,0},{7,1},{8,14},{9,15},{10,... | collective-permute-start | bytes 786440 | tf_op jit(solution)/shard_map/ppermute | solution.py:363
  25.1 0.0 collective-permute-done.9
  25.1 0.0 collective-permute-start.10
  25.1 0.0 collective-permute-done.8
  25.1 2.6 %collective-permute-start.11 = (bf16[4,64,512]{2,1,0:T(8,128)(2,1)S(1)}, bf16[4,64,512]{2,1,0:T(8,128)(2,1)S(1)}, u32[]{:S(2)}, u32[]{:S(2)}) collective-permute-start(bf16[4,64,512]{2,1,0:T(8,128)(2,1)S(1)} %get-tuple-element.53), channel_id=1, source_target_pairs={{0,4},{1,5},{2,6},{3,7},{4,0},{5,1},{6,2},{7,3},{8,12},{9,13},{10,... | collective-permute-start | bytes 786440 | tf_op jit(solution)/shard_map/ppermute | solution.py:363
  27.7 0.0 collective-permute-done.7
  27.7 0.0 collective-permute-done.6.other_ref
  27.7 19.8 %first.1 = (bf16[1024,512]{1,0:T(8,128)(2,1)S(1)}, f32[8,1024]{1,0:T(8,128)S(1)}, f32[768,1024]{1,0:T(8,128)S(1)}, bf16[768,1024]{1,0:T(8,128)(2,1)S(1)}, bf16[7...) custom-call(s32[4]{0:T(128)S(1)} %pad_add_fusion.at_ref, f32[1]{0:T(128)S(6)} %copy.8.amp_ref, ...), custom_call_target="tpu_custom_call" | custom-call | flops 1000000 | bytes 1000000 | tf_op jit(solution)/shard_map/first/pallas_call | solution.py:415
  47.6 0.0 collective-permute-done.12.refs_12_
  47.6 0.0 collective-permute-done.10.refs_10_
  47.6 0.0 collective-permute-done.11.refs_11_
  47.7 0.1 pad_maximum_fusion
  47.8 0.9 %collective-permute-start.13 = (bf16[4,3,64,512]{3,2,1,0:T(8,128)(2,1)S(1)}, bf16[4,3,64,512]{3,2,1,0:T(8,128)(2,1)S(1)}, u32[]{:S(2)}, u32[]{:S(2)}) collective-permute-start(bf16[4,3,64,512]{3,2,1,0:T(8,128)(2,1)S(1)} %pad_maximum_fusion), channel_id=1, source_target_pairs={{0,1},{1,0},{2,3},{3,2},{4,5},{5,4},{6,7},{7,6},{8,9},{9,8},{10,11... | collective-permute-start | bytes 2359304 | tf_op jit(solution)/shard_map/ppermute | solution.py:363
  48.7 5.3 %second.1 = (f32[256,1024]{1,0:T(8,128)S(1)}, bf16[256,1024]{1,0:T(8,128)(2,1)S(1)}, bf16[256,1024]{1,0:T(8,128)(2,1)S(1)}) custom-call(f32[256,1024]{1,0:T(8,128)S(1)} %get-tuple-element.33.rest_ref), custom_call_target="tpu_custom_call" | custom-call | flops 20000000000 | bytes 8000000 | tf_op jit(solution)/shard_map/second/pallas_call | solution.py:429
  54.0 0.0 collective-permute-done.13.refs_13_
  54.0 14.4 %bulk.1 = f32[4096,128]{1,0:T(8,128)} custom-call(s32[4]{0:T(128)S(1)} %pad_add_fusion.at_ref, f32[1]{0:T(128)S(6)} %copy.8.amp_ref, bf16[1024,512]{1,0:T(8,128)(2,1)S(1)} %get-tuple-element.26.refs_0_, f32[8,1024]{1,0:T(8,128)S(1)} %get-tuple-element.27.refs_1_, f32[768,1024]{1,0:T(8,128)S(1)} %get-tuple-element.28.refs_2_, ...), custom_call_target="tpu_custom_call" | custom-call | flops 20000000000 | bytes 8000000 | tf_op jit(solution)/shard_map/bulk/pallas_call | solution.py:441
  (6 shorter events, 0.1 us)
Async XLA Ops:
  0.0 4.6 %collective-permute-start.2 = (bf16[2,64,512]{2,1,0:T(8,128)(2,1)}, bf16[2,64,512]{2,1,0:T(8,128)(2,1)S(1)}, u32[]{:S(2)}, u32[]{:S(2)}) collective-permute-start(bf16[2,64,512]{2,1,0:T(8,128)(2,1)} %bitcast.55), channel_id=1, source_target_pairs={{0,8},{8,0},{16,24},{24,16},{1,9},{9,1},{17,25},{25,17},{2,10},{10... | collective-permute-start | bytes 393224 | tf_op jit(solution)/shard_map/ppermute | solution.py:363
  0.3 4.4 %collective-permute-start.1 = (bf16[2,64,512]{2,1,0:T(8,128)(2,1)}, bf16[2,64,512]{2,1,0:T(8,128)(2,1)S(1)}, u32[]{:S(2)}, u32[]{:S(2)}) collective-permute-start(bf16[2,64,512]{2,1,0:T(8,128)(2,1)} %bitcast.56), channel_id=1, source_target_pairs={{0,16},{8,24},{16,0},{24,8},{1,17},{9,25},{17,1},{25,9},{2,18},{10... | collective-permute-start | bytes 393224 | tf_op jit(solution)/shard_map/ppermute | solution.py:363
  0.5 6.8 %collective-permute-start = (bf16[2,64,512]{2,1,0:T(8,128)(2,1)}, bf16[2,64,512]{2,1,0:T(8,128)(2,1)S(1)}, u32[]{:S(2)}, u32[]{:S(2)}) collective-permute-start(bf16[2,64,512]{2,1,0:T(8,128)(2,1)} %bitcast.57), channel_id=1, source_target_pairs={{0,24},{8,16},{16,8},{24,0},{1,25},{9,17},{17,9},{25,1},{2,26},{10... | collective-permute-start | bytes 393224 | tf_op jit(solution)/shard_map/ppermute | solution.py:363
  2.7 21.3 %copy-start = (bf16[2,1,64,512]{3,2,1,0:T(8,128)(2,1)S(1)}, bf16[2,1,64,512]{3,2,1,0:T(8,128)(2,1)}, u32[]{:S(2)}) copy-start(bf16[2,1,64,512]{3,2,1,0:T(8,128)(2,1)} %param.3) | copy-start | bytes 393220
  8.2 5.8 %collective-permute-start.3 = (bf16[2,64,512]{2,1,0:T(8,128)(2,1)S(1)}, bf16[2,64,512]{2,1,0:T(8,128)(2,1)S(1)}, u32[]{:S(2)}, u32[]{:S(2)}) collective-permute-start(bf16[2,64,512]{2,1,0:T(8,128)(2,1)S(1)} %pad_maximum_fusion.7), channel_id=1, source_target_pairs={{0,2},{1,3},{2,0},{3,1},{4,6},{5,7},{6,4},{7,5},{8,10},{9,11},{10,... | collective-permute-start | bytes 393224 | tf_op jit(solution)/shard_map/ppermute | solution.py:363
  8.5 7.0 %collective-permute-start.5 = (bf16[2,64,512]{2,1,0:T(8,128)(2,1)S(1)}, bf16[2,64,512]{2,1,0:T(8,128)(2,1)S(1)}, u32[]{:S(2)}, u32[]{:S(2)}) collective-permute-start(bf16[2,64,512]{2,1,0:T(8,128)(2,1)S(1)} %pad_maximum_fusion.7), channel_id=1, source_target_pairs={{0,6},{1,7},{2,4},{3,5},{4,2},{5,3},{6,0},{7,1},{8,14},{9,15},{10,... | collective-permute-start | bytes 393224 | tf_op jit(solution)/shard_map/ppermute | solution.py:363
  9.5 12.1 %collective-permute-start.4 = (bf16[2,64,512]{2,1,0:T(8,128)(2,1)S(1)}, bf16[2,64,512]{2,1,0:T(8,128)(2,1)S(1)}, u32[]{:S(2)}, u32[]{:S(2)}) collective-permute-start(bf16[2,64,512]{2,1,0:T(8,128)(2,1)S(1)} %pad_maximum_fusion.7), channel_id=1, source_target_pairs={{0,4},{1,5},{2,6},{3,7},{4,0},{5,1},{6,2},{7,3},{8,12},{9,13},{10,... | collective-permute-start | bytes 393224 | tf_op jit(solution)/shard_map/ppermute | solution.py:363
  11.6 13.4 %collective-permute-start.9 = (f32[2,512]{1,0:T(2,128)S(1)}, f32[2,512]{1,0:T(2,128)S(1)}, u32[]{:S(2)}, u32[]{:S(2)}) collective-permute-start(f32[2,512]{1,0:T(2,128)S(1)} %bitcast.50), channel_id=1, source_target_pairs={{0,8},{8,0},{16,24},{24,16},{1,9},{9,1},{17,25},{25,17},{2,10},{10... | collective-permute-start | bytes 12296 | tf_op jit(solution)/shard_map/ppermute | solution.py:363
  11.8 13.2 %collective-permute-start.8 = (f32[2,512]{1,0:T(2,128)S(1)}, f32[2,512]{1,0:T(2,128)S(1)}, u32[]{:S(2)}, u32[]{:S(2)}) collective-permute-start(f32[2,512]{1,0:T(2,128)S(1)} %bitcast.51), channel_id=1, source_target_pairs={{0,16},{8,24},{16,0},{24,8},{1,17},{9,25},{17,1},{25,9},{2,18},{10... | collective-permute-start | bytes 12296 | tf_op jit(solution)/shard_map/ppermute | solution.py:363
  14.0 13.7 %collective-permute-start.7 = (f32[2,512]{1,0:T(2,128)S(1)}, f32[2,512]{1,0:T(2,128)S(1)}, u32[]{:S(2)}, u32[]{:S(2)}) collective-permute-start(f32[2,512]{1,0:T(2,128)S(1)} %bitcast.52), channel_id=1, source_target_pairs={{0,24},{8,16},{16,8},{24,0},{1,25},{9,17},{17,9},{25,1},{2,26},{10... | collective-permute-start | bytes 12296 | tf_op jit(solution)/shard_map/ppermute | solution.py:363
  21.7 6.1 %collective-permute-start.6 = (bf16[4,2,64,512]{3,2,1,0:T(8,128)(2,1)S(1)}, bf16[4,2,64,512]{3,2,1,0:T(8,128)(2,1)S(1)}, u32[]{:S(2)}, u32[]{:S(2)}) collective-permute-start(bf16[4,2,64,512]{3,2,1,0:T(8,128)(2,1)S(1)} %pad_maximum_fusion.2.mine_ref), channel_id=1, source_target_pairs={{0,1},{1,0},{2,3},{3,2},{4,5},{5,4},{6,7},{7,6},{8,9},{9,8},{10,11... | collective-permute-start | bytes 1572872 | tf_op jit(solution)/shard_map/ppermute | solution.py:363
  24.1 23.5 %collective-permute-start.12 = (bf16[4,64,512]{2,1,0:T(8,128)(2,1)S(1)}, bf16[4,64,512]{2,1,0:T(8,128)(2,1)S(1)}, u32[]{:S(2)}, u32[]{:S(2)}) collective-permute-start(bf16[4,64,512]{2,1,0:T(8,128)(2,1)S(1)} %get-tuple-element.51), channel_id=1, source_target_pairs={{0,6},{1,7},{2,4},{3,5},{4,2},{5,3},{6,0},{7,1},{8,14},{9,15},{10,... | collective-permute-start | bytes 786440 | tf_op jit(solution)/shard_map/ppermute | solution.py:363
  25.1 22.5 %collective-permute-start.10 = (bf16[4,64,512]{2,1,0:T(8,128)(2,1)S(1)}, bf16[4,64,512]{2,1,0:T(8,128)(2,1)S(1)}, u32[]{:S(2)}, u32[]{:S(2)}) collective-permute-start(bf16[4,64,512]{2,1,0:T(8,128)(2,1)S(1)} %get-tuple-element.52), channel_id=1, source_target_pairs={{0,2},{1,3},{2,0},{3,1},{4,6},{5,7},{6,4},{7,5},{8,10},{9,11},{10,... | collective-permute-start | bytes 786440 | tf_op jit(solution)/shard_map/ppermute | solution.py:363
  25.1 22.5 %collective-permute-start.11 = (bf16[4,64,512]{2,1,0:T(8,128)(2,1)S(1)}, bf16[4,64,512]{2,1,0:T(8,128)(2,1)S(1)}, u32[]{:S(2)}, u32[]{:S(2)}) collective-permute-start(bf16[4,64,512]{2,1,0:T(8,128)(2,1)S(1)} %get-tuple-element.53), channel_id=1, source_target_pairs={{0,4},{1,5},{2,6},{3,7},{4,0},{5,1},{6,2},{7,3},{8,12},{9,13},{10,... | collective-permute-start | bytes 786440 | tf_op jit(solution)/shard_map/ppermute | solution.py:363
  47.8 6.2 %collective-permute-start.13 = (bf16[4,3,64,512]{3,2,1,0:T(8,128)(2,1)S(1)}, bf16[4,3,64,512]{3,2,1,0:T(8,128)(2,1)S(1)}, u32[]{:S(2)}, u32[]{:S(2)}) collective-permute-start(bf16[4,3,64,512]{3,2,1,0:T(8,128)(2,1)S(1)} %pad_maximum_fusion), channel_id=1, source_target_pairs={{0,1},{1,0},{2,3},{3,2},{4,5},{5,4},{6,7},{7,6},{8,9},{9,8},{10,11... | collective-permute-start | bytes 2359304 | tf_op jit(solution)/shard_map/ppermute | solution.py:363

commit v9 on v8

--- a/solution.py
+++ b/solution.py
@@ -277,9 +277,11 @@
         cross = lax.dot_general(x, x_ref[...], TRANS_B, preferred_element_type=f32)
         return split(jnp.exp(cross - widen(col, n) - lead_sq))
 
-    def row_entries():
-        for a in range(nrows):
-            rows = slice(a * block, (a + 1) * block)
+    for a in range(nrows):
+        rows = slice(a * block, (a + 1) * block)
+
+        @pl.when(a * row_n + row_at >= PANELS)
+        def _():
             col_ref[rows, :] = half_norm_col(r_ref[rows, :])
             kh_ref[rows, :], kl_ref[rows, :] = entries(r_ref[rows, :], col_ref[rows, :])
 
@@ -293,7 +295,6 @@
             col_sq, col = half_norms(xc)
             col_sq = col_sq - log_row(amp_ref[0], block)
             zh_ref[...], zl_ref[...] = entries(xc, col)
-            row_entries()
             for s in range(0, n, block):
                 e = s + block
                 panel = dot_nt(zh_ref[:, :e], zl_ref[:, :e], *inverse(s, e, 0, e))
@@ -305,26 +306,23 @@
             for a in range(nrows):
                 i = a * row_n + row_at
                 rows = slice(a * block, (a + 1) * block)
-                cross = lax.dot_general(r_ref[rows, :], xc, TRANS_B, preferred_element_type=f32)
-                k = jnp.exp(cross - widen(col_ref[rows, :], block) - col_sq)
-                on_diag = diagonal(block) & (i == j)
-                k = k + jnp.where(on_diag, jnp.broadcast_to(nz_ref[a : a + 1, :], (block, block)), 0.0)
-                k = k - dot_nt(kh_ref[rows, :], kl_ref[rows, :], zh_ref[...], zl_ref[...])
-                store_block(out_ref, a, b, 0, ncols, jnp.where(i >= PANELS, k, 0.0))
+
+                @pl.when(i >= PANELS)
+                def _():
+                    xr = r_ref[rows, :]
+                    cross = lax.dot_general(xr, xc, TRANS_B, preferred_element_type=f32)
+                    k = jnp.exp(cross - widen(col_ref[rows, :], block) - col_sq)
+                    on_diag = diagonal(block) & (i == j)
+                    k = k + jnp.where(on_diag, jnp.broadcast_to(nz_ref[a : a + 1, :], (block, block)), 0.0)
+                    k = k - dot_nt(kh_ref[rows, :], kl_ref[rows, :], zh_ref[...], zl_ref[...])
+                    store_block(out_ref, a, b, 0, ncols, k)
+
+                @pl.when(i < PANELS)
+                def _():
+                    store_block(out_ref, a, b, 0, ncols, jnp.zeros((block, block), f32))
 
         if b:
             continue
-
-        @pl.when(j < PANELS)
-        def _():
-            def some_entries(step, carry):
-                o = pl.multiple_of(step * WB, WB)
-                x = r_ref[pl.ds(o, WB), :]
-                kh_ref[pl.ds(o, WB), :], kl_ref[pl.ds(o, WB), :] = entries(x, half_norm_col(x))
-                return carry
-
-            lax.fori_loop(0, nrows * block // WB, some_entries, 0)
-
         for s in range(PANELS):
             w = s * block
             e = w + block
@@ -338,7 +336,8 @@
                     store_block(out_ref, 0, b, o, ncols, panel)
                     return carry
 
-                lax.fori_loop(0, nrows * block // WB, some_rows, 0)
+                start = jnp.where(row_at < PANELS, block // WB, 0)
+                lax.fori_loop(start, nrows * block // WB, some_rows, 0)
 
             for v in range(PANELS):
 

time: 69.6 us -> 69 us (level); the launches traced: 68.4 us -> 68.8 us
  transfers between devices with their start and end apart: 14 -> 14, of which waited for: 4 -> 4; matrix products, arithmetic and copies ran while one was open for 3% -> 3% of each run, Pallas kernels for 37% -> 36%
where the time goes in v9:
time: 69 us; the launch traced here: 68.8 us
  Pallas kernels  39.9 us (58%)
  starting transfers between devices  15 us (22%)
  waiting for transfers between devices  10.1 us (15%)
  other arithmetic  2.2 us (3%)
  between operations  0.86 us (1%)
  local copies, waits for them, and re-layouts  0.82 us (1%)
    pallas_call x1, Pallas kernels, local(): pl.pallas_call(first_kernel, out_shape=[jax.ShapeDtypeStruct((n, width),...  19.8 us
    ppermute x14, starting transfers between devices, exchange(): lax.ppermute(x, axis, [(i, i ^ k) for i in range(lax.axis_size(axis))])  15 us
    pallas_call x1, Pallas kernels, local(): pl.pallas_call(bulk_kernel, out_shape=jax.ShapeDtypeStruct((nrows * block...  14.8 us
    ppermute x14, waiting for transfers between devices, exchange(): lax.ppermute(x, axis, [(i, i ^ k) for i in range(lax.axis_size(axis))])  10.1 us
    pallas_call x1, Pallas kernels, local(): pl.pallas_call(second_kernel, out_shape=factor_shapes(n1), in_specs=[VMEM...  5.25 us
  transfers between devices with their start and end apart: 14, of which 4 were waited for; matrix products, arithmetic and copies ran while one was open for 3% of the time, Pallas kernels for 36%

profile of v9, /device:TPU:31, one launch (start us, length us, event | category | flops | bytes accessed | tf_op | source)
XLA Modules:
  0.0 68.8 jit_solution(16048090059420593859)
XLA Ops:
  0.0 0.3 collective-permute-start.2
  0.3 0.2 collective-permute-start.1
  0.5 2.2 %collective-permute-start = (bf16[2,64,512]{2,1,0:T(8,128)(2,1)}, bf16[2,64,512]{2,1,0:T(8,128)(2,1)S(1)}, u32[]{:S(2)}, u32[]{:S(2)}) collective-permute-start(bf16[2,64,512]{2,1,0:T(8,128)(2,1)} %bitcast.57), channel_id=1, source_target_pairs={{0,24},{8,16},{16,8},{24,0},{1,25},{9,17},{17,9},{25,1},{2,26},{10... | collective-permute-start | bytes 393224 | tf_op jit(solution)/shard_map/ppermute | solution.py:362
  2.7 0.0 copy-start
  2.7 0.7 %copy.7 = f32[2,1,512]{2,0,1:T(2,128)S(1)} copy(f32[2,1,512]{2,1,0:T(1,128)} %param.5) | data formatting | bytes 8192
  3.4 0.1 pad_add_fusion.at_ref
  3.5 1.1 %collective-permute-done.2 = bf16[2,64,512]{2,1,0:T(8,128)(2,1)S(1)} collective-permute-done((bf16[2,64,512]{2,1,0:T(8,128)(2,1)}, bf16[2,64,512]{2,1,0:T(8,128)(2,1)S(1)}, u32[]{:S(2)}, u32[]{:S(2)}) %collective-permute-start.2) | collective-permute-done | bytes 131104 | tf_op jit(solution)/shard_map/ppermute | solution.py:362
  4.6 0.1 collective-permute-done.1
  4.6 2.7 %collective-permute-done = bf16[2,64,512]{2,1,0:T(8,128)(2,1)S(1)} collective-permute-done((bf16[2,64,512]{2,1,0:T(8,128)(2,1)}, bf16[2,64,512]{2,1,0:T(8,128)(2,1)S(1)}, u32[]{:S(2)}, u32[]{:S(2)}) %collective-permute-start) | collective-permute-done | bytes 131104 | tf_op jit(solution)/shard_map/ppermute | solution.py:362
  7.3 0.9 %fusion.5 = (bf16[1,64,512]{2,1,0:T(8,128)(2,1)S(1)}, bf16[1,64,512]{2,1,0:T(8,128)(2,1)S(1)}) fusion(pred[]{:T(512)S(6)} %eq.26, pred[]{:T(512)S(6)} %eq.25, pred[]{:T(512)S(6)} %eq.24, bf16[2,64,512]{2,1,0:T(8,128)(2,1)S(1)} %collective-permute-done.2, bf16[2,64,512]{2,1,0:T(8,128)(2,1)S(1)} %collective-permute-done.1, ...), kind=kLoop, calls=%fused_computation.19 | loop fusion | flops 196608 | bytes 393222 | tf_op jit(solution)/shard_map/jit(_where)/select_n | solution.py:368
  8.2 0.2 collective-permute-start.3
  8.5 1.1 %collective-permute-start.5 = (bf16[2,64,512]{2,1,0:T(8,128)(2,1)S(1)}, bf16[2,64,512]{2,1,0:T(8,128)(2,1)S(1)}, u32[]{:S(2)}, u32[]{:S(2)}) collective-permute-start(bf16[2,64,512]{2,1,0:T(8,128)(2,1)S(1)} %pad_maximum_fusion.7), channel_id=1, source_target_pairs={{0,6},{1,7},{2,4},{3,5},{4,2},{5,3},{6,0},{7,1},{8,14},{9,15},{10,... | collective-permute-start | bytes 393224 | tf_op jit(solution)/shard_map/ppermute | solution.py:362
  9.5 1.4 %collective-permute-start.4 = (bf16[2,64,512]{2,1,0:T(8,128)(2,1)S(1)}, bf16[2,64,512]{2,1,0:T(8,128)(2,1)S(1)}, u32[]{:S(2)}, u32[]{:S(2)}) collective-permute-start(bf16[2,64,512]{2,1,0:T(8,128)(2,1)S(1)} %pad_maximum_fusion.7), channel_id=1, source_target_pairs={{0,4},{1,5},{2,6},{3,7},{4,0},{5,1},{6,2},{7,3},{8,12},{9,13},{10,... | collective-permute-start | bytes 393224 | tf_op jit(solution)/shard_map/ppermute | solution.py:362
  11.6 0.2 collective-permute-start.9
  11.8 1.2 %collective-permute-start.8 = (f32[2,512]{1,0:T(2,128)S(1)}, f32[2,512]{1,0:T(2,128)S(1)}, u32[]{:S(2)}, u32[]{:S(2)}) collective-permute-start(f32[2,512]{1,0:T(2,128)S(1)} %bitcast.51), channel_id=1, source_target_pairs={{0,16},{8,24},{16,0},{24,8},{1,17},{9,25},{17,1},{25,9},{2,18},{10... | collective-permute-start | bytes 12296 | tf_op jit(solution)/shard_map/ppermute | solution.py:362
  13.1 1.0 %pad_maximum_fusion.1 = bf16[4,2,64,512]{3,2,1,0:T(8,128)(2,1)S(1)} fusion(bf16[1,2,64,512]{3,2,1,0:T(8,128)(2,1)S(1)} %bitcast.63, bf16[1,2,64,512]{3,2,1,0:T(8,128)(2,1)S(1)} %bitcast.62, bf16[1,2,64,512]{3,2,1,0:T(8,128)(2,1)S(1)} %bitcast.61, bf16[1,2,64,512]{3,2,1,0:T(8,128)(2,1)} %bitcast.58), kind=kLoop, calls=%fused_computation.1 | loop fusion | flops 786432 | bytes 1048576 | tf_op jit(solution)/shard_map/stack | solution.py:387
  14.0 0.0 collective-permute-done.3
  14.0 1.4 %collective-permute-start.7 = (f32[2,512]{1,0:T(2,128)S(1)}, f32[2,512]{1,0:T(2,128)S(1)}, u32[]{:S(2)}, u32[]{:S(2)}) collective-permute-start(f32[2,512]{1,0:T(2,128)S(1)} %bitcast.52), channel_id=1, source_target_pairs={{0,24},{8,16},{16,8},{24,0},{1,25},{9,17},{17,9},{25,1},{2,26},{10... | collective-permute-start | bytes 12296 | tf_op jit(solution)/shard_map/ppermute | solution.py:362
  15.4 0.0 collective-permute-done.5
  15.4 6.2 %collective-permute-done.4 = bf16[2,64,512]{2,1,0:T(8,128)(2,1)S(1)} collective-permute-done((bf16[2,64,512]{2,1,0:T(8,128)(2,1)S(1)}, bf16[2,64,512]{2,1,0:T(8,128)(2,1)S(1)}, u32[]{:S(2)}, u32[]{:S(2)}) %collective-permute-start.4) | collective-permute-done | bytes 131104 | tf_op jit(solution)/shard_map/ppermute | solution.py:362
  21.6 0.1 pad_maximum_fusion.2.mine_ref
  21.7 2.3 %collective-permute-start.6 = (bf16[4,2,64,512]{3,2,1,0:T(8,128)(2,1)S(1)}, bf16[4,2,64,512]{3,2,1,0:T(8,128)(2,1)S(1)}, u32[]{:S(2)}, u32[]{:S(2)}) collective-permute-start(bf16[4,2,64,512]{3,2,1,0:T(8,128)(2,1)S(1)} %pad_maximum_fusion.2.mine_ref), channel_id=1, source_target_pairs={{0,1},{1,0},{2,3},{3,2},{4,5},{5,4},{6,7},{7,6},{8,9},{9,8},{10,11... | collective-permute-start | bytes 1572872 | tf_op jit(solution)/shard_map/ppermute | solution.py:362
  24.0 0.0 copy-done
  24.0 0.1 fusion.3
  24.1 1.0 %collective-permute-start.12 = (bf16[4,64,512]{2,1,0:T(8,128)(2,1)S(1)}, bf16[4,64,512]{2,1,0:T(8,128)(2,1)S(1)}, u32[]{:S(2)}, u32[]{:S(2)}) collective-permute-start(bf16[4,64,512]{2,1,0:T(8,128)(2,1)S(1)} %get-tuple-element.51), channel_id=1, source_target_pairs={{0,6},{1,7},{2,4},{3,5},{4,2},{5,3},{6,0},{7,1},{8,14},{9,15},{10,... | collective-permute-start | bytes 786440 | tf_op jit(solution)/shard_map/ppermute | solution.py:362
  25.1 0.0 collective-permute-done.9
  25.1 0.0 collective-permute-start.10
  25.1 0.0 collective-permute-done.8
  25.1 2.6 %collective-permute-start.11 = (bf16[4,64,512]{2,1,0:T(8,128)(2,1)S(1)}, bf16[4,64,512]{2,1,0:T(8,128)(2,1)S(1)}, u32[]{:S(2)}, u32[]{:S(2)}) collective-permute-start(bf16[4,64,512]{2,1,0:T(8,128)(2,1)S(1)} %get-tuple-element.53), channel_id=1, source_target_pairs={{0,4},{1,5},{2,6},{3,7},{4,0},{5,1},{6,2},{7,3},{8,12},{9,13},{10,... | collective-permute-start | bytes 786440 | tf_op jit(solution)/shard_map/ppermute | solution.py:362
  27.7 0.0 collective-permute-done.7
  27.7 0.0 collective-permute-done.6.other_ref
  27.7 19.8 %first.1 = (bf16[1024,512]{1,0:T(8,128)(2,1)S(1)}, f32[8,1024]{1,0:T(8,128)S(1)}, f32[768,1024]{1,0:T(8,128)S(1)}, bf16[768,1024]{1,0:T(8,128)(2,1)S(1)}, bf16[7...) custom-call(s32[4]{0:T(128)S(1)} %pad_add_fusion.at_ref, f32[1]{0:T(128)S(6)} %copy.8.amp_ref, ...), custom_call_target="tpu_custom_call" | custom-call | flops 1000000 | bytes 1000000 | tf_op jit(solution)/shard_map/first/pallas_call | solution.py:414
  47.6 0.0 collective-permute-done.12.refs_12_
  47.6 0.0 collective-permute-done.10.refs_10_
  47.6 0.0 collective-permute-done.11.refs_11_
  47.7 0.1 pad_maximum_fusion
  47.8 0.9 %collective-permute-start.13 = (bf16[4,3,64,512]{3,2,1,0:T(8,128)(2,1)S(1)}, bf16[4,3,64,512]{3,2,1,0:T(8,128)(2,1)S(1)}, u32[]{:S(2)}, u32[]{:S(2)}) collective-permute-start(bf16[4,3,64,512]{3,2,1,0:T(8,128)(2,1)S(1)} %pad_maximum_fusion), channel_id=1, source_target_pairs={{0,1},{1,0},{2,3},{3,2},{4,5},{5,4},{6,7},{7,6},{8,9},{9,8},{10,11... | collective-permute-start | bytes 2359304 | tf_op jit(solution)/shard_map/ppermute | solution.py:362
  48.7 5.3 %second.1 = (f32[256,1024]{1,0:T(8,128)S(1)}, bf16[256,1024]{1,0:T(8,128)(2,1)S(1)}, bf16[256,1024]{1,0:T(8,128)(2,1)S(1)}) custom-call(f32[256,1024]{1,0:T(8,128)S(1)} %get-tuple-element.33.rest_ref), custom_call_target="tpu_custom_call" | custom-call | flops 20000000000 | bytes 8000000 | tf_op jit(solution)/shard_map/second/pallas_call | solution.py:428
  54.0 0.0 collective-permute-done.13.refs_13_
  54.0 14.8 %bulk.1 = f32[4096,128]{1,0:T(8,128)} custom-call(s32[4]{0:T(128)S(1)} %pad_add_fusion.at_ref, f32[1]{0:T(128)S(6)} %copy.8.amp_ref, bf16[1024,512]{1,0:T(8,128)(2,1)S(1)} %get-tuple-element.26.refs_0_, f32[8,1024]{1,0:T(8,128)S(1)} %get-tuple-element.27.refs_1_, f32[768,1024]{1,0:T(8,128)S(1)} %get-tuple-element.28.refs_2_, ...), custom_call_target="tpu_custom_call" | custom-call | flops 20000000000 | bytes 8000000 | tf_op jit(solution)/shard_map/bulk/pallas_call | solution.py:440
  (6 shorter events, 0.1 us)
Async XLA Ops:
  0.0 4.6 %collective-permute-start.2 = (bf16[2,64,512]{2,1,0:T(8,128)(2,1)}, bf16[2,64,512]{2,1,0:T(8,128)(2,1)S(1)}, u32[]{:S(2)}, u32[]{:S(2)}) collective-permute-start(bf16[2,64,512]{2,1,0:T(8,128)(2,1)} %bitcast.55), channel_id=1, source_target_pairs={{0,8},{8,0},{16,24},{24,16},{1,9},{9,1},{17,25},{25,17},{2,10},{10... | collective-permute-start | bytes 393224 | tf_op jit(solution)/shard_map/ppermute | solution.py:362
  0.3 4.4 %collective-permute-start.1 = (bf16[2,64,512]{2,1,0:T(8,128)(2,1)}, bf16[2,64,512]{2,1,0:T(8,128)(2,1)S(1)}, u32[]{:S(2)}, u32[]{:S(2)}) collective-permute-start(bf16[2,64,512]{2,1,0:T(8,128)(2,1)} %bitcast.56), channel_id=1, source_target_pairs={{0,16},{8,24},{16,0},{24,8},{1,17},{9,25},{17,1},{25,9},{2,18},{10... | collective-permute-start | bytes 393224 | tf_op jit(solution)/shard_map/ppermute | solution.py:362
  0.5 6.8 %collective-permute-start = (bf16[2,64,512]{2,1,0:T(8,128)(2,1)}, bf16[2,64,512]{2,1,0:T(8,128)(2,1)S(1)}, u32[]{:S(2)}, u32[]{:S(2)}) collective-permute-start(bf16[2,64,512]{2,1,0:T(8,128)(2,1)} %bitcast.57), channel_id=1, source_target_pairs={{0,24},{8,16},{16,8},{24,0},{1,25},{9,17},{17,9},{25,1},{2,26},{10... | collective-permute-start | bytes 393224 | tf_op jit(solution)/shard_map/ppermute | solution.py:362
  2.7 21.3 %copy-start = (bf16[2,1,64,512]{3,2,1,0:T(8,128)(2,1)S(1)}, bf16[2,1,64,512]{3,2,1,0:T(8,128)(2,1)}, u32[]{:S(2)}) copy-start(bf16[2,1,64,512]{3,2,1,0:T(8,128)(2,1)} %param.3) | copy-start | bytes 393220
  8.2 5.8 %collective-permute-start.3 = (bf16[2,64,512]{2,1,0:T(8,128)(2,1)S(1)}, bf16[2,64,512]{2,1,0:T(8,128)(2,1)S(1)}, u32[]{:S(2)}, u32[]{:S(2)}) collective-permute-start(bf16[2,64,512]{2,1,0:T(8,128)(2,1)S(1)} %pad_maximum_fusion.7), channel_id=1, source_target_pairs={{0,2},{1,3},{2,0},{3,1},{4,6},{5,7},{6,4},{7,5},{8,10},{9,11},{10,... | collective-permute-start | bytes 393224 | tf_op jit(solution)/shard_map/ppermute | solution.py:362
  8.5 7.0 %collective-permute-start.5 = (bf16[2,64,512]{2,1,0:T(8,128)(2,1)S(1)}, bf16[2,64,512]{2,1,0:T(8,128)(2,1)S(1)}, u32[]{:S(2)}, u32[]{:S(2)}) collective-permute-start(bf16[2,64,512]{2,1,0:T(8,128)(2,1)S(1)} %pad_maximum_fusion.7), channel_id=1, source_target_pairs={{0,6},{1,7},{2,4},{3,5},{4,2},{5,3},{6,0},{7,1},{8,14},{9,15},{10,... | collective-permute-start | bytes 393224 | tf_op jit(solution)/shard_map/ppermute | solution.py:362
  9.5 12.1 %collective-permute-start.4 = (bf16[2,64,512]{2,1,0:T(8,128)(2,1)S(1)}, bf16[2,64,512]{2,1,0:T(8,128)(2,1)S(1)}, u32[]{:S(2)}, u32[]{:S(2)}) collective-permute-start(bf16[2,64,512]{2,1,0:T(8,128)(2,1)S(1)} %pad_maximum_fusion.7), channel_id=1, source_target_pairs={{0,4},{1,5},{2,6},{3,7},{4,0},{5,1},{6,2},{7,3},{8,12},{9,13},{10,... | collective-permute-start | bytes 393224 | tf_op jit(solution)/shard_map/ppermute | solution.py:362
  11.6 13.4 %collective-permute-start.9 = (f32[2,512]{1,0:T(2,128)S(1)}, f32[2,512]{1,0:T(2,128)S(1)}, u32[]{:S(2)}, u32[]{:S(2)}) collective-permute-start(f32[2,512]{1,0:T(2,128)S(1)} %bitcast.50), channel_id=1, source_target_pairs={{0,8},{8,0},{16,24},{24,16},{1,9},{9,1},{17,25},{25,17},{2,10},{10... | collective-permute-start | bytes 12296 | tf_op jit(solution)/shard_map/ppermute | solution.py:362
  11.8 13.2 %collective-permute-start.8 = (f32[2,512]{1,0:T(2,128)S(1)}, f32[2,512]{1,0:T(2,128)S(1)}, u32[]{:S(2)}, u32[]{:S(2)}) collective-permute-start(f32[2,512]{1,0:T(2,128)S(1)} %bitcast.51), channel_id=1, source_target_pairs={{0,16},{8,24},{16,0},{24,8},{1,17},{9,25},{17,1},{25,9},{2,18},{10... | collective-permute-start | bytes 12296 | tf_op jit(solution)/shard_map/ppermute | solution.py:362
  14.0 13.7 %collective-permute-start.7 = (f32[2,512]{1,0:T(2,128)S(1)}, f32[2,512]{1,0:T(2,128)S(1)}, u32[]{:S(2)}, u32[]{:S(2)}) collective-permute-start(f32[2,512]{1,0:T(2,128)S(1)} %bitcast.52), channel_id=1, source_target_pairs={{0,24},{8,16},{16,8},{24,0},{1,25},{9,17},{17,9},{25,1},{2,26},{10... | collective-permute-start | bytes 12296 | tf_op jit(solution)/shard_map/ppermute | solution.py:362
  21.7 6.1 %collective-permute-start.6 = (bf16[4,2,64,512]{3,2,1,0:T(8,128)(2,1)S(1)}, bf16[4,2,64,512]{3,2,1,0:T(8,128)(2,1)S(1)}, u32[]{:S(2)}, u32[]{:S(2)}) collective-permute-start(bf16[4,2,64,512]{3,2,1,0:T(8,128)(2,1)S(1)} %pad_maximum_fusion.2.mine_ref), channel_id=1, source_target_pairs={{0,1},{1,0},{2,3},{3,2},{4,5},{5,4},{6,7},{7,6},{8,9},{9,8},{10,11... | collective-permute-start | bytes 1572872 | tf_op jit(solution)/shard_map/ppermute | solution.py:362
  24.1 23.5 %collective-permute-start.12 = (bf16[4,64,512]{2,1,0:T(8,128)(2,1)S(1)}, bf16[4,64,512]{2,1,0:T(8,128)(2,1)S(1)}, u32[]{:S(2)}, u32[]{:S(2)}) collective-permute-start(bf16[4,64,512]{2,1,0:T(8,128)(2,1)S(1)} %get-tuple-element.51), channel_id=1, source_target_pairs={{0,6},{1,7},{2,4},{3,5},{4,2},{5,3},{6,0},{7,1},{8,14},{9,15},{10,... | collective-permute-start | bytes 786440 | tf_op jit(solution)/shard_map/ppermute | solution.py:362
  25.1 22.5 %collective-permute-start.10 = (bf16[4,64,512]{2,1,0:T(8,128)(2,1)S(1)}, bf16[4,64,512]{2,1,0:T(8,128)(2,1)S(1)}, u32[]{:S(2)}, u32[]{:S(2)}) collective-permute-start(bf16[4,64,512]{2,1,0:T(8,128)(2,1)S(1)} %get-tuple-element.52), channel_id=1, source_target_pairs={{0,2},{1,3},{2,0},{3,1},{4,6},{5,7},{6,4},{7,5},{8,10},{9,11},{10,... | collective-permute-start | bytes 786440 | tf_op jit(solution)/shard_map/ppermute | solution.py:362
  25.1 22.5 %collective-permute-start.11 = (bf16[4,64,512]{2,1,0:T(8,128)(2,1)S(1)}, bf16[4,64,512]{2,1,0:T(8,128)(2,1)S(1)}, u32[]{:S(2)}, u32[]{:S(2)}) collective-permute-start(bf16[4,64,512]{2,1,0:T(8,128)(2,1)S(1)} %get-tuple-element.53), channel_id=1, source_target_pairs={{0,4},{1,5},{2,6},{3,7},{4,0},{5,1},{6,2},{7,3},{8,12},{9,13},{10,... | collective-permute-start | bytes 786440 | tf_op jit(solution)/shard_map/ppermute | solution.py:362
  47.8 6.2 %collective-permute-start.13 = (bf16[4,3,64,512]{3,2,1,0:T(8,128)(2,1)S(1)}, bf16[4,3,64,512]{3,2,1,0:T(8,128)(2,1)S(1)}, u32[]{:S(2)}, u32[]{:S(2)}) collective-permute-start(bf16[4,3,64,512]{3,2,1,0:T(8,128)(2,1)S(1)} %pad_maximum_fusion), channel_id=1, source_target_pairs={{0,1},{1,0},{2,3},{3,2},{4,5},{5,4},{6,7},{7,6},{8,9},{9,8},{10,11... | collective-permute-start | bytes 2359304 | tf_op jit(solution)/shard_map/ppermute | solution.py:362
